TPU v7x, 32 devices: a whole 2x2x4 slice. The times are simulated.
32 devices in a mesh: grp: 2 (over x), ep: 16 (over z, y, core).
Axes of the slice: x: 2, y: 2, z: 4, core: 2. Of those that a mesh axis runs over, the one named last changes fastest.
Arguments:
- tokens: bfloat16 [2, 4096, 1280], P('grp', 'ep'), may hold values from -18 to 18
- doc_lengths: int32 [2, 4], P('grp'), may hold values from 1 to 2048, 4096 in all within a row
- expert_ids: int32 [2, 4096, 7], P('grp', 'ep'), may hold values from 0 to 15, all different within a row; in each aligned block of 256 rows (0 to 255, 256 to 511, ..., all dimensions but the last counted through in order) at most 192 rows name the same one
- out_grad: bfloat16 [2, 4096, 1280], P('grp', 'ep'), may hold values from -6 to 6
- mixer_gain: float32 [1280], replicated, may hold values from 0.5 to 1.5
- query_weight: bfloat16 [1280, 1280], replicated, may hold values from -0.4375 to 0.4375
- key_weight: bfloat16 [1280, 1280], replicated, may hold values from -0.15625 to 0.15625
- value_weight: bfloat16 [1280, 1280], replicated, may hold values from -0.15625 to 0.15625
- output_weight: bfloat16 [1280, 1280], replicated, may hold values from -2.5 to 2.5
- ffn_gain: float32 [1280], replicated, may hold values from 0.5 to 1.5
- router_weight: bfloat16 [1280, 16], replicated, may hold values from -0.078125 to 0.078125
- shared_gate: bfloat16 [1280, 896], replicated, may hold values from -0.15625 to 0.15625
- shared_up: bfloat16 [1280, 896], replicated, may hold values from -0.15625 to 0.15625
- shared_down: bfloat16 [896, 1280], replicated, may hold values from -0.375 to 0.375
- expert_gate: bfloat16 [16, 1280, 896], P('ep'), may hold values from -0.15625 to 0.15625
- expert_up: bfloat16 [16, 1280, 896], P('ep'), may hold values from -0.15625 to 0.15625
- expert_down: bfloat16 [16, 896, 1280], P('ep'), may hold values from -0.75 to 0.75
Outputs:
- layer_out: bfloat16 [2, 4096, 1280], P('grp', 'ep')
- tokens_grad: bfloat16 [2, 4096, 1280], P('grp', 'ep')
- mixer_gain_grad: float32 [1280], P(('grp', 'ep'))
- query_weight_grad: float32 [1280, 1280], P(('grp', 'ep'))
- key_weight_grad: float32 [1280, 1280], P(('grp', 'ep'))
- value_weight_grad: float32 [1280, 1280], P(('grp', 'ep'))
- output_weight_grad: float32 [1280, 1280], P(('grp', 'ep'))
- ffn_gain_grad: float32 [1280], P(('grp', 'ep'))
- router_weight_grad: float32 [1280, 16], P(('grp', 'ep'))
- shared_gate_grad: float32 [1280, 896], P(('grp', 'ep'))
- shared_up_grad: float32 [1280, 896], P(('grp', 'ep'))
- shared_down_grad: float32 [896, 1280], P(None, ('grp', 'ep'))
- expert_gate_grad: float32 [16, 1280, 896], P('ep', 'grp')
- expert_up_grad: float32 [16, 1280, 896], P('ep', 'grp')
- expert_down_grad: float32 [16, 896, 1280], P('ep', None, 'grp')
- stream_rms: float32 [3], replicated
Inputs may be any that keep to these rules, and one draw needn't show every extreme that they name: Each row of doc_lengths sums to 4096, and its largest entry is 2048. `expert_ids`: a token names 7 different experts; the tokens of one device name one expert at most 192 times.
All inputs are finite; a program needn't handle non-finite values.
Results may differ from a plain program's by a relative error of at most 0.025.
Values may be sent and summed in bfloat16 or wider, within the bound.
A program may use at most 384 MiB of HBM per device.

v0:
```python
import jax
import jax.numpy as jnp
from jax import lax
from jax.sharding import PartitionSpec as P

HEADS = 10
HEAD = 128
TOP = 7


epsilon = 1e-06
rope_base = 10000.0
masked_value = -1e30


def normed(values, gain_vec):
    return (
        values * lax.rsqrt(jnp.mean(values * values, axis=-1, keepdims=True) + epsilon) * gain_vec
    )


def rotary(values, positions, direction):
    half_dim = values.shape[-1] // 2
    frequency = rope_base ** (-jnp.arange(half_dim, dtype=jnp.float32) / half_dim)
    angles = positions[:, None] * frequency[None, :]
    cosine = jnp.cos(angles)[:, None, :]
    sine_val = direction * jnp.sin(angles)[:, None, :]
    lower_half = values[..., :half_dim]
    upper_half = values[..., half_dim:]
    return jnp.concatenate(
        [lower_half * cosine - upper_half * sine_val, upper_half * cosine + lower_half * sine_val],
        axis=-1,
    )


def inner_left(left_op, right_op):
    return lax.dot_general(
        left_op, right_op, (((0,), (0,)), ((), ())), preferred_element_type=jnp.float32
    )


def inner_right(left_op, right_op):
    return lax.dot_general(
        left_op, right_op, (((1,), (1,)), ((), ())), preferred_element_type=jnp.float32
    )


def silu_parts(pre_act):
    sigmoid_val = jax.nn.sigmoid(pre_act)
    return (pre_act * sigmoid_val, sigmoid_val * (1.0 + pre_act * (1.0 - sigmoid_val)))


def doc_of(positions, doc_ends):
    return jnp.sum((positions[:, None] >= doc_ends[None, :]).astype(jnp.int32), axis=1)


def block_scores(queries, key_piece, first_row, query_pos, query_doc, doc_ends):
    key_count = key_piece.shape[0]
    key_pos = first_row + jnp.arange(key_count, dtype=jnp.int32)
    visible = (query_doc[:, None] == doc_of(key_pos, doc_ends)[None, :]) & (
        key_pos[None, :] <= query_pos[:, None]
    )
    key_heads = key_piece.reshape(key_count, queries.shape[1], queries.shape[2])
    scores = jnp.einsum("qhd,khd->hqk", queries, key_heads, preferred_element_type=jnp.float32)
    return (scores, visible, key_heads)


def local(
    tokens,
    doc_lengths,
    expert_ids,
    out_grad,
    mixer_gain,
    query_weight,
    key_weight,
    value_weight,
    output_weight,
    ffn_gain,
    router_weight,
    shared_gate,
    shared_up,
    shared_down,
    expert_gate,
    expert_up,
    expert_down,
):
    row_count = tokens.shape[1]
    model_width = tokens.shape[2]
    head_count = HEADS
    head_dim = HEAD
    top_k = TOP
    ep_count = lax.axis_size("ep")
    ep_index = lax.axis_index("ep")
    expert_count = router_weight.shape[1]
    capacity = min(row_count, 12 * row_count * top_k // (7 * expert_count))
    seq_total = row_count * ep_count
    key_block = min(seq_total, 1024)
    q_scale = head_dim ** (-0.5)
    doc_ends = jnp.cumsum(doc_lengths[0])
    query_pos = ep_index * row_count + jnp.arange(row_count, dtype=jnp.int32)
    query_doc = doc_of(query_pos, doc_ends)
    position = query_pos.astype(jnp.float32)
    stream = tokens[0].astype(jnp.float32)
    hidden_low = normed(stream, mixer_gain).astype(jnp.bfloat16)
    query_lin = jnp.dot(hidden_low, query_weight, preferred_element_type=jnp.float32).reshape(
        row_count, head_count, head_dim
    )
    key_lin = jnp.dot(hidden_low, key_weight, preferred_element_type=jnp.float32).reshape(
        row_count, head_count, head_dim
    )
    value_send = jnp.dot(hidden_low, value_weight, preferred_element_type=jnp.float32).astype(
        jnp.bfloat16
    )
    queries = (rotary(query_lin, position, 1.0) * q_scale).astype(jnp.bfloat16)
    key_send = (
        rotary(key_lin, position, 1.0)
        .astype(jnp.bfloat16)
        .reshape(row_count, head_count * head_dim)
    )
    run_max = jnp.full((head_count, row_count), masked_value, jnp.float32)
    key_piece = lax.all_gather(key_send, "ep", axis=0, tiled=True)
    value_piece = lax.all_gather(value_send, "ep", axis=0, tiled=True)
    scores, visible, key_heads = block_scores(
        queries, key_piece, jnp.int32(0), query_pos, query_doc, doc_ends
    )
    scores = jnp.where(visible[None], scores, masked_value)
    new_max = jnp.maximum(run_max, jnp.max(scores, axis=-1))
    weights = jnp.where(visible[None], jnp.exp(scores - new_max[:, :, None]), 0.0)
    value_heads = value_piece.reshape(key_heads.shape)
    run_acc = jnp.einsum(
        "hqk,khd->hqd",
        weights.astype(jnp.bfloat16),
        value_heads,
        preferred_element_type=jnp.float32,
    )
    run_max, run_sum, run_acc = (new_max, jnp.sum(weights, axis=-1), run_acc)
    log_total = run_max + jnp.log(run_sum)
    mixed_heads = jnp.transpose(run_acc / run_sum[:, :, None], (1, 0, 2))
    mixed_low = mixed_heads.reshape(row_count, head_count * head_dim).astype(jnp.bfloat16)
    mixer_out = jnp.dot(mixed_low, output_weight, preferred_element_type=jnp.float32)
    residual = stream + mixer_out
    ffn_low = normed(residual, ffn_gain).astype(jnp.bfloat16)
    logits = jnp.dot(ffn_low, router_weight, preferred_element_type=jnp.float32)
    local_ids = expert_ids[0]
    choose = (
        local_ids[:, :, None] == jnp.arange(expert_count, dtype=jnp.int32)[None, None, :]
    ).astype(jnp.float32)
    chosen = jnp.einsum("tke,te->tk", choose, logits)
    gate_probs = jax.nn.softmax(chosen, axis=-1)
    shared_pre = jnp.dot(ffn_low, shared_gate, preferred_element_type=jnp.float32)
    shared_lift = jnp.dot(ffn_low, shared_up, preferred_element_type=jnp.float32)
    shared_silu, shared_slope = silu_parts(shared_pre)
    shared_mid = (shared_silu * shared_lift).astype(jnp.bfloat16)
    shared_out = jnp.dot(shared_mid, shared_down, preferred_element_type=jnp.float32)
    choose_int = choose.reshape(row_count * top_k, expert_count).astype(jnp.int32)
    earlier = jnp.cumsum(choose_int, axis=0) - choose_int
    slot_index = jnp.sum(earlier * choose_int, axis=1)
    slot_target = local_ids.reshape(-1) * capacity + slot_index
    send_rows = (
        jnp.zeros((expert_count * capacity, model_width), jnp.bfloat16)
        .at[slot_target]
        .set(jnp.repeat(ffn_low, top_k, axis=0))
        .reshape(expert_count, capacity, model_width)
    )
    arrived = lax.all_to_all(send_rows, "ep", split_axis=0, concat_axis=0, tiled=True)
    source_count = arrived.shape[0]
    slot_count = arrived.shape[1]
    flat_in = arrived.reshape(-1, model_width)
    gate_pre = jnp.dot(flat_in, expert_gate[0], preferred_element_type=jnp.float32)
    up_pre = jnp.dot(flat_in, expert_up[0], preferred_element_type=jnp.float32)
    middle = (jax.nn.silu(gate_pre) * up_pre).astype(jnp.bfloat16)
    result = jnp.dot(middle, expert_down[0], preferred_element_type=jnp.float32).astype(
        jnp.bfloat16
    )
    returned = lax.all_to_all(
        result.reshape(source_count, slot_count, model_width),
        "ep",
        split_axis=0,
        concat_axis=0,
        tiled=True,
    )
    returned, arrived, gate_pre, up_pre = (
        returned,
        arrived,
        gate_pre.reshape(source_count, slot_count, -1),
        up_pre.reshape(source_count, slot_count, -1),
    )
    expert_rows = returned.reshape(-1, model_width)[slot_target].reshape(
        row_count, top_k, model_width
    )
    routed = jnp.einsum("tk,tkd->td", gate_probs, expert_rows, preferred_element_type=jnp.float32)
    ffn_out = shared_out + routed
    layer_out = residual + ffn_out
    sq_stream, sq_mixer, sq_layer = lax.psum(
        (
            jnp.sum(residual * residual),
            jnp.sum(mixer_out * mixer_out),
            jnp.sum(layer_out * layer_out),
        ),
        ("grp", "ep"),
    )
    entry_count = row_count * ep_count * lax.axis_size("grp") * model_width
    stream_rms = jnp.sqrt(jnp.stack([sq_stream, sq_mixer, sq_layer]) / entry_count)
    grad_low = out_grad[0]
    grad_out = grad_low.astype(jnp.float32)
    shared_mid_grad = inner_right(grad_low, shared_down)
    shared_pre_grad = (shared_mid_grad * shared_lift * shared_slope).astype(jnp.bfloat16)
    shared_lift_grad = (shared_mid_grad * shared_silu).astype(jnp.bfloat16)
    shared_down_grad = inner_left(shared_mid, grad_low)
    shared_gate_grad = inner_left(ffn_low, shared_pre_grad)
    shared_up_grad = inner_left(ffn_low, shared_lift_grad)
    ffn_grad = inner_right(shared_pre_grad, shared_gate) + inner_right(shared_lift_grad, shared_up)
    row_grads = (gate_probs[:, :, None] * grad_out[:, None, :]).astype(jnp.bfloat16)
    gate_grad = jnp.einsum("tkd,td->tk", expert_rows, grad_low, preferred_element_type=jnp.float32)
    grad_send = (
        jnp.zeros((expert_count * capacity, model_width), jnp.bfloat16)
        .at[slot_target]
        .set(row_grads.reshape(-1, model_width))
        .reshape(expert_count, capacity, model_width)
    )
    grad_arrived = lax.all_to_all(grad_send, "ep", split_axis=0, concat_axis=0, tiled=True)
    flat_grad = grad_arrived.reshape(-1, model_width)
    flat_in = arrived.reshape(-1, model_width)
    pre_flat = gate_pre.reshape(flat_in.shape[0], -1)
    lift_flat = up_pre.reshape(flat_in.shape[0], -1)
    expert_silu, expert_slope = silu_parts(pre_flat)
    middle = (expert_silu * lift_flat).astype(jnp.bfloat16)
    mid_grad = inner_right(flat_grad, expert_down[0])
    pre_grad = (mid_grad * lift_flat * expert_slope).astype(jnp.bfloat16)
    lift_grad = (mid_grad * expert_silu).astype(jnp.bfloat16)
    own_down_grad = inner_left(middle, flat_grad)
    own_gate_grad = inner_left(flat_in, pre_grad)
    own_up_grad = inner_left(flat_in, lift_grad)
    input_grad = (
        inner_right(pre_grad, expert_gate[0]) + inner_right(lift_grad, expert_up[0])
    ).astype(jnp.bfloat16)
    input_back = lax.all_to_all(
        input_grad.reshape(grad_arrived.shape), "ep", split_axis=0, concat_axis=0, tiled=True
    )
    back_rows = input_back.reshape(-1, model_width)[slot_target].reshape(
        row_count, top_k, model_width
    )
    ffn_grad = ffn_grad + jnp.sum(back_rows.astype(jnp.float32), axis=1)
    chosen_grad = gate_probs * (gate_grad - jnp.sum(gate_probs * gate_grad, axis=-1, keepdims=True))
    logit_grad = jnp.einsum("tk,tke->te", chosen_grad, choose).astype(jnp.bfloat16)
    router_grad = inner_left(ffn_low, logit_grad)
    ffn_grad = ffn_grad + inner_right(logit_grad, router_weight)
    unused_norm, ffn_pull = jax.vjp(normed, residual, ffn_gain)
    residual_part, ffn_gain_grad = ffn_pull(ffn_grad)
    residual_grad = grad_out + residual_part
    mixer_grad_low = residual_grad.astype(jnp.bfloat16)
    output_weight_grad = inner_left(mixed_low, mixer_grad_low)
    mixed_grad = inner_right(mixer_grad_low, output_weight).astype(jnp.bfloat16)
    mixed_grad3 = mixed_grad.reshape(row_count, head_count, head_dim)
    row_term = jnp.einsum(
        "qhd,qhd->hq", mixed_grad3, mixed_heads, preferred_element_type=jnp.float32
    )
    keys_all, values_all = (
        lax.all_gather(key_send, "ep", axis=0, tiled=True),
        lax.all_gather(value_send, "ep", axis=0, tiled=True),
    )

    def block_grads(block_index):
        first_row = block_index * key_block
        key_piece = lax.dynamic_slice_in_dim(keys_all, first_row, key_block, 0)
        value_piece = lax.dynamic_slice_in_dim(values_all, first_row, key_block, 0)
        scores, visible, key_heads = block_scores(
            queries, key_piece, first_row, query_pos, query_doc, doc_ends
        )
        value_heads = value_piece.reshape(key_heads.shape)
        probabilities = jnp.where(visible[None], jnp.exp(scores - log_total[:, :, None]), 0.0)
        prob_grad = jnp.einsum(
            "qhd,khd->hqk", mixed_grad3, value_heads, preferred_element_type=jnp.float32
        )
        score_grad = (probabilities * (prob_grad - row_term[:, :, None])).astype(jnp.bfloat16)
        return (probabilities, score_grad, key_heads)

    block_ids = jnp.arange(seq_total // key_block, dtype=jnp.int32)

    def back_block(query_acc, block_index):
        probabilities, score_grad, key_heads = block_grads(block_index)
        value_term = jnp.einsum(
            "hqk,qhd->khd",
            probabilities.astype(jnp.bfloat16),
            mixed_grad3,
            preferred_element_type=jnp.float32,
        )
        query_acc = query_acc + jnp.einsum(
            "hqk,khd->qhd", score_grad, key_heads, preferred_element_type=jnp.float32
        )
        key_term = jnp.einsum(
            "hqk,qhd->khd", score_grad, queries, preferred_element_type=jnp.float32
        )
        return (query_acc, (key_term.reshape(key_block, -1), value_term.reshape(key_block, -1)))

    query_acc, block_terms = lax.scan(back_block, jnp.zeros(queries.shape, jnp.float32), block_ids)
    key_terms = block_terms[0].reshape(seq_total, -1)
    value_terms = block_terms[1].reshape(seq_total, -1)
    key_part, value_part = (
        lax.psum_scatter(
            key_terms.astype(jnp.bfloat16), "ep", scatter_dimension=0, tiled=True
        ).astype(jnp.float32),
        lax.psum_scatter(
            value_terms.astype(jnp.bfloat16), "ep", scatter_dimension=0, tiled=True
        ).astype(jnp.float32),
    )
    query_lin_grad = (
        rotary(query_acc * q_scale, position, -1.0).reshape(row_count, -1).astype(jnp.bfloat16)
    )
    key_lin_grad = (
        rotary(key_part.reshape(row_count, head_count, head_dim), position, -1.0)
        .reshape(row_count, -1)
        .astype(jnp.bfloat16)
    )
    value_lin_grad = value_part.astype(jnp.bfloat16)
    query_weight_grad = inner_left(hidden_low, query_lin_grad)
    key_weight_grad = inner_left(hidden_low, key_lin_grad)
    value_weight_grad = inner_left(hidden_low, value_lin_grad)
    hidden_grad = (
        inner_right(query_lin_grad, query_weight)
        + inner_right(key_lin_grad, key_weight)
        + inner_right(value_lin_grad, value_weight)
    )
    unused_first, mixer_pull = jax.vjp(normed, stream, mixer_gain)
    stream_part, mixer_gain_grad = mixer_pull(hidden_grad)
    tokens_grad = (residual_grad + stream_part).astype(jnp.bfloat16)
    gate_sum, up_sum, down_sum = (
        lax.psum_scatter(
            own_gate_grad[None].astype(jnp.bfloat16), "grp", scatter_dimension=1, tiled=True
        ).astype(jnp.float32),
        lax.psum_scatter(
            own_up_grad[None].astype(jnp.bfloat16), "grp", scatter_dimension=1, tiled=True
        ).astype(jnp.float32),
        lax.psum_scatter(
            own_down_grad[None].astype(jnp.bfloat16), "grp", scatter_dimension=2, tiled=True
        ).astype(jnp.float32),
    )
    summed = (
        lax.psum_scatter(mixer_gain_grad, ("grp", "ep"), scatter_dimension=0, tiled=True),
        lax.psum_scatter(query_weight_grad, ("grp", "ep"), scatter_dimension=0, tiled=True),
        lax.psum_scatter(key_weight_grad, ("grp", "ep"), scatter_dimension=0, tiled=True),
        lax.psum_scatter(value_weight_grad, ("grp", "ep"), scatter_dimension=0, tiled=True),
        lax.psum_scatter(output_weight_grad, ("grp", "ep"), scatter_dimension=0, tiled=True),
        lax.psum_scatter(ffn_gain_grad, ("grp", "ep"), scatter_dimension=0, tiled=True),
        lax.psum_scatter(router_grad, ("grp", "ep"), scatter_dimension=0, tiled=True),
        lax.psum_scatter(shared_gate_grad, ("grp", "ep"), scatter_dimension=0, tiled=True),
        lax.psum_scatter(shared_up_grad, ("grp", "ep"), scatter_dimension=0, tiled=True),
        lax.psum_scatter(shared_down_grad, ("grp", "ep"), scatter_dimension=1, tiled=True),
    )
    return (
        layer_out.astype(jnp.bfloat16)[None],
        tokens_grad[None],
        summed[0],
        summed[1],
        summed[2],
        summed[3],
        summed[4],
        summed[5],
        summed[6],
        summed[7],
        summed[8],
        summed[9],
        gate_sum,
        up_sum,
        down_sum,
        stream_rms,
    )


def solution(mesh):
    return jax.shard_map(
        local,
        mesh=mesh,
        in_specs=(
            P("grp", "ep", None),
            P("grp", None),
            P("grp", "ep", None),
            P("grp", "ep", None),
            P(),
            P(),
            P(),
            P(),
            P(),
            P(),
            P(),
            P(),
            P(),
            P(),
            P("ep", None, None),
            P("ep", None, None),
            P("ep", None, None),
        ),
        out_specs=(
            P("grp", "ep", None),
            P("grp", "ep", None),
            P(("grp", "ep")),
            P(("grp", "ep"), None),
            P(("grp", "ep"), None),
            P(("grp", "ep"), None),
            P(("grp", "ep"), None),
            P(("grp", "ep")),
            P(("grp", "ep"), None),
            P(("grp", "ep"), None),
            P(("grp", "ep"), None),
            P(None, ("grp", "ep")),
            P("ep", "grp", None),
            P("ep", "grp", None),
            P("ep", None, "grp"),
            P(),
        ),
        check_vma=False,
    )
```

profile of v0, /device:TPU:0, one launch (start us, length us, event | category | flops | bytes accessed | tf_op | source)
XLA Modules:
  0.0 2845.8 jit_solution(1690131014616278346)
XLA Ops:
  36.6 8.1 reduce-window.19
  53.5 68.7 %all-gather.3.cloned.1.call-done = bf16[4096,1280]{0,1:T(8,128)(2,1)} async-done(((bf16[256,1280]{0,1:T(8,128)(2,1)}), bf16[4096,1280]{0,1:T(8,128)(2,1)}) %all-gather.3.cloned.1.call-update) | async-done | bytes 10485776 | tf_op jit(solution)/shard_map/all_gather | solution.py:121
  122.2 20.1 select_reduce_fusion
  142.3 20.1 fusion.11
  162.4 48.9 %all-gather.5.cloned.1.call-done = bf16[4096,1280]{1,0:T(8,128)(2,1)} async-done(((bf16[256,1280]{1,0:T(8,128)(2,1)}), bf16[4096,1280]{1,0:T(8,128)(2,1)}) %all-gather.5.cloned.1.call-update) | async-done | bytes 10485776 | tf_op jit(solution)/shard_map/all_gather | solution.py:122
  211.2 14.3 copy.99
  225.5 21.7 fusion.107
  256.4 7.5 reshape.547
  263.9 16.1 scatter_custom_fusion
  280.0 174.8 %all_to_all.20 = bf16[16,192,1280]{2,1,0:T(8,128)(2,1)S(1)} all-to-all(bf16[16,192,1280]{2,1,0:T(8,128)(2,1)} %bitcast.295), channel_id=1, replica_groups=mesh['grp'=2,'ep'=16] {'ep'}, dimensions={0} | all-to-all | bytes 15728640 | tf_op jit(solution)/shard_map/all_to_all | solution.py:165
  454.8 11.0 fusion.36
  465.8 14.7 multiply_convert_fusion.2
  480.5 12.8 convolution_convert_fusion
  504.5 10.0 mul.445
  517.2 123.0 %all-to-all-done.1 = bf16[16,192,1280]{2,1,0:T(8,128)(2,1)} async-done(((bf16[16,192,1280]{2,1,0:T(8,128)(2,1)}), bf16[16,192,1280]{2,1,0:T(8,128)(2,1)}, u32[]{:S(2)}, u32[]{:S(2)}) %all-to-all-start.1) | async-done | bytes 7864352 | tf_op jit(solution)/shard_map/all_to_all | solution.py:175
  640.3 14.6 gather_fusion
  654.8 7.4 reshape.515
  668.7 24.0 scatter_custom_fusion.1
  692.7 205.4 %all_to_all.21 = bf16[16,192,1280]{2,1,0:T(8,128)(2,1)} all-to-all(bf16[16,192,1280]{2,1,0:T(8,128)(2,1)} %bitcast.294), channel_id=1, replica_groups=mesh['grp'=2,'ep'=16] {'ep'}, dimensions={0} | all-to-all | bytes 15728640 | tf_op jit(solution)/shard_map/all_to_all | solution.py:221
  898.1 22.1 multiply_convert_fusion
  920.2 14.3 fusion.34
  934.5 13.2 add_convert_fusion
  963.1 132.1 %all-to-all-done.3 = bf16[16,192,1280]{2,1,0:T(8,128)(2,1)} async-done(((bf16[16,192,1280]{2,1,0:T(8,128)(2,1)}), bf16[16,192,1280]{2,1,0:T(8,128)(2,1)}, u32[]{:S(2)}, u32[]{:S(2)}) %all-to-all-start.3) | async-done | bytes 7864352 | tf_op jit(solution)/shard_map/all_to_all | solution.py:237
  1095.2 14.6 gather_fusion.1
  1109.7 8.1 reshape.524
  1117.8 8.1 reduce_sum.187
  1139.6 185.4 %while.15 = (s32[]{:T(128)}, f32[256,10,128]{0,2,1:T(8,128)}, bf16[4,1024,1280]{2,1,0:T(8,128)(2,1)}, bf16[4,1024,1280]{2,1,0:T(8,128)(2,1)}, s32[4]{0:T(128)S(1...) while((s32[]{:T(128)}, f32[256,10,128]{0,2,1:T(8,128)}, ...), condition=%wide.region_19.20_spmd.clone, body=%wide.region_17.19_spmd.clone.sunk | while | flops 3377869056 | bytes 197572096 | solution.py:296
  1170.3 5.9 fusion.212
  1216.8 5.9 fusion.212
  1263.1 5.9 fusion.212
  1328.1 12.6 fusion.25
  1340.7 10.3 copy.137
  1355.1 13.3 fusion.23
  1368.5 14.4 fusion.24
  1404.5 69.5 %reduce-scatter.25.cloned.1.call-done = bf16[256,1280]{1,0:T(8,128)(2,1)} async-done(((bf16[4096,1280]{1,0:T(8,128)(2,1)}), bf16[256,1280]{1,0:T(8,128)(2,1)}) %reduce-scatter.25.cloned.1.call-update) | async-done | bytes 655376 | tf_op jit(solution)/shard_map/reduce_scatter | solution.py:300
  1490.1 106.6 %reduce-scatter.27.cloned.1.call-done = bf16[256,1280]{1,0:T(8,128)(2,1)} async-done(((bf16[4096,1280]{1,0:T(8,128)(2,1)}), bf16[256,1280]{1,0:T(8,128)(2,1)}) %reduce-scatter.27.cloned.1.call-update) | async-done | bytes 655376 | tf_op jit(solution)/shard_map/reduce_scatter | solution.py:303
  1609.4 112.1 %all-reduce.9.cloned.1.call-done = f32[1280,16]{0,1:T(8,128)} async-done(((f32[1280,16]{0,1:T(8,128)}), f32[1280,16]{0,1:T(8,128)}) %all-reduce.9.cloned.1.call-update) | async-done | bytes 81936
  1722.8 37.3 %reduce-scatter.41.cloned.1.call-done = bf16[640,896]{1,0:T(8,128)(2,1)} async-done(((bf16[1280,896]{1,0:T(8,128)(2,1)}), bf16[640,896]{1,0:T(8,128)(2,1)}) %reduce-scatter.41.cloned.1.call-update) | async-done | bytes 1146896
  1772.3 24.8 reduce-scatter.37.cloned.1.call-done
  1799.9 33.5 %reduce-scatter.39.cloned.1.call-done = bf16[1,640,896]{2,1,0:T(8,128)(2,1)} async-done(((bf16[1,1280,896]{2,1,0:T(8,128)(2,1)}), bf16[1,640,896]{2,1,0:T(8,128)(2,1)}) %reduce-scatter.39.cloned.1.call-update) | async-done | bytes 1146896 | tf_op jit(solution)/shard_map/reduce_scatter | solution.py:331
  1842.2 40.7 %all-reduce.6 = (f32[1280]{0:T(1024)S(1)}, f32[1280]{0:T(1024)S(1)}, f32[1]{0:T(128)}, f32[1]{0:T(128)}, f32[1]{0:T(128)}) all-reduce(f32[1280]{0:T(1024)S(1)} %get-tuple-element.199, f32[1280]{0:T(1024)S(1)} %copy-done.55, f32[1]{0:T(128)} %bitcast.59, f32[1]{0:T(128)} %bitcast.58, ...), channel_id=4, replica_groups=mesh['grp'=2,'ep'=16] {'grp','ep'}, use_global_device_ids=true, to_apply=%region_24.25.clone | all-reduce | flops 2563 | bytes 20504
  1889.7 88.8 %reduce-scatter.43.cloned.1.call-done = f32[40,896]{1,0:T(8,128)} async-done(((f32[1280,896]{1,0:T(8,128)}), f32[40,896]{1,0:T(8,128)}) %reduce-scatter.43.cloned.1.call-update) | async-done | bytes 143376
  1978.5 140.8 %reduce-scatter.45.cloned.1.call-done = f32[40,896]{1,0:T(8,128)} async-done(((f32[1280,896]{1,0:T(8,128)}), f32[40,896]{1,0:T(8,128)}) %reduce-scatter.45.cloned.1.call-update) | async-done | bytes 143376
  2119.3 141.3 %reduce-scatter.47.cloned.1.call-done = f32[896,40]{0,1:T(8,128)} async-done(((f32[896,1280]{0,1:T(8,128)}), f32[896,40]{0,1:T(8,128)}) %reduce-scatter.47.cloned.1.call-update) | async-done | bytes 143376
  2260.6 144.6 %reduce-scatter.35.cloned.1.call-done = f32[40,1280]{1,0:T(8,128)} async-done(((f32[1280,1280]{1,0:T(8,128)}), f32[40,1280]{1,0:T(8,128)}) %reduce-scatter.35.cloned.1.call-update) | async-done | bytes 204816 | tf_op jit(solution)/shard_map/reduce_scatter | solution.py:343
  2405.2 145.0 %reduce-scatter.29.cloned.1.call-done = f32[40,1280]{1,0:T(8,128)} async-done(((f32[1280,1280]{1,0:T(8,128)}), f32[40,1280]{1,0:T(8,128)}) %reduce-scatter.29.cloned.1.call-update) | async-done | bytes 204816 | tf_op jit(solution)/shard_map/reduce_scatter | solution.py:340
  2550.2 144.4 %reduce-scatter.31.cloned.1.call-done = f32[40,1280]{1,0:T(8,128)} async-done(((f32[1280,1280]{1,0:T(8,128)}), f32[40,1280]{1,0:T(8,128)}) %reduce-scatter.31.cloned.1.call-update) | async-done | bytes 204816 | tf_op jit(solution)/shard_map/reduce_scatter | solution.py:341
  2694.6 144.5 %reduce-scatter.33.cloned.1.call-done = f32[40,1280]{1,0:T(8,128)} async-done(((f32[1280,1280]{1,0:T(8,128)}), f32[40,1280]{1,0:T(8,128)}) %reduce-scatter.33.cloned.1.call-update) | async-done | bytes 204816 | tf_op jit(solution)/shard_map/reduce_scatter | solution.py:342
  (383 shorter events, 349.8 us)
Async XLA Ops:
  7.2 21.6 copy-start
  7.2 115.0 %all-gather.3.cloned.1.call-start = ((), (), s32[]{:S(2)}) async-start(), calls=%async_computation.16 | async-start | bytes 11141120 | tf_op jit(solution)/shard_map/all_gather | solution.py:121
  14.9 13.8 copy-start.49
  28.5 182.8 %all-gather.5.cloned.1.call-start = ((), (), s32[]{:S(2)}) async-start(), calls=%async_computation.17 | async-start | bytes 11141120 | tf_op jit(solution)/shard_map/all_gather | solution.py:122
  31.9 483.9 %copy-start.31 = (s32[1,256,7]{2,1,0:T(8,128)}, s32[1,256,7]{2,1,0:T(8,128)S(1)}, u32[]{:S(2)}) copy-start(s32[1,256,7]{2,1,0:T(8,128)S(1)} %copy.132) | copy-start | bytes 21508
  142.3 20.1 copy-start.45
  162.3 63.2 %copy-start.51 = (f32[10,256]{1,0:T(8,128)}, f32[10,256]{1,0:T(8,128)S(1)}, u32[]{:S(2)}) copy-start(f32[10,256]{1,0:T(8,128)S(1)} %fusion.11) | copy-start | bytes 30724
  280.0 174.8 %copy-start.73 = (bf16[1,1280,896]{2,1,0:T(8,128)(2,1)S(1)}, bf16[1,1280,896]{2,1,0:T(8,128)(2,1)}, u32[]{:S(2)}) copy-start(bf16[1,1280,896]{2,1,0:T(8,128)(2,1)} %param.33) | copy-start | bytes 6881284
  454.8 11.0 copy-start.15
  454.8 11.0 copy-start.74
  465.8 14.7 copy-start.72
  493.3 146.9 %all-to-all-start.1 = ((bf16[16,192,1280]{2,1,0:T(8,128)(2,1)}), bf16[16,192,1280]{2,1,0:T(8,128)(2,1)}, u32[]{:S(2)}, u32[]{:S(2)}) async-start(bf16[16,192,1280]{2,1,0:T(8,128)(2,1)} %bitcast.307), calls=%async_computation.1 | async-start | bytes 15728640 | tf_op jit(solution)/shard_map/all_to_all | solution.py:175
  504.5 10.0 copy-start.43
  516.5 138.3 %copy-start.63 = (f32[256]{0:T(256)}, f32[256]{0:T(256)S(1)}, u32[]{:S(2)}) copy-start(f32[256]{0:T(256)S(1)} %reduce_max.19) | copy-start | bytes 3076
  668.5 293.9 %copy-start.28 = (f32[256,7]{1,0:T(8,128)}, f32[256,7]{1,0:T(8,128)S(1)}, u32[]{:S(2)}) copy-start(f32[256,7]{1,0:T(8,128)S(1)} %get-tuple-element.236) | copy-start | bytes 21508
  920.2 14.4 copy-start.75
  920.2 14.4 copy-start.76
  947.8 147.4 %all-to-all-start.3 = ((bf16[16,192,1280]{2,1,0:T(8,128)(2,1)}), bf16[16,192,1280]{2,1,0:T(8,128)(2,1)}, u32[]{:S(2)}, u32[]{:S(2)}) async-start(bf16[16,192,1280]{2,1,0:T(8,128)(2,1)} %bitcast.306), calls=%async_computation.3 | async-start | bytes 15728640 | tf_op jit(solution)/shard_map/all_to_all | solution.py:237
  953.6 520.4 %reduce-scatter.25.cloned.1.call-start = ((), (), s32[]{:S(2)}) async-start(), calls=%async_computation.18 | async-start | bytes 11141120 | tf_op jit(solution)/shard_map/reduce_scatter | solution.py:300
  963.0 166.5 %copy-start.38 = (f32[256,1,16]{2,1,0:T(1,128)}, f32[256,1,16]{2,1,0:T(1,128)S(1)}, u32[]{:S(2)}) copy-start(f32[256,1,16]{2,1,0:T(1,128)S(1)} %fusion.61) | copy-start | bytes 49156
  1133.3 6.4 copy-start.57
  1144.7 9.8 copy-start.2
  1154.5 6.7 copy-start.3
  1154.5 6.7 copy-start.60
  1190.9 9.8 copy-start.2
  1200.6 7.1 copy-start.3
  1200.6 7.1 copy-start.60
  1237.2 9.8 copy-start.2
  1247.0 7.1 copy-start.3
  1247.0 7.1 copy-start.60
  1283.5 9.8 copy-start.2
  1293.3 7.1 copy-start.3
  1293.3 7.1 copy-start.60
  1325.1 271.7 %reduce-scatter.27.cloned.1.call-start = ((), (), s32[]{:S(2)}) async-start(), calls=%async_computation.19 | async-start | bytes 11141120 | tf_op jit(solution)/shard_map/reduce_scatter | solution.py:303
  1325.7 395.8 %all-reduce.9.cloned.1.call-start = ((), (), s32[]{:S(2)}) async-start(), calls=%async_computation.27 | async-start | bytes 163840
  1328.0 432.1 %reduce-scatter.41.cloned.1.call-start = ((), (), s32[]{:S(2)}) async-start(), calls=%async_computation.26 | async-start | bytes 3440640
  1355.1 442.0 %reduce-scatter.37.cloned.1.call-start = ((), (), s32[]{:S(2)}) async-start(), calls=%async_computation.24 | async-start | bytes 3440640 | tf_op jit(solution)/shard_map/reduce_scatter | solution.py:328
  1368.5 464.9 %reduce-scatter.39.cloned.1.call-start = ((), (), s32[]{:S(2)}) async-start(), calls=%async_computation.25 | async-start | bytes 3440640 | tf_op jit(solution)/shard_map/reduce_scatter | solution.py:331
  1383.0 595.5 %reduce-scatter.43.cloned.1.call-start = ((), (), s32[]{:S(2)}) async-start(), calls=%async_computation.28 | async-start | bytes 4730880
  1387.3 732.0 %reduce-scatter.45.cloned.1.call-start = ((), (), s32[]{:S(2)}) async-start(), calls=%async_computation.29 | async-start | bytes 4730880
  1392.1 868.5 %reduce-scatter.47.cloned.1.call-start = ((), (), s32[]{:S(2)}) async-start(), calls=%async_computation.30 | async-start | bytes 4730880
  1396.5 1008.7 %reduce-scatter.35.cloned.1.call-start = ((), (), s32[]{:S(2)}) async-start(), calls=%async_computation.23 | async-start | bytes 6758400 | tf_op jit(solution)/shard_map/reduce_scatter | solution.py:343
  1401.9 74.6 %copy-start.35 = (f32[256,64]{0,1:T(8,128)S(1)}, f32[256,64]{0,1:T(8,128)}, u32[]{:S(2)}) copy-start(f32[256,64]{0,1:T(8,128)} %copy-done.34) | copy-start | bytes 196612
  1401.9 74.5 %copy-start.40 = (f32[256,64]{0,1:T(8,128)S(1)}, f32[256,64]{0,1:T(8,128)}, u32[]{:S(2)}) copy-start(f32[256,64]{0,1:T(8,128)} %get-tuple-element.261) | copy-start | bytes 196612
  1401.9 1148.3 %reduce-scatter.29.cloned.1.call-start = ((), (), s32[]{:S(2)}) async-start(), calls=%async_computation.20 | async-start | bytes 6758400 | tf_op jit(solution)/shard_map/reduce_scatter | solution.py:340
  1484.3 1210.3 %reduce-scatter.31.cloned.1.call-start = ((), (), s32[]{:S(2)}) async-start(), calls=%async_computation.21 | async-start | bytes 6758400 | tf_op jit(solution)/shard_map/reduce_scatter | solution.py:341
  1490.1 1349.0 %reduce-scatter.33.cloned.1.call-start = ((), (), s32[]{:S(2)}) async-start(), calls=%async_computation.22 | async-start | bytes 6758400 | tf_op jit(solution)/shard_map/reduce_scatter | solution.py:342
  1840.0 46.6 %copy-start.66 = (f32[256]{0:T(256)S(1)}, f32[256]{0:T(256)}, u32[]{:S(2)}) copy-start(f32[256]{0:T(256)} %copy-done.65) | copy-start | bytes 3076
  (70 other events, 227.1 us)
Sparse Core Ops, SparseCore 0:
  28.6 93.5 all-gather.2
  125.0 86.1 all-gather.4
  1325.2 148.7 reduce-scatter.24
  1477.9 118.8 reduce-scatter.26
  1602.2 119.2 all-reduce.8
  1724.1 35.9 reduce-scatter.40
  1763.0 33.9 reduce-scatter.36
  1799.3 33.9 reduce-scatter.38
  1836.3 142.1 reduce-scatter.42
  1981.3 137.9 reduce-scatter.44
  2122.3 138.3 reduce-scatter.46
  2263.5 141.6 reduce-scatter.34
  2408.2 141.9 reduce-scatter.28
  2553.1 141.5 reduce-scatter.30
  2697.5 141.5 reduce-scatter.32
where the time goes:
time: 2850 us
  waiting for transfers between devices  1710 us (60%)
  blocking collectives  421 us (15%)
  matrix products  342 us (12%)
  local copies, waits for them, and re-layouts  243 us (9%)
  other arithmetic  103 us (4%)
    unnamed x20, waiting for transfers between devices  521 us
    all_to_all x1, blocking collectives, local(): lax.all_to_all(grad_send, 'ep', split_axis=0, concat_axis=0, tiled=True)  205 us
    all_to_all x1, blocking collectives, local(): lax.all_to_all(send_rows, 'ep', split_axis=0, concat_axis=0, tiled=True)  175 us
    reduce_scatter x1, waiting for transfers between devices, local(): lax.psum_scatter(query_weight_grad, ('grp', 'ep'), scatter_dimension=0, t...  145 us
    reduce_scatter x1, waiting for transfers between devices, local(): lax.psum_scatter(output_weight_grad, ('grp', 'ep'), scatter_dimension=0,...  145 us
    reduce_scatter x1, waiting for transfers between devices, local(): lax.psum_scatter(value_weight_grad, ('grp', 'ep'), scatter_dimension=0, t...  144 us
    reduce_scatter x1, waiting for transfers between devices, local(): lax.psum_scatter(key_weight_grad, ('grp', 'ep'), scatter_dimension=0, til...  144 us
    all_to_all x1, waiting for transfers between devices, local(): lax.all_to_all(input_grad.reshape(grad_arrived.shape), 'ep', split_axis=0...  132 us
  transfers between devices with their start and end apart: 17, of which 17 were waited for; matrix products, arithmetic and copies ran while one was open for 8% of the time, Pallas kernels for 0%

commit v1 on v0

v1 whole, which is shorter than its diff:
```python
import functools

import jax
import jax.numpy as jnp
from jax import lax
from jax.experimental import pallas as pl
from jax.experimental.pallas import tpu as pltpu
from jax.sharding import PartitionSpec as P

HEADS = 10
HEAD = 128
TOP = 7

epsilon = 1e-06
rope_base = 10000.0
masked_value = -1e30


def normed(values, gain_vec):
    return (
        values * lax.rsqrt(jnp.mean(values * values, axis=-1, keepdims=True) + epsilon) * gain_vec
    )


def rotary(values, positions, direction):
    half_dim = values.shape[-1] // 2
    frequency = rope_base ** (-jnp.arange(half_dim, dtype=jnp.float32) / half_dim)
    angles = positions[:, None] * frequency[None, :]
    cosine = jnp.cos(angles)[:, None, :]
    sine_val = direction * jnp.sin(angles)[:, None, :]
    lower_half = values[..., :half_dim]
    upper_half = values[..., half_dim:]
    return jnp.concatenate(
        [lower_half * cosine - upper_half * sine_val, upper_half * cosine + lower_half * sine_val],
        axis=-1,
    )


def inner_left(left_op, right_op):
    return lax.dot_general(
        left_op, right_op, (((0,), (0,)), ((), ())), preferred_element_type=jnp.float32
    )


def inner_right(left_op, right_op):
    return lax.dot_general(
        left_op, right_op, (((1,), (1,)), ((), ())), preferred_element_type=jnp.float32
    )


def silu_parts(pre_act):
    sigmoid_val = jax.nn.sigmoid(pre_act)
    return (pre_act * sigmoid_val, sigmoid_val * (1.0 + pre_act * (1.0 - sigmoid_val)))


MESH = pl.DeviceIdType.MESH
VMEM_MOST = 64 * 1024 * 1024 - 65536


def when(cond):
    if cond is True:
        return lambda f: f()
    if cond is False:
        return lambda f: None
    return pl.when(cond)


def both(*conds):
    out = True
    for cond in conds:
        if cond is False:
            return False
        if cond is True:
            continue
        out = cond if out is True else jnp.logical_and(out, cond)
    return out


class Plan:
    def __init__(self, ep_count, window):
        self.long = 4
        self.wide = ep_count // 8
        self.window = window
        self.steps = (
            list(range(self.long // 2 + 1))
            if window
            else list(range(-(self.long - 1), self.long))
        )

    def place(self):
        me = lax.axis_index("ep")
        return me // (2 * self.wide), (me // 2) % self.wide, me % 2

    def slot(self, a, b, c):
        return (a * self.wide + b) * 2 + c

    def inside(self, a):
        return jnp.logical_and(a >= 0, a < self.long)

    def need(self, d, b, c, b0, c0):
        if not self.window or 0 < d < self.long // 2:
            return True
        if d == 0:
            return jnp.logical_or(b0 < b, jnp.logical_and(b0 == b, c0 <= c))
        return jnp.logical_or(b0 > b, jnp.logical_and(b0 == b, c0 >= c))

    def need_pair(self, d, b, b0):
        if not self.window or 0 < d < self.long // 2:
            return True
        return b0 < b if d == 0 else b0 > b

    def greet(self, a, b, c):
        barrier = pltpu.get_barrier_semaphore()

        def signal(cond, dev):
            @when(cond)
            def _():
                pl.semaphore_signal(barrier, inc=1, device_id={"ep": dev}, device_id_type=MESH)

        signal(a + 1 < self.long, self.slot(a + 1, b, c))
        signal(a > 0, self.slot(a - 1, b, c))
        for k in range(1, self.wide):
            signal(True, self.slot(a, (b + k) % self.wide, c))
        signal(True, self.slot(a, b, 1 - c))
        ends = (a == 0).astype(jnp.int32) + (a == self.long - 1).astype(jnp.int32)
        pl.semaphore_wait(barrier, self.wide + 2 - ends)


def gather_kernel(plan, pieces, x_ref, out_ref, ra, sa_up, sa_dn, rb, sb, rc, sc, own):
    a, b, c = plan.place()
    steps, wide = plan.steps, plan.wide
    at = {d: i for i, d in enumerate(steps)}
    rows = x_ref.shape[0] // pieces

    def part(q):
        return pl.ds(pl.multiple_of(q * rows, rows), rows)

    def copy(q, src, slot, ssem, rsem, dev):
        return pltpu.make_async_remote_copy(
            src_ref=src, dst_ref=out_ref.at[slot, part(q)], send_sem=ssem, recv_sem=rsem,
            device_id={"ep": dev}, device_id_type=MESH,
        )

    def hops(d, q):
        i = at[d]
        slot = plan.slot(a - d, b, c)
        src = x_ref.at[part(q)] if d == 0 else out_ref.at[slot, part(q)]
        real = plan.inside(a - d)
        out = []
        if d >= 0 and d + 1 in at:
            out.append((both(real, a + 1 < plan.long), lambda: copy(
                q, src, slot, sa_up.at[i, q], ra.at[at[d + 1], q], plan.slot(a + 1, b, c))))
        if d <= 0 and d - 1 in at:
            out.append((both(real, a > 0), lambda: copy(
                q, src, slot, sa_dn.at[i, q], ra.at[at[d - 1], q], plan.slot(a - 1, b, c))))
        for k in range(1, wide):
            to = (b + k) % wide
            out.append((both(real, plan.need_pair(d, to, b)), lambda k=k, to=to: copy(
                q, src, slot, sb.at[i, k, q], rb.at[i, k, q], plan.slot(a, to, c))))
        out.append((both(real, plan.need(d, b, 1 - c, b, c)), lambda: copy(
            q, src, slot, sc.at[i, 0, q], rc.at[i, 0, q], plan.slot(a, b, 1 - c))))
        return out

    def cross(d, k, q):
        i = at[d]
        b0 = (b + wide - k) % wide
        slot = plan.slot(a - d, b0, c)
        real = plan.inside(a - d)
        come = lambda: copy(q, x_ref.at[part(q)], slot, sb.at[i, k, q], rb.at[i, k, q], plan.slot(a, b, c))
        go = lambda: copy(q, out_ref.at[slot, part(q)], slot, sc.at[i, k, q], rc.at[i, k, q],
                          plan.slot(a, b, 1 - c))
        return (both(real, plan.need_pair(d, b, b0)), come,
                both(real, plan.need(d, b, 1 - c, b0, c)), go)

    plan.greet(a, b, c)
    keep = pltpu.make_async_copy(x_ref, out_ref.at[plan.slot(a, b, c)], own)

    @pl.loop(0, pieces)
    def _(q):
        for cond, go in hops(0, q):
            @when(cond)
            def _(go=go):
                go().start()

    keep.start()
    far = max(abs(d) for d in steps)
    for step in range(1, far + 3):
        @pl.loop(0, pieces)
        def _(q, step=step):
            for d in (step, -step):
                if d in at:
                    @when(plan.inside(a - d))
                    def _(d=d):
                        slot = plan.slot(a - d, b, c)
                        copy(q, x_ref.at[part(q)], slot, sa_up.at[0, q], ra.at[at[d], q],
                             plan.slot(a, b, c)).wait_recv()
                        for cond, go in hops(d, q):
                            @when(cond)
                            def _(go=go):
                                go().start()
            for d in sorted({step - 2, 2 - step}) if step > 1 else ():
                if d in at:
                    for k in range(1, wide):
                        came, come, goes, go = cross(d, k, q)
                        @when(came)
                        def _(come=come):
                            come().wait_recv()
                        @when(goes)
                        def _(go=go):
                            go().start()
    keep.wait()

    @pl.loop(0, pieces)
    def _(q):
        for d in steps:
            i = at[d]
            real = plan.inside(a - d)
            for k in range(wide):
                b0 = (b + wide - k) % wide
                slot = plan.slot(a - d, b0, 1 - c)
                @when(both(real, plan.need(d, b, c, b0, 1 - c)))
                def _(slot=slot, i=i, k=k):
                    copy(q, x_ref.at[part(q)], slot, sc.at[i, k, q], rc.at[i, k, q],
                         plan.slot(a, b, c)).wait_recv()
            for cond, go in hops(d, q):
                @when(cond)
                def _(go=go):
                    go().wait_send()
            for k in range(1, wide):
                came, come, goes, go = cross(d, k, q)
                @when(goes)
                def _(go=go):
                    go().wait_send()


def gather_rows(block, window, collective_id, pieces=4):
    ep_count = lax.axis_size("ep")
    plan = Plan(ep_count, window)
    n, wide = len(plan.steps), plan.wide
    sem = pltpu.SemaphoreType.DMA
    return pl.pallas_call(
        functools.partial(gather_kernel, plan, pieces),
        out_shape=jax.ShapeDtypeStruct((ep_count,) + block.shape, block.dtype),
        in_specs=[pl.BlockSpec(memory_space=pltpu.VMEM)],
        out_specs=pl.BlockSpec(memory_space=pl.ANY),
        scratch_shapes=[sem((n, pieces)), sem((n, pieces)), sem((n, pieces)), sem((n, wide, pieces)),
                        sem((n, wide, pieces)), sem((n, wide, pieces)), sem((n, wide, pieces)), sem],
        compiler_params=pltpu.CompilerParams(collective_id=collective_id, has_side_effects=True),
        name="gather_rows",
    )(block)


def add_rows(dst, others, out=None):
    rows = dst.shape[0]
    piece = next(p for p in (32, 16, 8, rows) if rows % p == 0)
    out = dst if out is None else out

    @pl.loop(0, rows // piece)
    def _(i):
        at = pl.ds(pl.multiple_of(i * piece, piece), piece)
        if len(others) == 1 and out.dtype == jnp.bfloat16:
            out[at, :] = dst[at, :] + others[0][at, :]
        else:
            total = dst[at, :].astype(jnp.float32)
            for other in others:
                total = total + other[at, :].astype(jnp.float32)
            out[at, :] = total.astype(out.dtype)


def scatter_kernel(plan, pieces, p_ref, out_ref, held, rcb, rbb, r_hi, r_lo, sc, rc, sb, rb, sa, rhi, rlo, ld):
    a, b, c = plan.place()
    steps, wide = plan.steps, plan.wide
    at = {d: i for i, d in enumerate(steps)}
    rows = p_ref.shape[1] // pieces

    def part(q):
        return pl.ds(pl.multiple_of(q * rows, rows), rows)

    def remote(src, dst, ssem, rsem, dev):
        return pltpu.make_async_remote_copy(
            src_ref=src, dst_ref=dst, send_sem=ssem, recv_sem=rsem,
            device_id={"ep": dev}, device_id_type=MESH,
        )

    order = sorted(steps, key=lambda d: -abs(d))
    ks = list(range(1, wide)) + [0]

    def load(d, k, q):
        i, b0 = at[d], (b + wide - k) % wide
        return (both(plan.inside(a - d), plan.need(d, b, c, b0, c)), lambda: pltpu.make_async_copy(
            p_ref.at[plan.slot(a - d, b0, c), part(q)], held.at[i, k, part(q)], ld.at[i, k, q]))

    def cross(d, k, q):
        i, b0 = at[d], (b + wide - k) % wide
        real = plan.inside(a - d)
        return (both(real, plan.need(d, b, c, b0, 1 - c)), lambda: remote(
            p_ref.at[plan.slot(a - d, b0, 1 - c), part(q)], rcb.at[i, k, part(q)], sc.at[i, k, q],
            rc.at[i, k, q], plan.slot(a, b, 1 - c)), both(real, plan.need(d, b, 1 - c, b0, c)))

    def over(d, k, q):
        i, b0 = at[d], (b + wide - k) % wide
        return (both(plan.inside(a - d), plan.need_pair(d, b, b0)), lambda: remote(
            held.at[i, k, part(q)], rbb.at[i, k - 1, part(q)], sb.at[i, k, q], rb.at[i, k, q],
            plan.slot(a, b0, c)))

    def along(d, q):
        i, up = at[d], d < 0
        j = at[d + 1 if up else d - 1]
        return plan.inside(a - d), lambda: remote(
            held.at[i, 0, part(q)], (r_lo if up else r_hi).at[j, part(q)], sa.at[i, q],
            (rlo if up else rhi).at[j, q], plan.slot(a + (1 if up else -1), b, c))

    plan.greet(a, b, c)
    for k in ks:
        @pl.loop(0, pieces)
        def _(q, k=k):
            for d in order:
                for cond, go in (cross(d, k, q)[:2], load(d, k, q)):
                    @when(cond)
                    def _(go=go):
                        go().start()

    def first(d, k, q):
        cond, go = load(d, k, q)
        @when(cond)
        def _():
            go().wait()
        _, cross_go, come = cross(d, k, q)
        @when(come)
        def _():
            cross_go().wait_recv()
            add_rows(held.at[at[d], k, part(q)], [rcb.at[at[d], k, part(q)]])

    for k in ks[:-1]:
        @pl.loop(0, pieces)
        def _(q, k=k):
            for d in order:
                first(d, k, q)
                cond, go = over(d, k, q)
                @when(cond)
                def _(go=go):
                    go().start()
    for d in order:
        @pl.loop(0, pieces)
        def _(q, d=d):
            i = at[d]
            real = plan.inside(a - d)
            first(d, 0, q)
            for k in range(1, wide):
                frm = (b + k) % wide
                @when(both(real, plan.need_pair(d, frm, b)))
                def _(k=k):
                    over(d, k, q)[1]().wait_recv()
                    add_rows(held.at[i, 0, part(q)], [rbb.at[i, k - 1, part(q)]])
            for inner, cond, buf, sem in ((d >= 0 and d + 1 in at, a + 1 < plan.long, r_hi, rhi),
                                          (d <= 0 and d - 1 in at, a > 0, r_lo, rlo)):
                if inner:
                    @when(both(real, cond))
                    def _(buf=buf, sem=sem):
                        remote(held.at[i, 0, part(q)], buf.at[i, part(q)], sa.at[i, q], sem.at[i, q],
                               plan.slot(a, b, c)).wait_recv()
                        add_rows(held.at[i, 0, part(q)], [buf.at[i, part(q)]])
            if d:
                cond, go = along(d, q)
                @when(cond)
                def _():
                    go().start()
    out_ref[...] = held[at[0], 0]

    @pl.loop(0, pieces)
    def _(q):
        for d in steps:
            sends = [cross(d, k, q)[:2] for k in range(wide)] + [over(d, k, q) for k in range(1, wide)]
            if d:
                sends.append(along(d, q))
            for cond, go in sends:
                @when(cond)
                def _(go=go):
                    go().wait_send()


def scatter_rows(parts, window, collective_id, pieces=4):
    ep_count, rows, width = parts.shape
    plan = Plan(ep_count, window)
    n, wide = len(plan.steps), plan.wide
    sem = lambda *lead: pltpu.SemaphoreType.DMA(lead + (pieces,))
    blocks = lambda *lead: pltpu.VMEM(lead + (rows, width), parts.dtype)
    return pl.pallas_call(
        functools.partial(scatter_kernel, plan, pieces),
        out_shape=jax.ShapeDtypeStruct((rows, width), parts.dtype),
        in_specs=[pl.BlockSpec(memory_space=pl.ANY)],
        out_specs=pl.BlockSpec(memory_space=pltpu.VMEM),
        scratch_shapes=[blocks(n, wide), blocks(n, wide), blocks(n, wide - 1), blocks(n), blocks(n),
                        sem(n, wide), sem(n, wide), sem(n, wide), sem(n, wide),
                        sem(n), sem(n), sem(n), sem(n, wide)],
        compiler_params=pltpu.CompilerParams(
            collective_id=collective_id, has_side_effects=True, vmem_limit_bytes=VMEM_MOST),
        name="scatter_rows",
    )(parts)


def whole_kernel(sizes, small, p_ref, s_ref, out_ref, so_ref, held, rcb, rxb, rbb, rab, sbuf, *sems):
    groups, long, wide = sizes
    g = lax.axis_index("grp")
    me = lax.axis_index("ep")
    a, b, c = me // (2 * wide), (me // 2) % wide, me % 2
    sc, rc, sx, rx, sb, rb, sa, ra, ld, ss, rs = sems

    def dev(gg, aa, bb, cc):
        return {"grp": gg, "ep": (aa * wide + bb) * 2 + cc}

    def slot(gg, aa, bb, cc):
        return ((gg * long + aa) * wide + bb) * 2 + cc

    def remote(src, dst, ssem, rsem, to):
        return pltpu.make_async_remote_copy(
            src_ref=src, dst_ref=dst, send_sem=ssem, recv_sem=rsem, device_id=to, device_id_type=MESH)

    peers = ([dev(g, a, b, 1 - c)] + [dev((g + k) % groups, a, b, c) for k in range(1, groups)]
             + [dev(g, a, (b + k) % wide, c) for k in range(1, wide)]
             + [dev(g, (a + k) % long, b, c) for k in range(1, long)])
    barrier = pltpu.get_barrier_semaphore()
    for to in peers:
        pl.semaphore_signal(barrier, inc=1, device_id=to, device_id_type=MESH)
    pl.semaphore_wait(barrier, len(peers))

    def spot(kx, ka, kb, cc):
        return slot((g + groups - kx) % groups, (a + long - ka) % long, (b + wide - kb) % wide, cc)

    keys = [(kx, ka, kb) for kx in list(range(1, groups)) + [0] for kb in list(range(1, wide)) + [0]
            for ka in list(range(1, long)) + [0]]
    cross = {}
    load = {}
    for kx, ka, kb in keys:
        key = (kx, ka, kb)
        cross[key] = remote(p_ref.at[spot(kx, ka, kb, 1 - c)], rcb.at[key], sc.at[key], rc.at[key],
                            dev(g, a, b, 1 - c))
        load[key] = pltpu.make_async_copy(p_ref.at[spot(kx, ka, kb, c)], held.at[key], ld.at[key])
        cross[key].start()
        load[key].start()

    def over_x(kx, ka, kb):
        return remote(held.at[kx, ka, kb], rxb.at[kx - 1, ka, kb], sx.at[kx - 1, ka, kb], rx.at[kx - 1, ka, kb],
                      dev((g + groups - kx) % groups, a, b, c))

    def over_b(ka, kb):
        return remote(held.at[0, ka, kb], rbb.at[ka, kb - 1], sb.at[ka, kb - 1], rb.at[ka, kb - 1],
                      dev(g, a, (b + wide - kb) % wide, c))

    def over_a(ka):
        return remote(held.at[0, ka, 0], rab.at[ka - 1], sa.at[ka - 1], ra.at[ka - 1],
                      dev(g, (a + long - ka) % long, b, c))

    for key in keys:
        load[key].wait()
        cross[key].wait_recv()
        add_rows(held.at[key], [rcb.at[key]])
        if key[0]:
            over_x(*key).start()

    if small:
        sbuf[0] = s_ref[...]
        spot_of = 1
        rounds = [[dev(g, a, b, 1 - c)],
                  [dev((g + k) % groups, a, b, c) for k in range(1, groups)],
                  [dev(g, a, (b + k) % wide, c) for k in range(1, wide)],
                  [dev(g, (a + k) % long, b, c) for k in range(1, long)]]
        copies = []
        for tos in rounds:
            mine = []
            for to in tos:
                mine.append(remote(so_ref if len(copies) else sbuf.at[0], sbuf.at[spot_of], ss.at[spot_of], rs.at[spot_of], to))
                spot_of += 1
            copies.append(mine)

    for kb in list(range(1, wide)) + [0]:
        for ka in list(range(1, long)) + [0]:
            for kx in range(1, groups):
                over_x(kx, ka, kb).wait_recv()
            add_rows(held.at[0, ka, kb], [rxb.at[kx - 1, ka, kb] for kx in range(1, groups)])
            if kb:
                over_b(ka, kb).start()
    for ka in list(range(1, long)) + [0]:
        for kb in range(1, wide):
            over_b(ka, kb).wait_recv()
        add_rows(held.at[0, ka, 0], [rbb.at[ka, kb - 1] for kb in range(1, wide)])
        if ka:
            over_a(ka).start()
    for ka in range(1, long):
        over_a(ka).wait_recv()
    add_rows(held.at[0, 0, 0], [rab.at[ka - 1] for ka in range(1, long)], out_ref)
    for key in keys:
        cross[key].wait_send()
        if key[0]:
            over_x(*key).wait_send()
    for ka in range(long):
        for kb in range(1, wide):
            over_b(ka, kb).wait_send()
        if ka:
            over_a(ka).wait_send()


def scatter_whole(parts, collective_id):
    count, rows, width = parts.shape
    groups, ep_count = lax.axis_size("grp"), lax.axis_size("ep")
    long, wide = 4, ep_count // 8
    sem = pltpu.SemaphoreType.DMA
    blocks = lambda *lead: pltpu.VMEM(lead + (rows, width), parts.dtype)
    full = (groups, long, wide)

    def kernel(p_ref, out_ref, *scratch):
        whole_kernel(full, False, p_ref, None, out_ref, None, *scratch[:5], None, *scratch[5:], None, None)

    return pl.pallas_call(
        kernel,
        out_shape=jax.ShapeDtypeStruct((rows, width), jnp.float32),
        in_specs=[pl.BlockSpec(memory_space=pl.ANY)],
        out_specs=pl.BlockSpec(memory_space=pltpu.VMEM),
        scratch_shapes=[blocks(*full), blocks(*full), blocks(groups - 1, long, wide), blocks(long, wide - 1),
                        blocks(long - 1),
                        sem(full), sem(full), sem((groups - 1, long, wide)), sem((groups - 1, long, wide)),
                        sem((long, wide - 1)), sem((long, wide - 1)), sem((long - 1,)), sem((long - 1,)), sem(full)],
        compiler_params=pltpu.CompilerParams(
            collective_id=collective_id, has_side_effects=True, vmem_limit_bytes=VMEM_MOST),
        name="scatter_whole",
    )(parts)


def visible_bias(shape, key_axis, first_key, start, first_query):
    key_pos = first_key + lax.broadcasted_iota(jnp.int32, shape, key_axis)
    query_pos = first_query + lax.broadcasted_iota(jnp.int32, shape, 1 - key_axis)
    seen = jnp.logical_and(key_pos >= start, key_pos <= query_pos)
    return jnp.where(seen, 0.0, masked_value)


def heads_at(h):
    return pl.ds(pl.multiple_of(h * HEAD, HEAD), HEAD)


def attend_kernel(info, q_ref, start_ref, kv_ref, mixed_ref, low_ref, total_ref, bias, top, norm, acc):
    step = pl.program_id(0)
    me, first_block = info[0], info[1]
    rows, width = q_ref.shape
    block = me - step

    @pl.when(step == 0)
    def _():
        top[...] = jnp.full_like(top, masked_value)
        norm[...] = jnp.zeros_like(norm)
        acc[...] = jnp.zeros_like(acc)

    @pl.when(block >= first_block)
    def _():
        bias[...] = visible_bias((rows, rows), 1, block * rows, start_ref[...], me * rows)

        @pl.loop(0, HEADS)
        def _(h):
            at = heads_at(h)
            values = kv_ref[0, :, pl.ds(pl.multiple_of(width + h * HEAD, HEAD), HEAD)]
            scores = inner_right(q_ref[:, at], kv_ref[0, :, at]) + bias[...]
            old = top[h]
            new = jnp.maximum(old, jnp.max(scores, axis=1, keepdims=True))
            weights = jnp.exp(scores - new)
            shrink = jnp.exp(old - new)
            top[h] = new
            norm[h] = norm[h] * shrink + jnp.sum(weights, axis=1, keepdims=True)
            acc[:, at] = acc[:, at] * shrink + jnp.dot(
                weights.astype(jnp.bfloat16), values, preferred_element_type=jnp.float32
            )

    @pl.when(step == pl.num_programs(0) - 1)
    def _():
        @pl.loop(0, HEADS)
        def _(h):
            at = heads_at(h)
            mixed = acc[:, at] / norm[h]
            mixed_ref[:, at] = mixed
            low_ref[:, at] = mixed.astype(jnp.bfloat16)
            total_ref[h] = top[h] + jnp.log(norm[h])


def attend(info, queries, start, pairs):
    rows, width = queries.shape
    steps = pairs.shape[0] // 2 + 1
    whole = lambda *shape: pl.BlockSpec(shape, lambda s, info: (0,) * len(shape))
    return pl.pallas_call(
        attend_kernel,
        out_shape=(
            jax.ShapeDtypeStruct((rows, width), jnp.float32),
            jax.ShapeDtypeStruct((rows, width), jnp.bfloat16),
            jax.ShapeDtypeStruct((HEADS, rows, 1), jnp.float32),
        ),
        grid_spec=pltpu.PrefetchScalarGridSpec(
            num_scalar_prefetch=1,
            grid=(steps,),
            in_specs=[
                whole(rows, width),
                whole(rows, 1),
                pl.BlockSpec((1, rows, 2 * width), lambda s, info: (jnp.maximum(info[0] - s, info[1]), 0, 0)),
            ],
            out_specs=(whole(rows, width), whole(rows, width), whole(HEADS, rows, 1)),
            scratch_shapes=[
                pltpu.VMEM((rows, rows), jnp.float32),
                pltpu.VMEM((HEADS, rows, 1), jnp.float32),
                pltpu.VMEM((HEADS, rows, 1), jnp.float32),
                pltpu.VMEM((rows, width), jnp.float32),
            ],
        ),
        cost_estimate=pl.CostEstimate(
            flops=4 * rows * rows * width * steps, bytes_accessed=4 * rows * width * steps, transcendentals=0
        ),
        name="attend",
    )(info, queries, start, pairs)


def attend_back_kernel(info, q_ref, g_ref, start_ref, total_ref, term_ref, kv_ref, dkv_ref, dq_ref, bias, acc):
    step = pl.program_id(0)
    me, first_block = info[0], info[1]
    rows, width = q_ref.shape
    block = me - step

    @pl.when(step == 0)
    def _():
        acc[...] = jnp.zeros_like(acc)

    @pl.when(block >= first_block)
    def _():
        bias[...] = visible_bias((rows, rows), 0, block * rows, start_ref[...], me * rows)

        @pl.loop(0, HEADS)
        def _(h):
            at = heads_at(h)
            late = pl.ds(pl.multiple_of(width + h * HEAD, HEAD), HEAD)
            keys, values = kv_ref[0, :, at], kv_ref[0, :, late]
            queries, grads = q_ref[:, at], g_ref[:, at]
            probs = jnp.exp(inner_right(keys, queries) + bias[...] - total_ref[h])
            prob_grad = inner_right(values, grads)
            score_grad = (probs * (prob_grad - term_ref[h])).astype(jnp.bfloat16)
            dkv_ref[0, :, late] = jnp.dot(
                probs.astype(jnp.bfloat16), grads, preferred_element_type=jnp.float32
            ).astype(jnp.bfloat16)
            dkv_ref[0, :, at] = jnp.dot(
                score_grad, queries, preferred_element_type=jnp.float32
            ).astype(jnp.bfloat16)
            acc[h] += inner_left(keys, score_grad)

    @pl.when(jnp.logical_and(block >= 0, block < first_block))
    def _():
        dkv_ref[...] = jnp.zeros_like(dkv_ref)

    @pl.when(step == pl.num_programs(0) - 1)
    def _():
        for h in range(HEADS):
            dq_ref[:, h * HEAD : (h + 1) * HEAD] = acc[h].T


def attend_back(info, queries, grads, start, total, term, pairs):
    rows, width = queries.shape
    count = pairs.shape[0]
    steps = count // 2 + 1
    whole = lambda *shape: pl.BlockSpec(shape, lambda s, info: (0,) * len(shape))
    return pl.pallas_call(
        attend_back_kernel,
        out_shape=(
            jax.ShapeDtypeStruct(pairs.shape, jnp.bfloat16),
            jax.ShapeDtypeStruct((rows, width), jnp.float32),
        ),
        grid_spec=pltpu.PrefetchScalarGridSpec(
            num_scalar_prefetch=1,
            grid=(steps,),
            in_specs=[
                whole(rows, width),
                whole(rows, width),
                whole(1, rows),
                whole(HEADS, 1, rows),
                whole(HEADS, 1, rows),
                pl.BlockSpec((1, rows, 2 * width), lambda s, info: (jnp.maximum(info[0] - s, info[1]), 0, 0)),
            ],
            out_specs=(
                pl.BlockSpec((1, rows, 2 * width), lambda s, info: (jnp.maximum(info[0] - s, 0), 0, 0)),
                whole(rows, width),
            ),
            scratch_shapes=[
                pltpu.VMEM((rows, rows), jnp.float32),
                pltpu.VMEM((HEADS, HEAD, rows), jnp.float32),
            ],
        ),
        cost_estimate=pl.CostEstimate(
            flops=10 * rows * rows * width * steps, bytes_accessed=8 * rows * width * steps, transcendentals=0
        ),
        name="attend_back",
    )(info, queries, grads, start, total, term, pairs)


def local(
    tokens,
    doc_lengths,
    expert_ids,
    out_grad,
    mixer_gain,
    query_weight,
    key_weight,
    value_weight,
    output_weight,
    ffn_gain,
    router_weight,
    shared_gate,
    shared_up,
    shared_down,
    expert_gate,
    expert_up,
    expert_down,
):
    rows, width = tokens.shape[1], tokens.shape[2]
    ep_count = lax.axis_size("ep")
    device_count = ep_count * lax.axis_size("grp")
    ep_index = lax.axis_index("ep")
    expert_count = router_weight.shape[1]
    capacity = min(rows, 12 * rows * TOP // (7 * expert_count))
    q_scale = HEAD ** (-0.5)
    low = lambda v: v.astype(jnp.bfloat16)
    wide = lambda v: v.astype(jnp.float32)
    dot = lambda left, right: jnp.dot(left, right, preferred_element_type=jnp.float32)

    grad_low = out_grad[0]
    grads_all = lax.all_gather(grad_low, "ep", axis=0, tiled=False)

    doc_ends = jnp.cumsum(doc_lengths[0])
    query_pos = ep_index * rows + jnp.arange(rows, dtype=jnp.int32)
    before = query_pos[:, None] >= doc_ends[None, :]
    start = jnp.max(jnp.where(before, doc_ends[None, :], 0), axis=1)
    info = jnp.stack([ep_index, start[0] // rows]).astype(jnp.int32)
    position = wide(query_pos)

    stream = wide(tokens[0])
    hidden_low = low(normed(stream, mixer_gain))
    heads = lambda v: v.reshape(rows, HEADS, HEAD)
    queries = low(rotary(heads(dot(hidden_low, query_weight)), position, 1.0) * q_scale).reshape(rows, width)
    keys = low(rotary(heads(dot(hidden_low, key_weight)), position, 1.0)).reshape(rows, width)
    values = low(dot(hidden_low, value_weight))
    pairs = gather_rows(jnp.concatenate([keys, values], axis=1), True, 1)
    mixed, mixed_low, log_total = attend(info, queries, start[:, None], pairs)
    mixer_out = dot(mixed_low, output_weight)
    residual = stream + mixer_out
    ffn_low = low(normed(residual, ffn_gain))

    logits = dot(ffn_low, router_weight)
    experts = jnp.arange(expert_count, dtype=jnp.int32)
    assigned = jnp.any(expert_ids[0][:, :, None] == experts[None, None, :], axis=1)
    shown = jnp.where(assigned, logits, masked_value)
    powers = jnp.where(assigned, jnp.exp(shown - jnp.max(shown, axis=1, keepdims=True)), 0.0)
    gate_probs = powers / jnp.sum(powers, axis=1, keepdims=True)
    probs_high = low(gate_probs)
    probs_rest = low(gate_probs - wide(probs_high))
    side = width + 2 * HEAD if 2 * expert_count > HEAD else width + HEAD
    pad = jnp.zeros((rows, side - width - 2 * expert_count), jnp.bfloat16)
    sent = jnp.concatenate([ffn_low, probs_high, probs_rest, pad], axis=1)
    arrived = gather_rows(sent, False, 2)

    own = experts[None, None, :] == ep_index
    high = arrived[:, :, width : width + expert_count]
    rest = arrived[:, :, width + expert_count : width + 2 * expert_count]
    share = jnp.sum(jnp.where(own, wide(high) + wide(rest), 0.0), axis=2)
    chosen = share > 0.0
    earlier = (jnp.arange(rows)[:, None] < jnp.arange(rows)[None, :]).astype(jnp.bfloat16)
    rank = dot(low(chosen), earlier).astype(jnp.int32)
    pick = (rank[:, None, :] == jnp.arange(capacity, dtype=jnp.int32)[None, :, None]) & chosen[:, None, :]
    pick_low = low(pick)
    take = lambda block: low(
        jnp.einsum("srt,std->srd", pick_low, block, preferred_element_type=jnp.float32)
    ).reshape(ep_count * capacity, -1)
    put = lambda flat: low(
        jnp.einsum(
            "srt,srd->std", pick_low, flat.reshape(ep_count, capacity, -1), preferred_element_type=jnp.float32
        )
    )
    flat_in = take(arrived[:, :, :width])
    flat_out_grad = take(grads_all)
    flat_share = jnp.sum(jnp.where(pick, share[:, None, :], 0.0), axis=2).reshape(-1, 1)
    gate_pre = dot(flat_in, expert_gate[0])
    up_pre = dot(flat_in, expert_up[0])
    expert_silu, expert_slope = silu_parts(gate_pre)
    middle = low(expert_silu * up_pre)
    result = low(dot(middle, expert_down[0]))
    gate_grad = jnp.sum(wide(result) * wide(flat_out_grad), axis=1, keepdims=True)
    result_grad = low(flat_share * wide(flat_out_grad))
    mid_grad = inner_right(result_grad, expert_down[0])
    pre_grad = low(mid_grad * up_pre * expert_slope)
    lift_grad = low(mid_grad * expert_silu)
    input_grad = low(inner_right(pre_grad, expert_gate[0]) + inner_right(lift_grad, expert_up[0]))
    gate_high = low(gate_grad)
    gate_rest = low(gate_grad - wide(gate_high))
    mine = low(experts[None, :] == ep_index)
    back = jnp.concatenate(
        [input_grad, gate_high * mine, gate_rest * mine,
         jnp.zeros((flat_in.shape[0], side - width - 2 * expert_count), jnp.bfloat16)], axis=1
    )
    back_sum = scatter_rows(put(back), False, 3)
    routed = wide(lax.psum_scatter(put(low(flat_share * wide(result))), "ep", scatter_dimension=0))
    half = lambda v: v.reshape(v.shape[0], lax.axis_size("grp"), -1)
    own_down_grad = low(jnp.einsum("rf,rgd->gfd", middle, half(result_grad), preferred_element_type=jnp.float32))
    own_gate_grad = low(inner_left(flat_in, pre_grad))
    own_up_grad = low(inner_left(flat_in, lift_grad))
    over_groups = lambda v: wide(lax.psum_scatter(v, "grp", scatter_dimension=0, tiled=True))
    gate_sum = over_groups(own_gate_grad)[None]
    up_sum = over_groups(own_up_grad)[None]
    down_sum = over_groups(own_down_grad)

    shared_pre = dot(ffn_low, shared_gate)
    shared_lift = dot(ffn_low, shared_up)
    shared_silu, shared_slope = silu_parts(shared_pre)
    shared_mid = low(shared_silu * shared_lift)
    shared_out = dot(shared_mid, shared_down)
    grad_out = wide(grad_low)
    shared_mid_grad = inner_right(grad_low, shared_down)
    shared_pre_grad = low(shared_mid_grad * shared_lift * shared_slope)
    shared_lift_grad = low(shared_mid_grad * shared_silu)
    ffn_grad = inner_right(shared_pre_grad, shared_gate) + inner_right(shared_lift_grad, shared_up)

    layer_out = residual + shared_out + routed
    gate_back = wide(back_sum[:, width : width + expert_count]) + wide(
        back_sum[:, width + expert_count : width + 2 * expert_count]
    )
    chosen_grad = gate_probs * (gate_back - jnp.sum(gate_probs * gate_back, axis=1, keepdims=True))
    logit_grad = low(chosen_grad)
    ffn_grad = ffn_grad + wide(back_sum[:, :width]) + inner_right(logit_grad, router_weight)
    _, ffn_pull = jax.vjp(normed, residual, ffn_gain)
    residual_part, ffn_gain_grad = ffn_pull(ffn_grad)
    residual_grad = grad_out + residual_part
    mixer_grad_low = low(residual_grad)
    mixed_grad = low(inner_right(mixer_grad_low, output_weight))
    row_term = jnp.sum(heads(wide(mixed_grad) * mixed), axis=2)
    pair_parts, query_sum = attend_back(
        info, queries, mixed_grad, start[None, :], log_total.reshape(HEADS, 1, rows),
        row_term.T.reshape(HEADS, 1, rows), pairs,
    )
    pair_grads = scatter_rows(pair_parts, True, 4)

    by_device = lambda v: low(v).reshape(device_count, width // device_count, -1)
    early = jnp.concatenate(
        [by_device(inner_left(ffn_low, shared_pre_grad)), by_device(inner_left(ffn_low, shared_lift_grad)),
         by_device(inner_left(grad_low, shared_mid)), by_device(inner_left(mixed_low, mixer_grad_low))], axis=2
    )
    early_sum = scatter_whole(early, 5)

    query_lin_grad = low(rotary(heads(query_sum * q_scale), position, -1.0)).reshape(rows, width)
    key_lin_grad = low(rotary(heads(wide(pair_grads[:, :width])), position, -1.0)).reshape(rows, width)
    value_lin_grad = pair_grads[:, width:]
    hidden_grad = (
        inner_right(query_lin_grad, query_weight)
        + inner_right(key_lin_grad, key_weight)
        + inner_right(value_lin_grad, value_weight)
    )
    _, mixer_pull = jax.vjp(normed, stream, mixer_gain)
    stream_part, mixer_gain_grad = mixer_pull(hidden_grad)
    tokens_grad = low(residual_grad + stream_part)

    squares = jnp.stack(
        [jnp.sum(residual * residual), jnp.sum(mixer_out * mixer_out), jnp.sum(layer_out * layer_out)]
    )
    extras = jnp.concatenate(
        [inner_left(ffn_low, logit_grad), mixer_gain_grad[:, None], ffn_gain_grad[:, None],
         jnp.broadcast_to(squares[None, :], (width, 3))], axis=1
    )
    extras = jnp.pad(extras, ((0, 0), (0, HEAD - extras.shape[1])))
    late = jnp.concatenate(
        [by_device(inner_left(hidden_low, query_lin_grad)), by_device(inner_left(hidden_low, key_lin_grad)),
         by_device(inner_left(hidden_low, value_lin_grad)), by_device(extras)], axis=2
    )
    late_sum = scatter_whole(late, 6)
    extra_sum = late_sum[:, 3 * width :]
    entry_count = rows * device_count * width
    stream_rms = jnp.sqrt(extra_sum[0, expert_count + 2 : expert_count + 5] / entry_count)
    ff = shared_gate.shape[1]
    return (
        low(layer_out)[None],
        tokens_grad[None],
        extra_sum[:, expert_count],
        late_sum[:, :width],
        late_sum[:, width : 2 * width],
        late_sum[:, 2 * width : 3 * width],
        early_sum[:, 3 * ff :],
        extra_sum[:, expert_count + 1],
        extra_sum[:, :expert_count],
        early_sum[:, :ff],
        early_sum[:, ff : 2 * ff],
        early_sum[:, 2 * ff : 3 * ff].T,
        gate_sum,
        up_sum,
        down_sum,
        stream_rms,
    )


def solution(mesh):
    return jax.shard_map(
        local,
        mesh=mesh,
        in_specs=(
            P("grp", "ep", None),
            P("grp", None),
            P("grp", "ep", None),
            P("grp", "ep", None),
            P(),
            P(),
            P(),
            P(),
            P(),
            P(),
            P(),
            P(),
            P(),
            P(),
            P("ep", None, None),
            P("ep", None, None),
            P("ep", None, None),
        ),
        out_specs=(
            P("grp", "ep", None),
            P("grp", "ep", None),
            P(("grp", "ep")),
            P(("grp", "ep"), None),
            P(("grp", "ep"), None),
            P(("grp", "ep"), None),
            P(("grp", "ep"), None),
            P(("grp", "ep")),
            P(("grp", "ep"), None),
            P(("grp", "ep"), None),
            P(("grp", "ep"), None),
            P(None, ("grp", "ep")),
            P("ep", "grp", None),
            P("ep", "grp", None),
            P("ep", None, "grp"),
            P(),
        ),
        check_vma=False,
    )
```

time: 2850 us -> 1090 us (0.38)
  waiting for transfers between devices: 1710 us -> 0.75 us
  Pallas kernels: 0 us -> 693 us
  blocking collectives: 421 us -> 0 us
  local copies, waits for them, and re-layouts: 243 us -> 104 us
  matrix products: 342 us -> 223 us
  other arithmetic: 103 us -> 50.5 us
    reduce_scatter x8 -> x4, waiting for transfers between devices: 813 us -> 0.01 us  [the longest x3 0.01 us: local(): lax.psum_scatter(v, 'grp', scatter_dimension=0, tiled=True)]
    pallas_call x0 -> x8, Pallas kernels: none -> 693 us  [the longest x2 245 us: scatter_whole(): pl.pallas_call(kernel, out_shape=jax.ShapeDtypeStruct((rows, width), jnp....]
    unnamed x20 -> x5, waiting for transfers between devices: 521 us -> 0.75 us
    all_to_all x2 -> x0, blocking collectives: 380 us -> none  [the longest x1 205 us: local(): lax.all_to_all(grad_send, 'ep', split_axis=0, concat_axis=0, tiled=True)]
    all_to_all x2 -> x0, waiting for transfers between devices: 255 us -> none  [the longest x1 132 us: local(): lax.all_to_all(input_grad.reshape(grad_arrived.shape), 'ep', split_axis=0...]
    all_gather x2 -> x1, waiting for transfers between devices: 118 us -> 0.01 us  [local(): grads_all = lax.all_gather(grad_low, 'ep', axis=0, tiled=False)]
    dot_general x37 -> x17, matrix products: 200 us -> 112 us  [the longest x12 59.7 us: local(): jnp.dot(left, right, preferred_element_type=jnp.float32)]
    dynamic_update_slice x12 -> x0, local copies, waits for them, and re-layouts: 56.5 us -> none  [local(): lax.scan(back_block, jnp.zeros(queries.shape, jnp.float32), block_ids)]
  transfers between devices with their start and end apart: 17 -> 5, of which waited for: 17 -> 0; matrix products, arithmetic and copies ran while one was open for 8% -> 23% of each run, Pallas kernels for 0% -> 56%
where the time goes in v1:
time: 1090 us
  Pallas kernels  693 us (64%)
  matrix products  223 us (20%)
  local copies, waits for them, and re-layouts  104 us (10%)
  other arithmetic  50.5 us (5%)
  between operations  17.4 us (2%)
    pallas_call x2, Pallas kernels, scatter_whole(): pl.pallas_call(kernel, out_shape=jax.ShapeDtypeStruct((rows, width), jnp....  245 us
    pallas_call x2, Pallas kernels, scatter_rows(): pl.pallas_call(functools.partial(scatter_kernel, plan, pieces), out_shape...  216 us
    pallas_call x2, Pallas kernels, gather_rows(): pl.pallas_call(functools.partial(gather_kernel, plan, pieces), out_shape=...  212 us
    dot_general x11, matrix products, inner_right(): lax.dot_general(left_op, right_op, (((1,), (1,)), ((), ())), preferred_el...  67.5 us
    dot_general x12, matrix products, local(): jnp.dot(left, right, preferred_element_type=jnp.float32)  59.7 us
    convert_element_type x2, local copies, waits for them, and re-layouts, local(): wide = lambda v: v.astype(jnp.float32)  43.4 us
    dot_general x10, matrix products, inner_left(): lax.dot_general(left_op, right_op, (((0,), (0,)), ((), ())), preferred_el...  42.8 us
    unnamed x142, local copies, waits for them, and re-layouts  27.8 us
  transfers between devices with their start and end apart: 5, of which 0 were waited for; matrix products, arithmetic and copies ran while one was open for 23% of the time, Pallas kernels for 56%

profile of v1, /device:TPU:0, one launch (start us, length us, event | category | flops | bytes accessed | tf_op | source)
XLA Modules:
  0.0 1088.6 jit_solution(8698068973108306444)
XLA Ops:
  12.0 5.6 copy.102
  17.6 5.8 copy.101
  24.6 3.2 fusion.61
  31.7 3.0 convolution_convert_fusion.13
  35.9 55.6 %gather_rows.2.kv_ref = bf16[16,256,2560]{2,1,0:T(8,128)(2,1)} custom-call(bf16[256,2560]{1,0:T(8,128)(2,1)} %pad_maximum_fusion.2.x_ref), custom_call_target="tpu_custom_call" | custom-call | tf_op jit(solution)/shard_map/gather_rows/pallas_call | solution.py:241
  92.3 11.1 %attend.1 = (f32[256,1280]{1,0:T(8,128)}, bf16[256,1280]{1,0:T(8,128)(2,1)}, f32[10,256,1]{2,1,0:T(8,128)}) custom-call(s32[2]{0:T(128)} %pad_add_fusion.info, bf16[256,1280]{1,0:T(8,128)(2,1)} %copy.104.q_ref, s32[256,1]{1,0:T(8,128)} %copy.105.start_ref, bf16[16,256,2560]{2,1,0:T(8,128)(2,1)} %gather_rows.2.kv_ref), custom_call_target="tpu_custom_call" | custom-call | flops 3019898880 | bytes 11796480 | tf_op jit(solution)/shard_map/attend/pallas_call | solution.py:586
  103.4 3.9 multiply_reduce_fusion.5
  111.0 156.0 %gather_rows.3 = bf16[16,256,1408]{2,1,0:T(8,128)(2,1)} custom-call(bf16[256,1408]{1,0:T(8,128)(2,1)} %concatenate.35.x_ref), custom_call_target="tpu_custom_call" | custom-call | tf_op jit(solution)/shard_map/gather_rows/pallas_call | solution.py:241
  267.5 2.6 select_reduce_fusion.1
  271.1 9.5 fusion.7
  280.6 13.7 %fusion.27 = f32[3072,896]{1,0:T(8,128)} fusion(bf16[3072,1280]{1,0:T(8,128)(2,1)} %bitcast.199, bf16[1,1280,896]{2,1,0:T(8,128)(2,1)S(1)} %copy-done.64), kind=kOutput, calls=%fused_computation.55 | convolution fusion | flops 7046430720 | bytes 21168128 | tf_op jit(solution)/shard_map/dot_general | solution.py:723
  294.4 11.1 %fusion.23 = f32[3072,896]{1,0:T(8,128)} fusion(bf16[3072,1280]{1,0:T(8,128)(2,1)S(1)} %bitcast.202, bf16[1,1280,896]{2,1,0:T(8,128)(2,1)S(1)} %copy-done.65), kind=kOutput, calls=%fused_computation.51 | convolution fusion | flops 7046430720 | bytes 21168128 | tf_op jit(solution)/shard_map/dot_general | solution.py:723
  305.5 13.7 %multiply_convert_fusion.1 = (bf16[16,192,1280]{2,1,0:T(8,128)(2,1)}, f32[16,192,1280]{2,1,0:T(8,128)}) fusion(f32[16,192]{1,0:T(8,128)S(1)} %select_reduce_fusion, bf16[16,256,1280]{2,1,0:T(8,128)(2,1)} %all-gather.2.cloned.1.call-done, s32[16,256]{1,0:T(8,128)S(1)} %convolution_convert_fusion.15, pred[16,256]{1,0:T(8,128)(4,1)S(1)} %broadcast_compare_fusion), kind=kOutput, calls=%fused_computation.6 | convolution fusion | flops 2030567424 | bytes 34111488 | tf_op jit(solution)/shard_map/srt,std->srd/dot_general | solution.py:770
  319.1 19.6 %reshape.405 = f32[3072,2,640]{2,1,0:T(2,128)} reshape(f32[16,192,1280]{2,1,0:T(8,128)} %get-tuple-element.157) | data formatting | bytes 31457280 | tf_op jit(solution)/shard_map/convert_element_type | solution.py:722
  338.8 23.7 %copy.117 = f32[3072,2,640]{0,2,1:T(8,128)} copy(f32[3072,2,640]{2,1,0:T(2,128)} %reshape.405) | data formatting | bytes 31457280 | tf_op jit(solution)/shard_map/convert_element_type | solution.py:722
  362.5 21.2 %multiply_convert_fusion.2 = (bf16[3072,896]{1,0:T(8,128)(2,1)}, bf16[3072,896]{1,0:T(8,128)(2,1)}, bf16[3072,896]{1,0:T(8,128)(2,1)}) fusion(f32[3072,896]{1,0:T(8,128)} %fusion.27, f32[3072,896]{1,0:T(8,128)} %fusion.23, bf16[3072,1280]{1,0:T(8,128)(2,1)} %bitcast.192, bf16[1,896,1280]{2,1,0:T(8,128)(2,1)S(1)} %copy-done.62), kind=kOutput, calls=%fused_computation.10 | convolution fusion | flops 7087718400 | bytes 48693248 | tf_op jit(solution)/shard_map/dot_general | solution.py:46
  383.7 14.3 %convert_bitcast_fusion = bf16[2,896,640]{1,2,0:T(8,128)(2,1)} fusion(bf16[3072,896]{1,0:T(8,128)(2,1)} %get-tuple-element.122, f32[3072,2,640]{0,2,1:T(8,128)} %copy.117, f32[3072]{0:T(1024)S(1)} %mul.445), kind=kOutput, calls=%fused_computation.57 | convolution fusion | flops 7055441920 | bytes 23539712 | tf_op jit(solution)/shard_map/rf,rgd->gfd/dot_general | solution.py:801
  398.1 13.7 %convolution_convert_fusion.8 = bf16[1280,896]{1,0:T(8,128)(2,1)} fusion(bf16[3072,1280]{1,0:T(8,128)(2,1)} %bitcast.200, bf16[3072,896]{1,0:T(8,128)(2,1)} %get-tuple-element.121), kind=kOutput, calls=%fused_computation.30 | convolution fusion | flops 7047577600 | bytes 15663104 | tf_op jit(solution)/shard_map/dot_general | solution.py:40
  417.9 13.4 %convolution_convert_fusion.7 = bf16[1280,896]{1,0:T(8,128)(2,1)} fusion(bf16[3072,1280]{1,0:T(8,128)(2,1)} %bitcast.201, bf16[3072,896]{1,0:T(8,128)(2,1)} %get-tuple-element.120), kind=kOutput, calls=%fused_computation.29 | convolution fusion | flops 7047577600 | bytes 15663104 | tf_op jit(solution)/shard_map/dot_general | solution.py:40
  432.7 3.8 multiply_convert_fusion.9
  438.0 3.4 copy.116
  441.5 2.3 convolution_convert_fusion.10
  443.8 2.3 convolution_convert_fusion.11
  446.0 2.0 fusion.90
  448.0 14.9 %fusion.1 = (f32[3072]{0:T(1024)S(1)}, bf16[3072,1280]{1,0:T(8,128)(2,1)S(1)}) fusion(f32[16,192,1280]{2,1,0:T(8,128)} %get-tuple-element.157, f32[3072]{0:T(1024)S(1)} %mul.445, bf16[3072,896]{1,0:T(8,128)(2,1)} %get-tuple-element.122, bf16[1,896,1280]{2,1,0:T(8,128)(2,1)S(1)} %copy-done.63), kind=kOutput, calls=%fused_computation.3 | convolution fusion | flops 7070020608 | bytes 31416320 | tf_op jit(solution)/shard_map/dot_general | solution.py:723
  463.0 5.6 convolution_convert_fusion.1
  468.6 14.5 %fusion.25 = f32[3072,1280]{0,1:T(8,128)} fusion(bf16[3072,896]{1,0:T(8,128)(2,1)} %get-tuple-element.121, bf16[1,1280,896]{2,1,0:T(8,128)(2,1)} %param.31), kind=kOutput, calls=%fused_computation.53 | convolution fusion | flops 7046430720 | bytes 23527424 | tf_op jit(solution)/shard_map/dot_general | solution.py:46
  483.2 13.4 %add_convert_fusion = bf16[3072,1280]{0,1:T(8,128)(2,1)S(1)} fusion(f32[3072,1280]{0,1:T(8,128)} %fusion.25, bf16[3072,896]{1,0:T(8,128)(2,1)} %get-tuple-element.120, bf16[1,1280,896]{2,1,0:T(8,128)(2,1)S(1)} %copy-done.66), kind=kOutput, calls=%fused_computation.5 | convolution fusion | flops 7054295040 | bytes 31391744 | tf_op jit(solution)/shard_map/dot_general | solution.py:46
  496.6 10.2 maximum_maximum_fusion
  506.8 11.5 %copy.110 = bf16[3072,1408]{1,0:T(8,128)(2,1)} copy(bf16[3072,1408]{0,1:T(8,128)(2,1)} %maximum_maximum_fusion) | data formatting | bytes 17301504 | tf_op jit(solution)/shard_map/concatenate | solution.py:794
  518.2 9.7 convolution_convert_fusion.p_ref
  527.9 127.2 %scatter_rows.2 = bf16[256,1408]{1,0:T(8,128)(2,1)} custom-call(bf16[16,256,1408]{2,1,0:T(8,128)(2,1)} %convolution_convert_fusion.p_ref), custom_call_target="tpu_custom_call" | custom-call | tf_op jit(solution)/shard_map/scatter_rows/pallas_call | solution.py:388
  656.3 3.3 fusion.17
  659.8 2.3 multiply_reduce_fusion.2
  667.9 9.4 attend_back.1
  677.3 88.9 %scatter_rows.3 = bf16[256,2560]{1,0:T(8,128)(2,1)} custom-call(bf16[16,256,2560]{2,1,0:T(8,128)(2,1)} %get-tuple-element.25.p_ref), custom_call_target="tpu_custom_call" | custom-call | tf_op jit(solution)/shard_map/scatter_rows/pallas_call | solution.py:388
  767.8 2.6 broadcast_multiply_fusion
  779.6 2.9 fusion.47
  786.1 4.5 pad_maximum_fusion.1.p_ref
  790.7 156.8 %scatter_whole.3 = f32[40,3968]{1,0:T(8,128)} custom-call(bf16[32,40,3968]{2,1,0:T(8,128)(2,1)} %pad_maximum_fusion.1.p_ref), custom_call_target="tpu_custom_call" | custom-call | tf_op jit(solution)/shard_map/scatter_whole/pallas_call | solution.py:514
  955.3 3.0 convolution_convert_fusion.5
  958.3 2.9 convolution_convert_fusion.6
  962.4 2.9 copy.119
  965.3 2.8 bitcast_convert_fusion.1
  968.1 2.8 bitcast_convert_fusion
  970.9 4.7 multiply_reduce_fusion
  979.7 7.8 pad_maximum_fusion.p_ref
  987.4 88.3 %scatter_whole.2 = f32[40,3968]{1,0:T(8,128)} custom-call(bf16[32,40,3968]{2,1,0:T(8,128)(2,1)} %pad_maximum_fusion.p_ref), custom_call_target="tpu_custom_call" | custom-call | tf_op jit(solution)/shard_map/scatter_whole/pallas_call | solution.py:514
  (226 shorter events, 64.2 us)
Async XLA Ops:
  7.2 298.3 %all-gather.2.cloned.1.call-start = ((), (), s32[]{:S(2)}) async-start(), calls=%async_computation.5 | async-start | bytes 11141120 | tf_op jit(solution)/shard_map/all_gather | solution.py:726
  7.9 954.5 %reduce-scatter.11.cloned.1.call-start = ((), (), s32[]{:S(2)}) async-start(), calls=%async_computation.8 | async-start | bytes 3440640 | tf_op jit(solution)/shard_map/reduce_scatter | solution.py:804
  8.9 21.8 %copy-start.57 = (s32[256]{0:T(256)}, s32[256]{0:T(256)S(1)}, u32[]{:S(2)}) copy-start(s32[256]{0:T(256)S(1)} %select_reduce_fusion.2) | copy-start | bytes 3076
  17.6 5.8 copy-start.1
  17.6 7.0 copy-start.39
  23.7 8.1 copy-start.46
  24.6 4.4 copy-start.36
  24.6 3.2 copy-start.22
  35.9 55.6 %copy-start.56 = (s32[1,256,7]{1,0,2:T(1,128)S(1)}, s32[1,256,7]{1,0,2:T(1,128)}, u32[]{:S(2)}) copy-start(s32[1,256,7]{1,0,2:T(1,128)} %param.19) | copy-start | bytes 21508
  103.4 5.0 copy-start.44
  103.4 5.2 copy-start.42
  107.3 2.7 copy-start.58
  107.3 2.7 copy-start.52
  108.6 335.2 %copy-start = (bf16[256,1280]{1,0:T(8,128)(2,1)}, bf16[256,1280]{1,0:T(8,128)(2,1)S(1)}, u32[]{:S(2)}) copy-start(bf16[256,1280]{1,0:T(8,128)(2,1)S(1)} %multiply_convert_fusion.8) | copy-start | bytes 1966084
  271.1 9.6 copy-start.64
  280.6 13.7 %copy-start.13 = (bf16[16,192,1280]{2,1,0:T(8,128)(2,1)S(1)}, bf16[16,192,1280]{2,1,0:T(8,128)(2,1)}, u32[]{:S(2)}) copy-start(bf16[16,192,1280]{2,1,0:T(8,128)(2,1)} %fusion.7) | copy-start | bytes 23592964
  280.6 13.7 %copy-start.65 = (bf16[1,1280,896]{2,1,0:T(8,128)(2,1)S(1)}, bf16[1,1280,896]{2,1,0:T(8,128)(2,1)}, u32[]{:S(2)}) copy-start(bf16[1,1280,896]{2,1,0:T(8,128)(2,1)} %param.32) | copy-start | bytes 6881284
  338.8 23.7 %copy-start.62 = (bf16[1,896,1280]{2,1,0:T(8,128)(2,1)S(1)}, bf16[1,896,1280]{2,1,0:T(8,128)(2,1)}, u32[]{:S(2)}) copy-start(bf16[1,896,1280]{2,1,0:T(8,128)(2,1)} %param.33) | copy-start | bytes 6881284
  398.0 567.3 %reduce-scatter.7.cloned.1.call-start = ((), (), s32[]{:S(2)}) async-start(), calls=%async_computation.6 | async-start | bytes 3440640 | tf_op jit(solution)/shard_map/reduce_scatter | solution.py:804
  411.8 556.3 %reduce-scatter.9.cloned.1.call-start = ((), (), s32[]{:S(2)}) async-start(), calls=%async_computation.7 | async-start | bytes 3440640 | tf_op jit(solution)/shard_map/reduce_scatter | solution.py:804
  431.3 539.6 %reduce-scatter.5.cloned.1.call-start = ((), (), s32[]{:S(2)}) async-start(), calls=%async_computation.4 | async-start | bytes 11141120 | tf_op jit(solution)/shard_map/reduce_scatter | solution.py:799
  432.7 4.6 copy-start.17
  436.4 5.1 copy-start.31
  468.6 14.5 %copy-start.60 = (bf16[16]{0:T(256)(128)(2,1)S(1)}, bf16[16]{0:T(256)(128)(2,1)}, u32[]{:S(2)}) copy-start(bf16[16]{0:T(256)(128)(2,1)} %get-tuple-element.163) | copy-start | bytes 100
  468.6 14.6 %copy-start.66 = (bf16[1,1280,896]{2,1,0:T(8,128)(2,1)S(1)}, bf16[1,1280,896]{2,1,0:T(8,128)(2,1)}, u32[]{:S(2)}) copy-start(bf16[1,1280,896]{2,1,0:T(8,128)(2,1)} %param.32) | copy-start | bytes 6881284
  656.3 3.4 copy-start.55
  656.3 3.4 copy-start.5
  656.3 3.4 copy-start.30
  656.3 3.4 copy-start.43
  656.3 3.4 copy-start.45
  656.3 3.4 copy-start.53
  662.1 2.8 copy-start.35
  662.5 4.3 copy-start.6
  767.8 4.3 copy-start.51
  767.8 4.9 copy-start.37
  767.8 4.9 copy-start.38
  773.2 3.1 copy-start.24
  773.2 3.0 copy-start.14
  779.6 3.5 copy-start.7
  779.6 3.5 copy-start.29
  783.1 3.0 copy-start.12
  947.5 5.8 copy-start.3
  947.5 5.8 copy-start.20
  955.3 3.0 copy-start.25
  958.3 2.9 copy-start.8
  958.3 2.9 copy-start.34
  970.9 6.7 copy-start.49
  970.9 6.7 copy-start.50
  (25 other events, 46.5 us)
Sparse Core Ops, SparseCore 0:
  10.3 116.7 all-gather.1
  398.1 51.4 reduce-scatter.10
  452.0 33.9 reduce-scatter.6
  488.2 33.9 reduce-scatter.8
  526.6 142.8 reduce-scatter.4

commit v2 on v1

--- a/solution.py
+++ b/solution.py
@@ -19,20 +19,6 @@
 def normed(values, gain_vec):
     return (
         values * lax.rsqrt(jnp.mean(values * values, axis=-1, keepdims=True) + epsilon) * gain_vec
-    )
-
-
-def rotary(values, positions, direction):
-    half_dim = values.shape[-1] // 2
-    frequency = rope_base ** (-jnp.arange(half_dim, dtype=jnp.float32) / half_dim)
-    angles = positions[:, None] * frequency[None, :]
-    cosine = jnp.cos(angles)[:, None, :]
-    sine_val = direction * jnp.sin(angles)[:, None, :]
-    lower_half = values[..., :half_dim]
-    upper_half = values[..., half_dim:]
-    return jnp.concatenate(
-        [lower_half * cosine - upper_half * sine_val, upper_half * cosine + lower_half * sine_val],
-        axis=-1,
     )
 
 
@@ -399,12 +385,12 @@
     )(parts)
 
 
-def whole_kernel(sizes, small, p_ref, s_ref, out_ref, so_ref, held, rcb, rxb, rbb, rab, sbuf, *sems):
+def whole_kernel(sizes, p_ref, out_ref, held, rcb, rxb, rbb, rab, *sems):
     groups, long, wide = sizes
     g = lax.axis_index("grp")
     me = lax.axis_index("ep")
     a, b, c = me // (2 * wide), (me // 2) % wide, me % 2
-    sc, rc, sx, rx, sb, rb, sa, ra, ld, ss, rs = sems
+    sc, rc, sx, rx, sb, rb, sa, ra, ld = sems
 
     def dev(gg, aa, bb, cc):
         return {"grp": gg, "ep": (aa * wide + bb) * 2 + cc}
@@ -457,21 +443,6 @@
         add_rows(held.at[key], [rcb.at[key]])
         if key[0]:
             over_x(*key).start()
-
-    if small:
-        sbuf[0] = s_ref[...]
-        spot_of = 1
-        rounds = [[dev(g, a, b, 1 - c)],
-                  [dev((g + k) % groups, a, b, c) for k in range(1, groups)],
-                  [dev(g, a, (b + k) % wide, c) for k in range(1, wide)],
-                  [dev(g, (a + k) % long, b, c) for k in range(1, long)]]
-        copies = []
-        for tos in rounds:
-            mine = []
-            for to in tos:
-                mine.append(remote(so_ref if len(copies) else sbuf.at[0], sbuf.at[spot_of], ss.at[spot_of], rs.at[spot_of], to))
-                spot_of += 1
-            copies.append(mine)
 
     for kb in list(range(1, wide)) + [0]:
         for ka in list(range(1, long)) + [0]:
@@ -509,7 +480,7 @@
     full = (groups, long, wide)
 
     def kernel(p_ref, out_ref, *scratch):
-        whole_kernel(full, False, p_ref, None, out_ref, None, *scratch[:5], None, *scratch[5:], None, None)
+        whole_kernel(full, p_ref, out_ref, *scratch)
 
     return pl.pallas_call(
         kernel,
@@ -526,84 +497,124 @@
     )(parts)
 
 
-def visible_bias(shape, key_axis, first_key, start, first_query):
-    key_pos = first_key + lax.broadcasted_iota(jnp.int32, shape, key_axis)
-    query_pos = first_query + lax.broadcasted_iota(jnp.int32, shape, 1 - key_axis)
+def visible_bias(shape, first_key, start, first_query):
+    key_pos = first_key + lax.broadcasted_iota(jnp.int32, shape, 0)
+    query_pos = first_query + lax.broadcasted_iota(jnp.int32, shape, 1)
     seen = jnp.logical_and(key_pos >= start, key_pos <= query_pos)
     return jnp.where(seen, 0.0, masked_value)
 
 
-def heads_at(h):
-    return pl.ds(pl.multiple_of(h * HEAD, HEAD), HEAD)
-
-
-def attend_kernel(info, q_ref, start_ref, kv_ref, mixed_ref, low_ref, total_ref, bias, top, norm, acc):
+def lanes(first):
+    return pl.ds(pl.multiple_of(first, HEAD), HEAD)
+
+
+def turned(values, cosine, sine):
+    return values * cosine + pltpu.roll(values, HEAD // 2, 1) * sine
+
+
+def whole_spec(*shape):
+    return pl.BlockSpec(shape, lambda *s: (0,) * len(shape))
+
+
+def project_kernel(x_ref, gain_ref, cos_ref, sin_ref, wq_ref, wk_ref, wv_ref, hid_ref, q_ref, kv_ref, hidden):
+    @pl.when(pl.program_id(0) == 0)
+    def _():
+        hidden[...] = normed(x_ref[...].astype(jnp.float32), gain_ref[...]).astype(jnp.bfloat16)
+        hid_ref[...] = hidden[...]
+
+    cosine, sine = cos_ref[...], sin_ref[...]
+    q = jnp.dot(hidden[...], wq_ref[...], preferred_element_type=jnp.float32)
+    k = jnp.dot(hidden[...], wk_ref[...], preferred_element_type=jnp.float32)
+    v = jnp.dot(hidden[...], wv_ref[...], preferred_element_type=jnp.float32)
+    for h in range(q.shape[1] // HEAD):
+        at = slice(h * HEAD, (h + 1) * HEAD)
+        q_ref[:, at] = (turned(q[:, at], cosine, sine) * HEAD ** (-0.5)).astype(jnp.bfloat16)
+        kv_ref[:, 2 * h * HEAD : (2 * h + 1) * HEAD] = turned(k[:, at], cosine, sine).astype(jnp.bfloat16)
+        kv_ref[:, (2 * h + 1) * HEAD : (2 * h + 2) * HEAD] = v[:, at].astype(jnp.bfloat16)
+
+
+def project(tokens, gain, cosine, sine, wq, wk, wv):
+    rows, width = tokens.shape
+    tile = 2 * HEAD
+    column = pl.BlockSpec((width, tile), lambda i: (0, i))
+    return pl.pallas_call(
+        project_kernel,
+        out_shape=(
+            jax.ShapeDtypeStruct((rows, width), jnp.bfloat16),
+            jax.ShapeDtypeStruct((rows, width), jnp.bfloat16),
+            jax.ShapeDtypeStruct((rows, 2 * width), jnp.bfloat16),
+        ),
+        grid=(width // tile,),
+        in_specs=[whole_spec(rows, width), whole_spec(1, width), whole_spec(rows, HEAD), whole_spec(rows, HEAD),
+                  column, column, column],
+        out_specs=(whole_spec(rows, width), pl.BlockSpec((rows, tile), lambda i: (0, i)),
+                   pl.BlockSpec((rows, 2 * tile), lambda i: (0, i))),
+        scratch_shapes=[pltpu.VMEM((rows, width), jnp.bfloat16)],
+        cost_estimate=pl.CostEstimate(flops=6 * rows * width * width, bytes_accessed=6 * width * width, transcendentals=0),
+        name="project",
+    )(tokens, gain[None, :], cosine, sine, wq, wk, wv)
+
+
+def attend_kernel(info, q_ref, start_ref, kv_ref, mixed_ref, low_ref, total_ref, bias, top, norm):
     step = pl.program_id(0)
     me, first_block = info[0], info[1]
-    rows, width = q_ref.shape
+    rows = q_ref.shape[0]
     block = me - step
 
     @pl.when(step == 0)
     def _():
         top[...] = jnp.full_like(top, masked_value)
         norm[...] = jnp.zeros_like(norm)
-        acc[...] = jnp.zeros_like(acc)
+        mixed_ref[...] = jnp.zeros_like(mixed_ref)
 
     @pl.when(block >= first_block)
     def _():
-        bias[...] = visible_bias((rows, rows), 1, block * rows, start_ref[...], me * rows)
-
-        @pl.loop(0, HEADS)
+        bias[...] = visible_bias((rows, rows), block * rows, start_ref[...], me * rows)
+
+        @pl.loop(0, HEADS, unroll=2)
         def _(h):
-            at = heads_at(h)
-            values = kv_ref[0, :, pl.ds(pl.multiple_of(width + h * HEAD, HEAD), HEAD)]
-            scores = inner_right(q_ref[:, at], kv_ref[0, :, at]) + bias[...]
+            keys, values = kv_ref[0, :, lanes(2 * h * HEAD)], kv_ref[0, :, lanes((2 * h + 1) * HEAD)]
+            scores = inner_right(keys, q_ref[:, lanes(h * HEAD)]) + bias[...]
             old = top[h]
-            new = jnp.maximum(old, jnp.max(scores, axis=1, keepdims=True))
+            new = jnp.maximum(old, jnp.max(scores, axis=0, keepdims=True))
             weights = jnp.exp(scores - new)
             shrink = jnp.exp(old - new)
             top[h] = new
-            norm[h] = norm[h] * shrink + jnp.sum(weights, axis=1, keepdims=True)
-            acc[:, at] = acc[:, at] * shrink + jnp.dot(
-                weights.astype(jnp.bfloat16), values, preferred_element_type=jnp.float32
-            )
+            norm[h] = norm[h] * shrink + jnp.sum(weights, axis=0, keepdims=True)
+            mixed_ref[h] = mixed_ref[h] * shrink + inner_left(values, weights.astype(jnp.bfloat16))
 
     @pl.when(step == pl.num_programs(0) - 1)
     def _():
-        @pl.loop(0, HEADS)
-        def _(h):
-            at = heads_at(h)
-            mixed = acc[:, at] / norm[h]
-            mixed_ref[:, at] = mixed
-            low_ref[:, at] = mixed.astype(jnp.bfloat16)
+        for h in range(HEADS):
+            mixed = mixed_ref[h] / norm[h]
+            mixed_ref[h] = mixed
+            low_ref[:, h * HEAD : (h + 1) * HEAD] = mixed.T.astype(jnp.bfloat16)
             total_ref[h] = top[h] + jnp.log(norm[h])
 
 
 def attend(info, queries, start, pairs):
     rows, width = queries.shape
     steps = pairs.shape[0] // 2 + 1
-    whole = lambda *shape: pl.BlockSpec(shape, lambda s, info: (0,) * len(shape))
     return pl.pallas_call(
         attend_kernel,
         out_shape=(
-            jax.ShapeDtypeStruct((rows, width), jnp.float32),
+            jax.ShapeDtypeStruct((HEADS, HEAD, rows), jnp.float32),
             jax.ShapeDtypeStruct((rows, width), jnp.bfloat16),
-            jax.ShapeDtypeStruct((HEADS, rows, 1), jnp.float32),
+            jax.ShapeDtypeStruct((HEADS, 1, rows), jnp.float32),
         ),
         grid_spec=pltpu.PrefetchScalarGridSpec(
             num_scalar_prefetch=1,
             grid=(steps,),
             in_specs=[
-                whole(rows, width),
-                whole(rows, 1),
+                whole_spec(rows, width),
+                whole_spec(1, rows),
                 pl.BlockSpec((1, rows, 2 * width), lambda s, info: (jnp.maximum(info[0] - s, info[1]), 0, 0)),
             ],
-            out_specs=(whole(rows, width), whole(rows, width), whole(HEADS, rows, 1)),
+            out_specs=(whole_spec(HEADS, HEAD, rows), whole_spec(rows, width), whole_spec(HEADS, 1, rows)),
             scratch_shapes=[
                 pltpu.VMEM((rows, rows), jnp.float32),
-                pltpu.VMEM((HEADS, rows, 1), jnp.float32),
-                pltpu.VMEM((HEADS, rows, 1), jnp.float32),
-                pltpu.VMEM((rows, width), jnp.float32),
+                pltpu.VMEM((HEADS, 1, rows), jnp.float32),
+                pltpu.VMEM((HEADS, 1, rows), jnp.float32),
             ],
         ),
         cost_estimate=pl.CostEstimate(
@@ -613,33 +624,37 @@
     )(info, queries, start, pairs)
 
 
-def attend_back_kernel(info, q_ref, g_ref, start_ref, total_ref, term_ref, kv_ref, dkv_ref, dq_ref, bias, acc):
+def attend_back_kernel(
+    info, q_ref, g_ref, mixed_ref, start_ref, total_ref, cos_ref, sin_ref, kv_ref, dkv_ref, dq_ref, bias, acc, term
+):
     step = pl.program_id(0)
     me, first_block = info[0], info[1]
-    rows, width = q_ref.shape
+    rows = q_ref.shape[0]
     block = me - step
 
     @pl.when(step == 0)
     def _():
         acc[...] = jnp.zeros_like(acc)
+        for h in range(HEADS):
+            grads = g_ref[:, h * HEAD : (h + 1) * HEAD].astype(jnp.float32).T
+            term[h] = jnp.sum(grads * mixed_ref[h], axis=0, keepdims=True)
 
     @pl.when(block >= first_block)
     def _():
-        bias[...] = visible_bias((rows, rows), 0, block * rows, start_ref[...], me * rows)
-
-        @pl.loop(0, HEADS)
+        bias[...] = visible_bias((rows, rows), block * rows, start_ref[...], me * rows)
+
+        @pl.loop(0, HEADS, unroll=2)
         def _(h):
-            at = heads_at(h)
-            late = pl.ds(pl.multiple_of(width + h * HEAD, HEAD), HEAD)
-            keys, values = kv_ref[0, :, at], kv_ref[0, :, late]
+            early, late, at = lanes(2 * h * HEAD), lanes((2 * h + 1) * HEAD), lanes(h * HEAD)
+            keys, values = kv_ref[0, :, early], kv_ref[0, :, late]
             queries, grads = q_ref[:, at], g_ref[:, at]
             probs = jnp.exp(inner_right(keys, queries) + bias[...] - total_ref[h])
             prob_grad = inner_right(values, grads)
-            score_grad = (probs * (prob_grad - term_ref[h])).astype(jnp.bfloat16)
+            score_grad = (probs * (prob_grad - term[h])).astype(jnp.bfloat16)
             dkv_ref[0, :, late] = jnp.dot(
                 probs.astype(jnp.bfloat16), grads, preferred_element_type=jnp.float32
             ).astype(jnp.bfloat16)
-            dkv_ref[0, :, at] = jnp.dot(
+            dkv_ref[0, :, early] = jnp.dot(
                 score_grad, queries, preferred_element_type=jnp.float32
             ).astype(jnp.bfloat16)
             acc[h] += inner_left(keys, score_grad)
@@ -651,45 +666,176 @@
     @pl.when(step == pl.num_programs(0) - 1)
     def _():
         for h in range(HEADS):
-            dq_ref[:, h * HEAD : (h + 1) * HEAD] = acc[h].T
-
-
-def attend_back(info, queries, grads, start, total, term, pairs):
+            back = turned(acc[h].T * HEAD ** (-0.5), cos_ref[...], -sin_ref[...])
+            dq_ref[:, h * HEAD : (h + 1) * HEAD] = back.astype(jnp.bfloat16)
+
+
+def attend_back(info, queries, grads, mixed, start, total, cosine, sine, pairs):
     rows, width = queries.shape
     count = pairs.shape[0]
     steps = count // 2 + 1
-    whole = lambda *shape: pl.BlockSpec(shape, lambda s, info: (0,) * len(shape))
     return pl.pallas_call(
         attend_back_kernel,
         out_shape=(
             jax.ShapeDtypeStruct(pairs.shape, jnp.bfloat16),
-            jax.ShapeDtypeStruct((rows, width), jnp.float32),
+            jax.ShapeDtypeStruct((rows, width), jnp.bfloat16),
         ),
         grid_spec=pltpu.PrefetchScalarGridSpec(
             num_scalar_prefetch=1,
             grid=(steps,),
             in_specs=[
-                whole(rows, width),
-                whole(rows, width),
-                whole(1, rows),
-                whole(HEADS, 1, rows),
-                whole(HEADS, 1, rows),
+                whole_spec(rows, width),
+                whole_spec(rows, width),
+                whole_spec(HEADS, HEAD, rows),
+                whole_spec(1, rows),
+                whole_spec(HEADS, 1, rows),
+                whole_spec(rows, HEAD),
+                whole_spec(rows, HEAD),
                 pl.BlockSpec((1, rows, 2 * width), lambda s, info: (jnp.maximum(info[0] - s, info[1]), 0, 0)),
             ],
             out_specs=(
                 pl.BlockSpec((1, rows, 2 * width), lambda s, info: (jnp.maximum(info[0] - s, 0), 0, 0)),
-                whole(rows, width),
+                whole_spec(rows, width),
             ),
             scratch_shapes=[
                 pltpu.VMEM((rows, rows), jnp.float32),
                 pltpu.VMEM((HEADS, HEAD, rows), jnp.float32),
+                pltpu.VMEM((HEADS, 1, rows), jnp.float32),
             ],
         ),
         cost_estimate=pl.CostEstimate(
             flops=10 * rows * rows * width * steps, bytes_accessed=8 * rows * width * steps, transcendentals=0
         ),
         name="attend_back",
-    )(info, queries, grads, start, total, term, pairs)
+    )(info, queries, grads, mixed, start, total, cosine, sine, pairs)
+
+
+def finish_kernel(
+    x_ref, gain_ref, res_ref, hid_ref, q_ref, kv_ref, cos_ref, sin_ref, wq_ref, wk_ref, wv_ref,
+    dw_ref, out_ref, gain_out, acc,
+):
+    step = pl.program_id(0)
+
+    @pl.when(step == 0)
+    def _():
+        acc[...] = jnp.zeros_like(acc)
+
+    cosine, sine = cos_ref[...], sin_ref[...]
+    count = q_ref.shape[1] // HEAD
+    keys = jnp.concatenate(
+        [turned(kv_ref[:, 2 * h * HEAD : (2 * h + 1) * HEAD].astype(jnp.float32), cosine, -sine).astype(jnp.bfloat16)
+         for h in range(count)], axis=1)
+    values = jnp.concatenate([kv_ref[:, (2 * h + 1) * HEAD : (2 * h + 2) * HEAD] for h in range(count)], axis=1)
+    grads = (q_ref[...], keys, values)
+    acc[...] += (
+        inner_right(grads[0], wq_ref[...]) + inner_right(grads[1], wk_ref[...]) + inner_right(grads[2], wv_ref[...])
+    )
+    hidden = hid_ref[...]
+    for i in range(3):
+        dw_ref[i] = inner_left(hidden, grads[i]).astype(jnp.bfloat16)
+
+    @pl.when(step == pl.num_programs(0) - 1)
+    def _():
+        values, gain, grad = x_ref[...].astype(jnp.float32), gain_ref[...], acc[...]
+        scale = lax.rsqrt(jnp.mean(values * values, axis=1, keepdims=True) + epsilon)
+        inner = jnp.mean(gain * grad * values, axis=1, keepdims=True)
+        part = scale * gain * grad - values * (scale * scale * scale) * inner
+        out_ref[...] = (res_ref[...] + part).astype(jnp.bfloat16)
+        gain_out[...] = jnp.sum(grad * values * scale, axis=0, keepdims=True)
+
+
+def finish(tokens, gain, residual_grad, hidden, query_grad, pair_grads, cosine, sine, wq, wk, wv):
+    rows, width = tokens.shape
+    tile = 2 * HEAD
+    column = pl.BlockSpec((width, tile), lambda i: (0, i))
+    return pl.pallas_call(
+        finish_kernel,
+        out_shape=(
+            jax.ShapeDtypeStruct((3, width, width), jnp.bfloat16),
+            jax.ShapeDtypeStruct((rows, width), jnp.bfloat16),
+            jax.ShapeDtypeStruct((1, width), jnp.float32),
+        ),
+        grid=(width // tile,),
+        in_specs=[whole_spec(rows, width), whole_spec(1, width), whole_spec(rows, width), whole_spec(rows, width),
+                  pl.BlockSpec((rows, tile), lambda i: (0, i)), pl.BlockSpec((rows, 2 * tile), lambda i: (0, i)),
+                  whole_spec(rows, HEAD), whole_spec(rows, HEAD), column, column, column],
+        out_specs=(pl.BlockSpec((3, width, tile), lambda i: (0, 0, i)), whole_spec(rows, width), whole_spec(1, width)),
+        scratch_shapes=[pltpu.VMEM((rows, width), jnp.float32)],
+        cost_estimate=pl.CostEstimate(flops=12 * rows * width * width, bytes_accessed=12 * width * width, transcendentals=0),
+        name="finish",
+    )(tokens, gain[None, :], residual_grad, hidden, query_grad, pair_grads, cosine, sine, wq, wk, wv)
+
+
+def experts_kernel(
+    where_ref, x_ref, g_ref, rank_row, rank_col, share_row, wg_ref, wu_ref, wd_ref,
+    back_ref, routed_ref, in_ref, pre_ref, lift_ref, mid_ref, og_ref, grads,
+):
+    blocks, rows, side = x_ref.shape
+    capacity = in_ref.shape[0] // blocks
+    width = og_ref.shape[1]
+    dot = lambda left, right: jnp.dot(left, right, preferred_element_type=jnp.float32)
+    shares = []
+    for i in range(blocks):
+        at = slice(i * capacity, (i + 1) * capacity)
+        hit = rank_row[i] == lax.broadcasted_iota(jnp.int32, (capacity, rows), 0)
+        pick = jnp.where(hit, 1.0, 0.0)
+        shares.append(jnp.sum(pick * share_row[i], axis=1, keepdims=True))
+        pick = pick.astype(jnp.bfloat16)
+        in_ref[at, :] = dot(pick, x_ref[i, :, :width]).astype(jnp.bfloat16)
+        grads[at, :] = dot(pick, g_ref[i]).astype(jnp.bfloat16)
+    share = jnp.concatenate(shares, axis=0)
+    pre = dot(in_ref[...], wg_ref[0])
+    lift = dot(in_ref[...], wu_ref[0])
+    silu, slope = silu_parts(pre)
+    mid_ref[...] = (silu * lift).astype(jnp.bfloat16)
+    lift_slope = lift * slope
+    result = dot(mid_ref[...], wd_ref[0]).astype(jnp.bfloat16).astype(jnp.float32)
+    grad = grads[...].astype(jnp.float32)
+    gate_grad = jnp.sum(result * grad, axis=1, keepdims=True)
+    og_ref[...] = (share * grad).astype(jnp.bfloat16)
+    given = (share * result).astype(jnp.bfloat16)
+    mid_grad = inner_right(og_ref[...], wd_ref[0])
+    pre_ref[...] = (mid_grad * lift_slope).astype(jnp.bfloat16)
+    lift_ref[...] = (mid_grad * silu).astype(jnp.bfloat16)
+    in_grad = (inner_right(pre_ref[...], wg_ref[0]) + inner_right(lift_ref[...], wu_ref[0])).astype(jnp.bfloat16)
+    lane = lax.broadcasted_iota(jnp.int32, (blocks * capacity, side - width), 1)
+    high = gate_grad.astype(jnp.bfloat16).astype(jnp.float32)
+    extra = jnp.where(lane == where_ref[0], high, jnp.where(lane == where_ref[1], gate_grad - high, 0.0))
+    extra = extra.astype(jnp.bfloat16)
+    for i in range(blocks):
+        at = slice(i * capacity, (i + 1) * capacity)
+        hit = rank_col[i] == lax.broadcasted_iota(jnp.int32, (rows, capacity), 1)
+        put = jnp.where(hit, 1.0, 0.0).astype(jnp.bfloat16)
+        back_ref[i, :, :width] = dot(put, in_grad[at, :]).astype(jnp.bfloat16)
+        back_ref[i, :, width:] = dot(put, extra[at, :]).astype(jnp.bfloat16)
+        routed_ref[i] = dot(put, given[at, :]).astype(jnp.bfloat16)
+
+
+def run_experts(places, arrived, grads, rank, share, gate, up, down, capacity):
+    count, rows, side = arrived.shape
+    width, ff = gate.shape[1], gate.shape[2]
+    blocks = 384 // capacity
+    flat = count * capacity
+    once = lambda *shape: pl.BlockSpec(shape, lambda i, p: (0,) * len(shape), pipeline_mode=pl.Buffered(1))
+    lead = lambda *shape: pl.BlockSpec((blocks,) + shape, lambda i, p: (i, 0, 0))
+    tall = lambda wide: pl.BlockSpec((blocks * capacity, wide), lambda i, p: (i, 0))
+    shape = lambda *dims: jax.ShapeDtypeStruct(dims, jnp.bfloat16)
+    return pl.pallas_call(
+        experts_kernel,
+        out_shape=(shape(count, rows, side), shape(count, rows, width), shape(flat, width), shape(flat, ff),
+                   shape(flat, ff), shape(flat, ff), shape(flat, width)),
+        grid_spec=pltpu.PrefetchScalarGridSpec(
+            num_scalar_prefetch=1,
+            grid=(count // blocks,),
+            in_specs=[lead(rows, side), lead(rows, width), lead(1, rows), lead(rows, 1), lead(1, rows),
+                      once(1, width, ff), once(1, width, ff), once(1, ff, width)],
+            out_specs=(lead(rows, side), lead(rows, width), tall(width), tall(ff), tall(ff), tall(ff), tall(width)),
+            scratch_shapes=[pltpu.VMEM((blocks * capacity, width), jnp.bfloat16)],
+        ),
+        compiler_params=pltpu.CompilerParams(vmem_limit_bytes=VMEM_MOST),
+        cost_estimate=pl.CostEstimate(flops=16 * flat * width * ff, bytes_accessed=16 * flat * width, transcendentals=0),
+        name="run_experts",
+    )(places, arrived, grads, rank[:, None, :], rank[:, :, None], share[:, None, :], gate, up, down)
 
 
 def local(
@@ -717,29 +863,32 @@
     ep_index = lax.axis_index("ep")
     expert_count = router_weight.shape[1]
     capacity = min(rows, 12 * rows * TOP // (7 * expert_count))
-    q_scale = HEAD ** (-0.5)
     low = lambda v: v.astype(jnp.bfloat16)
     wide = lambda v: v.astype(jnp.float32)
     dot = lambda left, right: jnp.dot(left, right, preferred_element_type=jnp.float32)
 
     grad_low = out_grad[0]
-    grads_all = lax.all_gather(grad_low, "ep", axis=0, tiled=False)
 
     doc_ends = jnp.cumsum(doc_lengths[0])
     query_pos = ep_index * rows + jnp.arange(rows, dtype=jnp.int32)
     before = query_pos[:, None] >= doc_ends[None, :]
     start = jnp.max(jnp.where(before, doc_ends[None, :], 0), axis=1)
     info = jnp.stack([ep_index, start[0] // rows]).astype(jnp.int32)
-    position = wide(query_pos)
+    half_dim = HEAD // 2
+    frequency = rope_base ** (-jnp.arange(half_dim, dtype=jnp.float32) / half_dim)
+    angles = wide(query_pos)[:, None] * frequency[None, :]
+    cosine, sine = jnp.cos(angles), jnp.sin(angles)
+    cosine = jnp.concatenate([cosine, cosine], axis=1)
+    sine = jnp.concatenate([-sine, sine], axis=1)
 
     stream = wide(tokens[0])
-    hidden_low = low(normed(stream, mixer_gain))
-    heads = lambda v: v.reshape(rows, HEADS, HEAD)
-    queries = low(rotary(heads(dot(hidden_low, query_weight)), position, 1.0) * q_scale).reshape(rows, width)
-    keys = low(rotary(heads(dot(hidden_low, key_weight)), position, 1.0)).reshape(rows, width)
-    values = low(dot(hidden_low, value_weight))
-    pairs = gather_rows(jnp.concatenate([keys, values], axis=1), True, 1)
-    mixed, mixed_low, log_total = attend(info, queries, start[:, None], pairs)
+    hidden_low, queries, own_pairs = project(
+        tokens[0], mixer_gain, cosine, sine, query_weight, key_weight, value_weight
+    )
+    pairs = gather_rows(own_pairs, True, 1, 8)
+    grad_later, pairs = lax.optimization_barrier((grad_low, pairs))
+    grads_all = lax.all_gather(grad_later, "ep", axis=0, tiled=False)
+    mixed, mixed_low, log_total = attend(info, queries, start[None, :], pairs)
     mixer_out = dot(mixed_low, output_weight)
     residual = stream + mixer_out
     ffn_low = low(normed(residual, ffn_gain))
@@ -764,46 +913,24 @@
     chosen = share > 0.0
     earlier = (jnp.arange(rows)[:, None] < jnp.arange(rows)[None, :]).astype(jnp.bfloat16)
     rank = dot(low(chosen), earlier).astype(jnp.int32)
-    pick = (rank[:, None, :] == jnp.arange(capacity, dtype=jnp.int32)[None, :, None]) & chosen[:, None, :]
-    pick_low = low(pick)
-    take = lambda block: low(
-        jnp.einsum("srt,std->srd", pick_low, block, preferred_element_type=jnp.float32)
-    ).reshape(ep_count * capacity, -1)
-    put = lambda flat: low(
-        jnp.einsum(
-            "srt,srd->std", pick_low, flat.reshape(ep_count, capacity, -1), preferred_element_type=jnp.float32
-        )
-    )
-    flat_in = take(arrived[:, :, :width])
-    flat_out_grad = take(grads_all)
-    flat_share = jnp.sum(jnp.where(pick, share[:, None, :], 0.0), axis=2).reshape(-1, 1)
-    gate_pre = dot(flat_in, expert_gate[0])
-    up_pre = dot(flat_in, expert_up[0])
-    expert_silu, expert_slope = silu_parts(gate_pre)
-    middle = low(expert_silu * up_pre)
-    result = low(dot(middle, expert_down[0]))
-    gate_grad = jnp.sum(wide(result) * wide(flat_out_grad), axis=1, keepdims=True)
-    result_grad = low(flat_share * wide(flat_out_grad))
-    mid_grad = inner_right(result_grad, expert_down[0])
-    pre_grad = low(mid_grad * up_pre * expert_slope)
-    lift_grad = low(mid_grad * expert_silu)
-    input_grad = low(inner_right(pre_grad, expert_gate[0]) + inner_right(lift_grad, expert_up[0]))
-    gate_high = low(gate_grad)
-    gate_rest = low(gate_grad - wide(gate_high))
-    mine = low(experts[None, :] == ep_index)
-    back = jnp.concatenate(
-        [input_grad, gate_high * mine, gate_rest * mine,
-         jnp.zeros((flat_in.shape[0], side - width - 2 * expert_count), jnp.bfloat16)], axis=1
-    )
-    back_sum = scatter_rows(put(back), False, 3)
-    routed = wide(lax.psum_scatter(put(low(flat_share * wide(result))), "ep", scatter_dimension=0))
-    half = lambda v: v.reshape(v.shape[0], lax.axis_size("grp"), -1)
-    own_down_grad = low(jnp.einsum("rf,rgd->gfd", middle, half(result_grad), preferred_element_type=jnp.float32))
+    rank = jnp.where(chosen, rank, -1)
+    places = jnp.stack([ep_index, expert_count + ep_index]).astype(jnp.int32)
+    back, given, flat_in, pre_grad, lift_grad, middle, result_grad = run_experts(
+        places, arrived, grads_all, rank, share, expert_gate, expert_up, expert_down, capacity
+    )
+    back_sum = scatter_rows(back, False, 3, 2)
+    given, back_sum = lax.optimization_barrier((given, back_sum))
+    routed = wide(lax.psum_scatter(given, "ep", scatter_dimension=0))
+    group_count = lax.axis_size("grp")
+    split = width // group_count
+    own_down_grad = jnp.concatenate(
+        [low(inner_left(middle, result_grad[:, i * split : (i + 1) * split])) for i in range(group_count)], axis=0
+    )
     own_gate_grad = low(inner_left(flat_in, pre_grad))
     own_up_grad = low(inner_left(flat_in, lift_grad))
-    over_groups = lambda v: wide(lax.psum_scatter(v, "grp", scatter_dimension=0, tiled=True))
-    gate_sum = over_groups(own_gate_grad)[None]
-    up_sum = over_groups(own_up_grad)[None]
+    over_groups = lambda v: wide(lax.psum_scatter(v, "grp", scatter_dimension=0, tiled=True))[None]
+    gate_sum = over_groups(own_gate_grad)
+    up_sum = over_groups(own_up_grad)
     down_sum = over_groups(own_down_grad)
 
     shared_pre = dot(ffn_low, shared_gate)
@@ -829,12 +956,10 @@
     residual_grad = grad_out + residual_part
     mixer_grad_low = low(residual_grad)
     mixed_grad = low(inner_right(mixer_grad_low, output_weight))
-    row_term = jnp.sum(heads(wide(mixed_grad) * mixed), axis=2)
-    pair_parts, query_sum = attend_back(
-        info, queries, mixed_grad, start[None, :], log_total.reshape(HEADS, 1, rows),
-        row_term.T.reshape(HEADS, 1, rows), pairs,
-    )
-    pair_grads = scatter_rows(pair_parts, True, 4)
+    pair_parts, query_lin_grad = attend_back(
+        info, queries, mixed_grad, mixed, start[None, :], log_total, cosine, sine, pairs
+    )
+    pair_grads = scatter_rows(pair_parts, True, 4, 2)
 
     by_device = lambda v: low(v).reshape(device_count, width // device_count, -1)
     early = jnp.concatenate(
@@ -843,29 +968,20 @@
     )
     early_sum = scatter_whole(early, 5)
 
-    query_lin_grad = low(rotary(heads(query_sum * q_scale), position, -1.0)).reshape(rows, width)
-    key_lin_grad = low(rotary(heads(wide(pair_grads[:, :width])), position, -1.0)).reshape(rows, width)
-    value_lin_grad = pair_grads[:, width:]
-    hidden_grad = (
-        inner_right(query_lin_grad, query_weight)
-        + inner_right(key_lin_grad, key_weight)
-        + inner_right(value_lin_grad, value_weight)
-    )
-    _, mixer_pull = jax.vjp(normed, stream, mixer_gain)
-    stream_part, mixer_gain_grad = mixer_pull(hidden_grad)
-    tokens_grad = low(residual_grad + stream_part)
-
+    weight_grads, tokens_grad, mixer_gain_grad = finish(
+        tokens[0], mixer_gain, residual_grad, hidden_low, query_lin_grad, pair_grads, cosine, sine,
+        query_weight, key_weight, value_weight,
+    )
     squares = jnp.stack(
         [jnp.sum(residual * residual), jnp.sum(mixer_out * mixer_out), jnp.sum(layer_out * layer_out)]
     )
     extras = jnp.concatenate(
-        [inner_left(ffn_low, logit_grad), mixer_gain_grad[:, None], ffn_gain_grad[:, None],
+        [inner_left(ffn_low, logit_grad), mixer_gain_grad.T, ffn_gain_grad[:, None],
          jnp.broadcast_to(squares[None, :], (width, 3))], axis=1
     )
     extras = jnp.pad(extras, ((0, 0), (0, HEAD - extras.shape[1])))
     late = jnp.concatenate(
-        [by_device(inner_left(hidden_low, query_lin_grad)), by_device(inner_left(hidden_low, key_lin_grad)),
-         by_device(inner_left(hidden_low, value_lin_grad)), by_device(extras)], axis=2
+        [by_device(weight_grads[0]), by_device(weight_grads[1]), by_device(weight_grads[2]), by_device(extras)], axis=2
     )
     late_sum = scatter_whole(late, 6)
     extra_sum = late_sum[:, 3 * width :]

time: 1090 us -> 865 us (0.79)
  matrix products: 223 us -> 66.7 us
  local copies, waits for them, and re-layouts: 104 us -> 34.7 us
  other arithmetic: 50.5 us -> 36 us
    pallas_call x1 -> x4, Pallas kernels: 11.1 us -> 105 us  [the longest x1 73.9 us: run_experts(): pl.pallas_call(experts_kernel, out_shape=(shape(count, rows, side), shape...]
    dot_general x11 -> x5, matrix products: 67.5 us -> 9.29 us  [inner_right(): lax.dot_general(left_op, right_op, (((1,), (1,)), ((), ())), preferred_el...]
    dot_general x5 -> x0, matrix products: 52.7 us -> none  [the longest x2 23.2 us: local(): jnp.einsum('srt,std->srd', pick_low, block, preferred_element_type=jnp.fl...]
    pallas_call x2, Pallas kernels: 216 us -> 165 us  [scatter_rows(): pl.pallas_call(functools.partial(scatter_kernel, plan, pieces), out_shape...]
    dot_general x12 -> x6, matrix products: 59.7 us -> 10.2 us  [local(): jnp.dot(left, right, preferred_element_type=jnp.float32)]
    convert_element_type x2 -> x0, local copies, waits for them, and re-layouts: 43.4 us -> none  [local(): wide = lambda v: v.astype(jnp.float32)]
    pallas_call x2, Pallas kernels: 212 us -> 181 us  [gather_rows(): pl.pallas_call(functools.partial(gather_kernel, plan, pieces), out_shape=...]
    unnamed x142 -> x71, local copies, waits for them, and re-layouts: 27.8 us -> 9.8 us
  transfers between devices with their start and end apart: 5 -> 5, of which waited for: 0 -> 0; matrix products, arithmetic and copies ran while one was open for 23% -> 10% of each run, Pallas kernels for 56% -> 54%
where the time goes in v2:
time: 865 us; the launch traced here: 858 us
  Pallas kernels  703 us (81%)
  matrix products  66.7 us (8%)
  other arithmetic  36 us (4%)
  local copies, waits for them, and re-layouts  34.7 us (4%)
  between operations  17.1 us (2%)
    pallas_call x2, Pallas kernels, scatter_whole(): pl.pallas_call(kernel, out_shape=jax.ShapeDtypeStruct((rows, width), jnp....  243 us
    pallas_call x2, Pallas kernels, gather_rows(): pl.pallas_call(functools.partial(gather_kernel, plan, pieces), out_shape=...  181 us
    pallas_call x2, Pallas kernels, scatter_rows(): pl.pallas_call(functools.partial(scatter_kernel, plan, pieces), out_shape...  165 us
    pallas_call x1, Pallas kernels, run_experts(): pl.pallas_call(experts_kernel, out_shape=(shape(count, rows, side), shape...  73.9 us
    dot_general x9, matrix products, inner_left(): lax.dot_general(left_op, right_op, (((0,), (0,)), ((), ())), preferred_el...  47.2 us
  transfers between devices with their start and end apart: 5, of which 0 were waited for; matrix products, arithmetic and copies ran while one was open for 10% of the time, Pallas kernels for 54%

profile of v2, /device:TPU:0, one launch (start us, length us, event | category | flops | bytes accessed | tf_op | source)
XLA Modules:
  0.0 858.0 jit_solution(17028475567069566744)
XLA Ops:
  8.6 1.3 broadcast_in_dim.107.gain_ref
  10.6 8.7 %project.1 = (bf16[256,1280]{1,0:T(8,128)(2,1)}, bf16[256,1280]{1,0:T(8,128)(2,1)}, bf16[256,2560]{1,0:T(8,128)(2,1)}) custom-call(bf16[256,1280]{1,0:T(8,128)(2,1)} %bitcast.99, f32[1,1280]{1,0:T(1,128)} %broadcast_in_dim.107.gain_ref, f32[256,128]{1,0:T(8,128)} %pad_maximum_fusion.3.cos_ref, f32[256,128]{1,0:T(8,128)} %pad_maximum_fusion.4.sin_ref, ...), custom_call_target="tpu_custom_call" | custom-call | flops 2516582400 | bytes 9830400 | tf_op jit(solution)/shard_map/project/pallas_call | solution.py:540
  19.3 34.8 %gather_rows.2.kv_ref = bf16[16,256,2560]{2,1,0:T(8,128)(2,1)} custom-call(bf16[256,2560]{1,0:T(8,128)(2,1)} %get-tuple-element.39.x_ref), custom_call_target="tpu_custom_call" | custom-call | tf_op jit(solution)/shard_map/gather_rows/pallas_call | solution.py:227
  58.3 7.9 attend.1
  66.2 3.9 multiply_reduce_fusion.5
  70.1 1.0 copy-done.2
  72.8 1.0 concatenate.24.x_ref
  73.8 146.6 %gather_rows.3.x_ref = bf16[16,256,1408]{2,1,0:T(8,128)(2,1)} custom-call(bf16[256,1408]{1,0:T(8,128)(2,1)} %concatenate.24.x_ref), custom_call_target="tpu_custom_call" | custom-call | tf_op jit(solution)/shard_map/gather_rows/pallas_call | solution.py:227
  220.5 2.6 select_reduce_fusion
  223.8 2.0 copy.60.rank_col
  227.0 73.9 %run_experts.1 = (bf16[16,256,1408]{2,1,0:T(8,128)(2,1)}, bf16[16,256,1280]{2,1,0:T(8,128)(2,1)}, bf16[3072,1280]{1,0:T(8,128)(2,1)}, bf16[3072,896]{1,0:T(8,128...) custom-call(s32[2]{0:T(128)} %pad_add_fusion.1.where_ref, ...), custom_call_target="tpu_custom_call" | custom-call | flops 56371445760 | bytes 62914560 | tf_op jit(solution)/shard_map/run_experts/pallas_call | solution.py:823
  300.9 8.4 fusion.10
  309.3 4.5 fusion.7
  313.8 1.5 pad_maximum_fusion.2
  315.4 13.3 %convolution_convert_fusion.1 = bf16[1280,896]{1,0:T(8,128)(2,1)} fusion(bf16[3072,1280]{1,0:T(8,128)(2,1)} %get-tuple-element.55, bf16[3072,896]{1,0:T(8,128)(2,1)} %get-tuple-element.57), kind=kOutput, calls=%fused_computation.7 | convolution fusion | flops 7047577600 | bytes 15663104 | tf_op jit(solution)/shard_map/dot_general | solution.py:26
  328.8 13.5 %convolution_convert_fusion.2 = bf16[1280,896]{1,0:T(8,128)(2,1)} fusion(bf16[3072,1280]{1,0:T(8,128)(2,1)} %get-tuple-element.55, bf16[3072,896]{1,0:T(8,128)(2,1)} %get-tuple-element.56), kind=kOutput, calls=%fused_computation.8 | convolution fusion | flops 7047577600 | bytes 15663104 | tf_op jit(solution)/shard_map/dot_general | solution.py:26
  342.4 88.6 %scatter_rows.2 = bf16[256,1408]{1,0:T(8,128)(2,1)} custom-call(bf16[16,256,1408]{2,1,0:T(8,128)(2,1)} %get-tuple-element.44.p_ref), custom_call_target="tpu_custom_call" | custom-call | tf_op jit(solution)/shard_map/scatter_rows/pallas_call | solution.py:374
  431.1 1.0 copy-done.1
  436.5 1.9 multiply_convert_fusion.1
  439.2 2.2 fusion.4
  441.4 3.2 copy.62
  444.6 1.9 convolution_convert_fusion.5
  446.5 0.9 convolution_convert_fusion.4
  448.2 0.9 fusion.36
  449.5 1.0 copy-done.12
  450.6 0.9 fusion.5
  451.9 1.3 multiply_reduce_fusion.2
  454.4 1.1 convolution_convert_fusion
  455.5 4.7 pad_maximum_fusion.1.p_ref
  460.2 124.2 %scatter_whole.3 = f32[40,3968]{1,0:T(8,128)} custom-call(bf16[32,40,3968]{2,1,0:T(8,128)(2,1)} %pad_maximum_fusion.1.p_ref), custom_call_target="tpu_custom_call" | custom-call | tf_op jit(solution)/shard_map/scatter_whole/pallas_call | solution.py:485
  584.3 1.6 slice.84
  586.0 4.3 convolution_convert_fusion.6.g_ref
  590.3 9.4 %attend_back.1 = (bf16[16,256,2560]{2,1,0:T(8,128)(2,1)}, bf16[256,1280]{1,0:T(8,128)(2,1)}) custom-call(s32[2]{0:T(128)} %pad_add_fusion.info, bf16[256,1280]{1,0:T(8,128)(2,1)} %get-tuple-element.38.q_ref, bf16[256,1280]{1,0:T(8,128)(2,1)} %convolution_convert_fusion.6.g_ref, f32[10,128,256]{2,1,0:T(8,128)} %get-tuple-element.48.mixed_ref, ...), custom_call_target="tpu_custom_call" | custom-call | flops 7549747200 | bytes 23592960 | tf_op jit(solution)/shard_map/attend_back/pallas_call | solution.py:677
  599.7 76.1 %scatter_rows.3.kv_ref = bf16[256,2560]{1,0:T(8,128)(2,1)} custom-call(bf16[16,256,2560]{2,1,0:T(8,128)(2,1)} %get-tuple-element.51.p_ref), custom_call_target="tpu_custom_call" | custom-call | tf_op jit(solution)/shard_map/scatter_rows/pallas_call | solution.py:374
  676.4 1.8 slice_bitcast_fusion
  678.3 1.5 convolution_convert_fusion.7
  679.8 14.4 %finish.1 = (bf16[3,1280,1280]{2,1,0:T(8,128)(2,1)}, bf16[256,1280]{1,0:T(8,128)(2,1)}, f32[1,1280]{1,0:T(1,128)}) custom-call(bf16[256,1280]{1,0:T(8,128)(2,1)} %bitcast.100, f32[1,1280]{1,0:T(1,128)} %broadcast_in_dim.107.gain_ref, f32[256,1280]{1,0:T(8,128)} %copy-done.7, bf16[256,1280]{1,0:T(8,128)(2,1)} %get-tuple-element.47.hid_ref, ...), custom_call_target="tpu_custom_call" | custom-call | flops 5033164800 | bytes 19660800 | tf_op jit(solution)/shard_map/finish/pallas_call | solution.py:751
  694.9 7.1 fusion.31
  702.0 2.8 bitcast_convert_fusion
  704.8 2.8 bitcast_convert_fusion.1
  707.6 2.9 bitcast_convert_fusion.2
  710.5 4.1 multiply_reduce_fusion
  714.6 2.0 maximum_convert_fusion
  717.1 9.4 %pad_maximum_fusion.p_ref = bf16[32,40,3968]{2,1,0:T(8,128)(2,1)} fusion(bf16[32,40,128]{2,1,0:T(8,128)(2,1)S(1)} %bitcast.98, bf16[32,40,1280]{2,1,0:T(8,128)(2,1)} %bitcast.92, bf16[32,40,1280]{2,1,0:T(8,128)(2,1)} %bitcast.93, bf16[32,40,1280]{2,1,0:T(8,128)(2,1)} %bitcast.91), kind=kLoop, calls=%fused_computation | loop fusion | flops 40632320 | bytes 20316160 | tf_op jit(solution)/shard_map/concatenate | solution.py:983
  726.5 118.7 %scatter_whole.2 = f32[40,3968]{1,0:T(8,128)} custom-call(bf16[32,40,3968]{2,1,0:T(8,128)(2,1)} %pad_maximum_fusion.p_ref), custom_call_target="tpu_custom_call" | custom-call | tf_op jit(solution)/shard_map/scatter_whole/pallas_call | solution.py:485
  845.1 2.0 fusion.32
  847.8 1.5 slice_reduce_fusion
  849.3 1.3 sqrt_bitcast_fusion
  (116 shorter events, 18.7 us)
Async XLA Ops:
  7.2 219.8 %all-gather.3.cloned.1.call-start = ((), (), s32[]{:S(2)}) async-start(), calls=%async_computation.8 | async-start | bytes 11141120 | tf_op jit(solution)/shard_map/all_gather | solution.py:890
  19.3 34.9 %copy-start.31 = (s32[1,4]{1,0:T(1,128)S(1)}, s32[1,4]{1,0:T(1,128)}, u32[]{:S(2)}) copy-start(s32[1,4]{1,0:T(1,128)} %param.18) | copy-start | bytes 52
  19.3 38.3 %copy-start.27 = (s32[1,256,7]{1,0,2:T(1,128)S(1)}, s32[1,256,7]{1,0,2:T(1,128)}, u32[]{:S(2)}) copy-start(s32[1,256,7]{1,0,2:T(1,128)} %param.19) | copy-start | bytes 21508
  54.1 647.9 %reduce-scatter.11.cloned.1.call-start = ((), (), s32[]{:S(2)}) async-start(), calls=%async_computation.7 | async-start | bytes 3440640 | tf_op jit(solution)/shard_map/reduce_scatter | solution.py:931
  54.4 3.9 copy-start.28
  58.3 7.9 copy-start.19
  66.2 5.0 copy-start.22
  66.2 5.1 copy-start.20
  70.1 1.0 copy-start.2
  70.1 2.6 copy-start.29
  70.1 2.6 copy-start.24
  71.4 149.1 %copy-start = (bf16[256,1280]{1,0:T(8,128)(2,1)}, bf16[256,1280]{1,0:T(8,128)(2,1)S(1)}, u32[]{:S(2)}) copy-start(bf16[256,1280]{1,0:T(8,128)(2,1)S(1)} %multiply_convert_fusion) | copy-start | bytes 1966084
  300.9 8.4 copy-start.32
  300.9 8.4 copy-start.33
  315.4 389.4 %reduce-scatter.9.cloned.1.call-start = ((), (), s32[]{:S(2)}) async-start(), calls=%async_computation.6 | async-start | bytes 3440640 | tf_op jit(solution)/shard_map/reduce_scatter | solution.py:931
  328.8 378.8 %reduce-scatter.7.cloned.1.call-start = ((), (), s32[]{:S(2)}) async-start(), calls=%async_computation.5 | async-start | bytes 3440640 | tf_op jit(solution)/shard_map/reduce_scatter | solution.py:931
  342.3 368.2 %reduce-scatter.5.cloned.1.call-start = ((), (), s32[]{:S(2)}) async-start(), calls=%async_computation.4 | async-start | bytes 11141120 | tf_op jit(solution)/shard_map/reduce_scatter | solution.py:923
  431.0 1.1 copy-start.1
  431.1 1.9 copy-start.9
  433.0 1.6 copy-start.11
  434.6 1.1 copy-start.5
  434.6 1.9 copy-start.13
  438.4 0.8 copy-start.16
  446.5 1.6 copy-start.10
  446.5 1.7 copy-start.18
  448.2 1.1 copy-start.8
  448.2 1.1 copy-start.15
  448.2 2.3 copy-start.12
  450.5 0.9 copy-start.26
  450.5 1.4 copy-start.3
  450.5 1.4 copy-start.21
  450.5 1.4 copy-start.23
  450.5 1.4 copy-start.25
  451.9 1.3 copy-start.30
  451.9 1.3 copy-start.6
  453.2 1.2 copy-start.14
  454.4 1.1 copy-start.7
  707.6 2.9 copy-start.4
  707.6 2.9 copy-start.17
Sparse Core Ops, SparseCore 0:
  54.2 160.9 all-gather.2
  315.5 49.1 reduce-scatter.10
  367.7 33.9 reduce-scatter.8
  404.4 33.9 reduce-scatter.6
  442.8 144.5 reduce-scatter.4

commit v3 on v2

--- a/solution.py
+++ b/solution.py
@@ -79,6 +79,12 @@
 
     def slot(self, a, b, c):
         return (a * self.wide + b) * 2 + c
+
+    def plane(self, a, d):
+        return d if self.window else jnp.clip(a - d, 0, self.long - 1)
+
+    def planes(self):
+        return len(self.steps) if self.window else self.long
 
     def inside(self, a):
         return jnp.logical_and(a >= 0, a < self.long)
@@ -237,264 +243,443 @@
 
 
 def add_rows(dst, others, out=None):
-    rows = dst.shape[0]
-    piece = next(p for p in (32, 16, 8, rows) if rows % p == 0)
+    rows, width = dst.shape
     out = dst if out is None else out
-
-    @pl.loop(0, rows // piece)
-    def _(i):
-        at = pl.ds(pl.multiple_of(i * piece, piece), piece)
+    small = rows <= 64
+    piece = 32 if rows % 32 == 0 else rows
+    lanes = width if rows % 32 == 0 else 4 * HEAD
+    whole = width // lanes * lanes
+
+    def add(at):
         if len(others) == 1 and out.dtype == jnp.bfloat16:
-            out[at, :] = dst[at, :] + others[0][at, :]
+            out[at] = dst[at] + others[0][at]
         else:
-            total = dst[at, :].astype(jnp.float32)
+            total = dst[at].astype(jnp.float32)
             for other in others:
-                total = total + other[at, :].astype(jnp.float32)
-            out[at, :] = total.astype(out.dtype)
-
-
-def scatter_kernel(plan, pieces, p_ref, out_ref, held, rcb, rbb, r_hi, r_lo, sc, rc, sb, rb, sa, rhi, rlo, ld):
-    a, b, c = plan.place()
-    steps, wide = plan.steps, plan.wide
-    at = {d: i for i, d in enumerate(steps)}
-    rows = p_ref.shape[1] // pieces
-
-    def part(q):
-        return pl.ds(pl.multiple_of(q * rows, rows), rows)
-
-    def remote(src, dst, ssem, rsem, dev):
-        return pltpu.make_async_remote_copy(
-            src_ref=src, dst_ref=dst, send_sem=ssem, recv_sem=rsem,
-            device_id={"ep": dev}, device_id_type=MESH,
-        )
-
-    order = sorted(steps, key=lambda d: -abs(d))
-    ks = list(range(1, wide)) + [0]
-
-    def load(d, k, q):
-        i, b0 = at[d], (b + wide - k) % wide
-        return (both(plan.inside(a - d), plan.need(d, b, c, b0, c)), lambda: pltpu.make_async_copy(
-            p_ref.at[plan.slot(a - d, b0, c), part(q)], held.at[i, k, part(q)], ld.at[i, k, q]))
-
-    def cross(d, k, q):
-        i, b0 = at[d], (b + wide - k) % wide
-        real = plan.inside(a - d)
-        return (both(real, plan.need(d, b, c, b0, 1 - c)), lambda: remote(
-            p_ref.at[plan.slot(a - d, b0, 1 - c), part(q)], rcb.at[i, k, part(q)], sc.at[i, k, q],
-            rc.at[i, k, q], plan.slot(a, b, 1 - c)), both(real, plan.need(d, b, 1 - c, b0, c)))
-
-    def over(d, k, q):
-        i, b0 = at[d], (b + wide - k) % wide
-        return (both(plan.inside(a - d), plan.need_pair(d, b, b0)), lambda: remote(
-            held.at[i, k, part(q)], rbb.at[i, k - 1, part(q)], sb.at[i, k, q], rb.at[i, k, q],
-            plan.slot(a, b0, c)))
-
-    def along(d, q):
-        i, up = at[d], d < 0
-        j = at[d + 1 if up else d - 1]
-        return plan.inside(a - d), lambda: remote(
-            held.at[i, 0, part(q)], (r_lo if up else r_hi).at[j, part(q)], sa.at[i, q],
-            (rlo if up else rhi).at[j, q], plan.slot(a + (1 if up else -1), b, c))
-
-    plan.greet(a, b, c)
-    for k in ks:
-        @pl.loop(0, pieces)
-        def _(q, k=k):
-            for d in order:
-                for cond, go in (cross(d, k, q)[:2], load(d, k, q)):
-                    @when(cond)
-                    def _(go=go):
-                        go().start()
-
-    def first(d, k, q):
-        cond, go = load(d, k, q)
-        @when(cond)
-        def _():
-            go().wait()
-        _, cross_go, come = cross(d, k, q)
-        @when(come)
-        def _():
-            cross_go().wait_recv()
-            add_rows(held.at[at[d], k, part(q)], [rcb.at[at[d], k, part(q)]])
-
-    for k in ks[:-1]:
-        @pl.loop(0, pieces)
-        def _(q, k=k):
-            for d in order:
-                first(d, k, q)
-                cond, go = over(d, k, q)
-                @when(cond)
-                def _(go=go):
-                    go().start()
-    for d in order:
-        @pl.loop(0, pieces)
-        def _(q, d=d):
-            i = at[d]
-            real = plan.inside(a - d)
-            first(d, 0, q)
-            for k in range(1, wide):
-                frm = (b + k) % wide
-                @when(both(real, plan.need_pair(d, frm, b)))
-                def _(k=k):
-                    over(d, k, q)[1]().wait_recv()
-                    add_rows(held.at[i, 0, part(q)], [rbb.at[i, k - 1, part(q)]])
-            for inner, cond, buf, sem in ((d >= 0 and d + 1 in at, a + 1 < plan.long, r_hi, rhi),
-                                          (d <= 0 and d - 1 in at, a > 0, r_lo, rlo)):
-                if inner:
-                    @when(both(real, cond))
-                    def _(buf=buf, sem=sem):
-                        remote(held.at[i, 0, part(q)], buf.at[i, part(q)], sa.at[i, q], sem.at[i, q],
-                               plan.slot(a, b, c)).wait_recv()
-                        add_rows(held.at[i, 0, part(q)], [buf.at[i, part(q)]])
-            if d:
-                cond, go = along(d, q)
-                @when(cond)
-                def _():
-                    go().start()
-    out_ref[...] = held[at[0], 0]
-
-    @pl.loop(0, pieces)
-    def _(q):
-        for d in steps:
-            sends = [cross(d, k, q)[:2] for k in range(wide)] + [over(d, k, q) for k in range(1, wide)]
-            if d:
-                sends.append(along(d, q))
-            for cond, go in sends:
-                @when(cond)
-                def _(go=go):
-                    go().wait_send()
+                total = total + other[at].astype(jnp.float32)
+            out[at] = total.astype(out.dtype)
+
+    if piece == rows:
+        @pl.loop(0, whole // lanes)
+        def _(i):
+            add((slice(None), pl.ds(pl.multiple_of(i * lanes, lanes), lanes)))
+
+        if whole < width:
+            add((slice(None), pl.ds(whole, width - whole)))
+    else:
+        @pl.loop(0, rows // piece)
+        def _(i):
+            add((pl.ds(pl.multiple_of(i * piece, piece), piece), slice(None)))
+
+
+def send(src, dst, ssem, rsem, to):
+    return pltpu.make_async_remote_copy(
+        src_ref=src, dst_ref=dst, send_sem=ssem, recv_sem=rsem, device_id=to, device_id_type=MESH
+    )
+
+
+def run_if(cond, go):
+    @when(cond)
+    def _():
+        go()
+
+
+class RowSum:
+    @staticmethod
+    def scratch(plan, rows, width, dtype, pieces):
+        n, wide = plan.planes(), plan.wide
+        blocks = lambda *lead: pltpu.VMEM(lead + (rows, width), dtype)
+        sem = lambda *lead: pltpu.SemaphoreType.DMA(lead + (pieces,))
+        return [blocks(n, wide), blocks(n, wide), blocks(n, wide - 1), blocks(n), blocks(n),
+                sem(n, wide), sem(n, wide), sem(n, wide), sem(n, wide), sem(n), sem(n), sem(n), sem(n, wide)]
+
+    def __init__(self, plan, pieces, p_ref, scratch):
+        self.plan, self.pieces, self.p_ref = plan, pieces, p_ref
+        (self.held, self.rcb, self.rbb, self.r_hi, self.r_lo,
+         self.sc, self.rc, self.sb, self.rb, self.sa, self.rhi, self.rlo, self.ld) = scratch
+        self.a, self.b, self.c = plan.place()
+        self.rows = p_ref.shape[1] // pieces
+        self.order = sorted(plan.steps, key=lambda d: -abs(d))
+
+    def part(self, q):
+        return pl.ds(pl.multiple_of(q * self.rows, self.rows), self.rows)
+
+    def dev(self, a, b, c):
+        return {"ep": self.plan.slot(a, b, c)}
+
+    def source(self, k):
+        return (self.b + self.plan.wide - k) % self.plan.wide
+
+    def load(self, d, k, q):
+        p, i, b0 = self.plan, self.plan.plane(self.a, d), self.source(k)
+        return both(p.inside(self.a - d), p.need(d, self.b, self.c, b0, self.c)), lambda: pltpu.make_async_copy(
+            self.p_ref.at[p.slot(self.a - d, b0, self.c), self.part(q)], self.held.at[i, k, self.part(q)],
+            self.ld.at[i, k, q])
+
+    def cross(self, d, k, q):
+        p, i, b0, c = self.plan, self.plan.plane(self.a, d), self.source(k), self.c
+        real = p.inside(self.a - d)
+        return (both(real, p.need(d, self.b, c, b0, 1 - c)), lambda: send(
+            self.p_ref.at[p.slot(self.a - d, b0, 1 - c), self.part(q)], self.rcb.at[i, k, self.part(q)],
+            self.sc.at[i, k, q], self.rc.at[i, k, q], self.dev(self.a, self.b, 1 - c)),
+            both(real, p.need(d, self.b, 1 - c, b0, c)))
+
+    def over(self, d, k, q):
+        p, i, b0 = self.plan, self.plan.plane(self.a, d), self.source(k)
+        return both(p.inside(self.a - d), p.need_pair(d, self.b, b0)), lambda: send(
+            self.held.at[i, k, self.part(q)], self.rbb.at[i, k - 1, self.part(q)], self.sb.at[i, k, q],
+            self.rb.at[i, k, q], self.dev(self.a, b0, self.c))
+
+    def along(self, d, q):
+        p, i, up = self.plan, self.plan.plane(self.a, d), d < 0
+        j = d - 1 if p.window else i
+        return p.inside(self.a - d), lambda: send(
+            self.held.at[i, 0, self.part(q)], (self.r_lo if up else self.r_hi).at[j, self.part(q)],
+            self.sa.at[i, q], (self.rlo if up else self.rhi).at[j, q],
+            self.dev(self.a + (1 if up else -1), self.b, self.c))
+
+    def start(self, ks):
+        for k in ks:
+            @pl.loop(0, self.pieces)
+            def _(q, k=k):
+                for d in self.order:
+                    for cond, go in (self.cross(d, k, q)[:2], self.load(d, k, q)):
+                        run_if(cond, lambda go=go: go().start())
+
+    def first(self, d, k, q):
+        i = self.plan.plane(self.a, d)
+        cond, go = self.load(d, k, q)
+        run_if(cond, lambda: go().wait())
+        _, come_go, come = self.cross(d, k, q)
+
+        def take():
+            come_go().wait_recv()
+            add_rows(self.held.at[i, k, self.part(q)], [self.rcb.at[i, k, self.part(q)]])
+
+        run_if(come, take)
+
+    def stage_over(self, k):
+        @pl.loop(0, self.pieces)
+        def _(q):
+            for d in self.order:
+                self.first(d, k, q)
+                cond, go = self.over(d, k, q)
+                run_if(cond, lambda go=go: go().start())
+
+    def stage_dests(self, low, high):
+        @pl.loop(low, high)
+        def _(q):
+            for d in self.order:
+                self.dest(d, q)
+
+    def dest(self, d, q):
+        p, a, b, steps = self.plan, self.a, self.b, self.plan.steps
+        i = p.plane(a, d)
+        real = p.inside(a - d)
+        mine = self.held.at[i, 0, self.part(q)]
+        self.first(d, 0, q)
+        for k in range(1, p.wide):
+            def take(k=k):
+                self.over(d, k, q)[1]().wait_recv()
+                add_rows(mine, [self.rbb.at[i, k - 1, self.part(q)]])
+
+            run_if(both(real, p.need_pair(d, (b + k) % p.wide, b)), take)
+        for inner, cond, buf, sem in ((d >= 0 and d + 1 in steps, a + 1 < p.long, self.r_hi, self.rhi),
+                                      (d <= 0 and d - 1 in steps, a > 0, self.r_lo, self.rlo)):
+            if inner:
+                def take(buf=buf, sem=sem):
+                    send(mine, buf.at[i, self.part(q)], self.sa.at[i, q], sem.at[i, q],
+                         self.dev(a, b, self.c)).wait_recv()
+                    add_rows(mine, [buf.at[i, self.part(q)]])
+
+                run_if(both(real, cond), take)
+        if d:
+            cond, go = self.along(d, q)
+            run_if(cond, lambda: go().start())
+
+    def result(self):
+        return self.held[self.plan.plane(self.a, 0), 0]
+
+    def drain(self):
+        @pl.loop(0, self.pieces)
+        def _(q):
+            for d in self.plan.steps:
+                sends = [self.cross(d, k, q)[:2] for k in range(self.plan.wide)]
+                sends += [self.over(d, k, q) for k in range(1, self.plan.wide)]
+                if d:
+                    sends.append(self.along(d, q))
+                for cond, go in sends:
+                    run_if(cond, lambda go=go: go().wait_send())
 
 
 def scatter_rows(parts, window, collective_id, pieces=4):
     ep_count, rows, width = parts.shape
     plan = Plan(ep_count, window)
-    n, wide = len(plan.steps), plan.wide
-    sem = lambda *lead: pltpu.SemaphoreType.DMA(lead + (pieces,))
-    blocks = lambda *lead: pltpu.VMEM(lead + (rows, width), parts.dtype)
+
+    def kernel(p_ref, out_ref, *scratch):
+        total = RowSum(plan, pieces, p_ref, scratch)
+        plan.greet(total.a, total.b, total.c)
+        ks = list(range(1, plan.wide)) + [0]
+        total.start(ks)
+        for k in ks[:-1]:
+            total.stage_over(k)
+        total.stage_dests(0, pieces)
+        out_ref[...] = total.result()
+        total.drain()
+
     return pl.pallas_call(
-        functools.partial(scatter_kernel, plan, pieces),
+        kernel,
         out_shape=jax.ShapeDtypeStruct((rows, width), parts.dtype),
         in_specs=[pl.BlockSpec(memory_space=pl.ANY)],
         out_specs=pl.BlockSpec(memory_space=pltpu.VMEM),
-        scratch_shapes=[blocks(n, wide), blocks(n, wide), blocks(n, wide - 1), blocks(n), blocks(n),
-                        sem(n, wide), sem(n, wide), sem(n, wide), sem(n, wide),
-                        sem(n), sem(n), sem(n), sem(n, wide)],
+        scratch_shapes=RowSum.scratch(plan, rows, width, parts.dtype, pieces),
         compiler_params=pltpu.CompilerParams(
             collective_id=collective_id, has_side_effects=True, vmem_limit_bytes=VMEM_MOST),
         name="scatter_rows",
     )(parts)
 
 
-def whole_kernel(sizes, p_ref, out_ref, held, rcb, rxb, rbb, rab, *sems):
-    groups, long, wide = sizes
-    g = lax.axis_index("grp")
-    me = lax.axis_index("ep")
-    a, b, c = me // (2 * wide), (me // 2) % wide, me % 2
-    sc, rc, sx, rx, sb, rb, sa, ra, ld = sems
-
-    def dev(gg, aa, bb, cc):
-        return {"grp": gg, "ep": (aa * wide + bb) * 2 + cc}
-
-    def slot(gg, aa, bb, cc):
-        return ((gg * long + aa) * wide + bb) * 2 + cc
-
-    def remote(src, dst, ssem, rsem, to):
-        return pltpu.make_async_remote_copy(
-            src_ref=src, dst_ref=dst, send_sem=ssem, recv_sem=rsem, device_id=to, device_id_type=MESH)
-
-    peers = ([dev(g, a, b, 1 - c)] + [dev((g + k) % groups, a, b, c) for k in range(1, groups)]
-             + [dev(g, a, (b + k) % wide, c) for k in range(1, wide)]
-             + [dev(g, (a + k) % long, b, c) for k in range(1, long)])
-    barrier = pltpu.get_barrier_semaphore()
-    for to in peers:
-        pl.semaphore_signal(barrier, inc=1, device_id=to, device_id_type=MESH)
-    pl.semaphore_wait(barrier, len(peers))
-
-    def spot(kx, ka, kb, cc):
-        return slot((g + groups - kx) % groups, (a + long - ka) % long, (b + wide - kb) % wide, cc)
-
-    keys = [(kx, ka, kb) for kx in list(range(1, groups)) + [0] for kb in list(range(1, wide)) + [0]
-            for ka in list(range(1, long)) + [0]]
-    cross = {}
-    load = {}
-    for kx, ka, kb in keys:
-        key = (kx, ka, kb)
-        cross[key] = remote(p_ref.at[spot(kx, ka, kb, 1 - c)], rcb.at[key], sc.at[key], rc.at[key],
-                            dev(g, a, b, 1 - c))
-        load[key] = pltpu.make_async_copy(p_ref.at[spot(kx, ka, kb, c)], held.at[key], ld.at[key])
-        cross[key].start()
-        load[key].start()
-
-    def over_x(kx, ka, kb):
-        return remote(held.at[kx, ka, kb], rxb.at[kx - 1, ka, kb], sx.at[kx - 1, ka, kb], rx.at[kx - 1, ka, kb],
-                      dev((g + groups - kx) % groups, a, b, c))
-
-    def over_b(ka, kb):
-        return remote(held.at[0, ka, kb], rbb.at[ka, kb - 1], sb.at[ka, kb - 1], rb.at[ka, kb - 1],
-                      dev(g, a, (b + wide - kb) % wide, c))
-
-    def over_a(ka):
-        return remote(held.at[0, ka, 0], rab.at[ka - 1], sa.at[ka - 1], ra.at[ka - 1],
-                      dev(g, (a + long - ka) % long, b, c))
-
-    for key in keys:
-        load[key].wait()
-        cross[key].wait_recv()
-        add_rows(held.at[key], [rcb.at[key]])
-        if key[0]:
-            over_x(*key).start()
-
-    for kb in list(range(1, wide)) + [0]:
-        for ka in list(range(1, long)) + [0]:
-            for kx in range(1, groups):
-                over_x(kx, ka, kb).wait_recv()
-            add_rows(held.at[0, ka, kb], [rxb.at[kx - 1, ka, kb] for kx in range(1, groups)])
-            if kb:
-                over_b(ka, kb).start()
-    for ka in list(range(1, long)) + [0]:
-        for kb in range(1, wide):
-            over_b(ka, kb).wait_recv()
-        add_rows(held.at[0, ka, 0], [rbb.at[ka, kb - 1] for kb in range(1, wide)])
-        if ka:
-            over_a(ka).start()
-    for ka in range(1, long):
-        over_a(ka).wait_recv()
-    add_rows(held.at[0, 0, 0], [rab.at[ka - 1] for ka in range(1, long)], out_ref)
-    for key in keys:
-        cross[key].wait_send()
-        if key[0]:
-            over_x(*key).wait_send()
-    for ka in range(long):
-        for kb in range(1, wide):
-            over_b(ka, kb).wait_send()
-        if ka:
-            over_a(ka).wait_send()
-
-
-def scatter_whole(parts, collective_id):
-    count, rows, width = parts.shape
+class Place:
+    def __init__(self, groups, ep_count):
+        self.sizes = {"x": groups, "a": 4, "b": ep_count // 8}
+
+    def locate(self):
+        me, wide = lax.axis_index("ep"), self.sizes["b"]
+        self.at = {"x": lax.axis_index("grp"), "a": me // (2 * wide), "b": (me // 2) % wide, "c": me % 2}
+
+    def dev(self, **moved):
+        at = {**self.at, **moved}
+        return {"grp": at["x"], "ep": (at["a"] * self.sizes["b"] + at["b"]) * 2 + at["c"]}
+
+    def slot(self, **moved):
+        at = {**self.at, **moved}
+        return ((at["x"] * self.sizes["a"] + at["a"]) * self.sizes["b"] + at["b"]) * 2 + at["c"]
+
+    def back(self, axis, k):
+        return (self.at[axis] + self.sizes[axis] - k) % self.sizes[axis]
+
+    def greet(self):
+        peers = [self.dev(c=1 - self.at["c"])] + [
+            self.dev(**{axis: self.back(axis, k)}) for axis in "xba" for k in range(1, self.sizes[axis])]
+        barrier = pltpu.get_barrier_semaphore()
+        for to in peers:
+            pl.semaphore_signal(barrier, inc=1, device_id=to, device_id_type=MESH)
+        pl.semaphore_wait(barrier, len(peers))
+
+
+def from_far(size):
+    return list(range(1, size)) + [0]
+
+
+class WholeSum:
+    @staticmethod
+    def scratch(sizes, axes, rows, width, dtype, sources):
+        n1, n2, n3 = (sizes[axis] for axis in axes)
+        blocks = lambda *lead: pltpu.VMEM(lead + (rows, width), dtype)
+        sem = lambda *lead: pltpu.SemaphoreType.DMA(lead)
+        full = (n1, n2, n3)
+        one, two, three = (n1 - 1, n2, n3), (n2 - 1, n3), (n3 - 1,)
+        return [blocks(*full), blocks(*full), blocks(*one), blocks(*two), blocks(*three),
+                sem(*full, sources), sem(*full, sources), sem(*full, sources), sem(*one), sem(*one), sem(*two), sem(*two), sem(*three), sem(*three)]
+
+    def __init__(self, place, axes, pieces, scratch):
+        self.place, self.axes, self.pieces = place, axes, pieces
+        (self.held, self.rcb, self.r1, self.r2, self.r3,
+         self.ld, self.sc, self.rc, self.s1, self.q1, self.s2, self.q2, self.s3, self.q3) = scratch
+        self.n1, self.n2, self.n3 = (place.sizes[axis] for axis in axes)
+        self.groups = [[(k1, k2, k3) for k2 in from_far(self.n2) for k3 in from_far(self.n3)]
+                       for k1 in from_far(self.n1)]
+
+    def slot(self, key, c):
+        return self.place.slot(c=c, **{axis: self.place.back(axis, k) for axis, k in zip(self.axes, key)})
+
+    def loads(self, key):
+        c = self.place.at["c"]
+        for n, (ref, first, at, count) in enumerate(self.pieces):
+            frm, to = pl.ds(first, count), pl.ds(at, count)
+            yield pltpu.make_async_copy(
+                ref.at[self.slot(key, c), :, frm], self.held.at[key + (slice(None), to)],
+                self.ld.at[key + (n,)])
+
+    def crossings(self, key):
+        c = self.place.at["c"]
+        for n, (ref, first, at, count) in enumerate(self.pieces):
+            frm, to = pl.ds(first, count), pl.ds(at, count)
+            yield send(ref.at[self.slot(key, 1 - c), :, frm], self.rcb.at[key + (slice(None), to)],
+                       self.sc.at[key + (n,)], self.rc.at[key + (n,)], self.place.dev(c=1 - c))
+
+    def hop(self, level, key):
+        buf, ssem, rsem = ((self.r1, self.s1, self.q1), (self.r2, self.s2, self.q2), (self.r3, self.s3, self.q3))[level]
+        axis, k = self.axes[level], key[level]
+        far = (k - 1,) + key[level + 1 :]
+        return send(self.held.at[key], buf.at[far], ssem.at[far], rsem.at[far],
+                    self.place.dev(**{axis: self.place.back(axis, k)}))
+
+    def start(self, i):
+        for key in self.groups[i]:
+            for go in self.crossings(key):
+                go.start()
+            for go in self.loads(key):
+                go.start()
+
+    def stage_core(self, i):
+        for key in self.groups[i]:
+            for go in self.loads(key):
+                go.wait()
+            for go in self.crossings(key):
+                go.wait_recv()
+            add_rows(self.held.at[key], [self.rcb.at[key]])
+            if key[0]:
+                self.hop(0, key).start()
+
+    def stage_one(self, k2):
+        for k3 in from_far(self.n3):
+            for k1 in range(1, self.n1):
+                self.hop(0, (k1, k2, k3)).wait_recv()
+            add_rows(self.held.at[0, k2, k3], [self.r1.at[k1 - 1, k2, k3] for k1 in range(1, self.n1)])
+            if k2:
+                self.hop(1, (0, k2, k3)).start()
+
+    def stage_two(self):
+        for k3 in from_far(self.n3):
+            for k2 in range(1, self.n2):
+                self.hop(1, (0, k2, k3)).wait_recv()
+            add_rows(self.held.at[0, 0, k3], [self.r2.at[k2 - 1, k3] for k2 in range(1, self.n2)])
+            if k3:
+                self.hop(2, (0, 0, k3)).start()
+
+    def stage_three(self, out):
+        for k3 in range(1, self.n3):
+            self.hop(2, (0, 0, k3)).wait_recv()
+        add_rows(self.held.at[0, 0, 0], [self.r3.at[k3 - 1] for k3 in range(1, self.n3)], out)
+
+    def drain(self):
+        for group in self.groups:
+            for key in group:
+                for go in self.crossings(key):
+                    go.wait_send()
+                if key[0]:
+                    self.hop(0, key).wait_send()
+                elif key[1]:
+                    self.hop(1, key).wait_send()
+                elif key[2]:
+                    self.hop(2, key).wait_send()
+
+
+def scatter_whole(parts, collective_id, pairs=None):
+    rows = parts[0].shape[1]
+    width = sum(part.shape[2] for part in parts)
     groups, ep_count = lax.axis_size("grp"), lax.axis_size("ep")
-    long, wide = 4, ep_count // 8
-    sem = pltpu.SemaphoreType.DMA
-    blocks = lambda *lead: pltpu.VMEM(lead + (rows, width), parts.dtype)
-    full = (groups, long, wide)
-
-    def kernel(p_ref, out_ref, *scratch):
-        whole_kernel(full, p_ref, out_ref, *scratch)
-
-    return pl.pallas_call(
+    place = Place(groups, ep_count)
+    tiles = width // HEAD
+    cuts = [0, tiles // 2 * HEAD, width]
+    orders = ["xba", "xba" if pairs is not None else "bxa"]
+
+    def kernel(*refs):
+        sources, refs = refs[: len(parts)], refs[len(parts) :]
+        if pairs is not None:
+            pair_ref, refs = refs[0], refs[1:]
+        out_ref, refs = refs[0], refs[1:]
+        if pairs is not None:
+            pair_out, refs = refs[0], refs[1:]
+        place.locate()
+        sums = []
+        for n, axes in enumerate(orders):
+            low, high, first, pieces = cuts[n], cuts[n + 1], 0, []
+            for ref in sources:
+                begin, end = max(low, first), min(high, first + ref.shape[2])
+                if begin < end:
+                    pieces.append((ref, begin - first, begin - low, end - begin))
+                first += ref.shape[2]
+            sums.append(WholeSum(place, axes, pieces, refs[:14]))
+            refs = refs[14:]
+        outs = [out_ref.at[:, pl.ds(cuts[n], cuts[n + 1] - cuts[n])] for n in range(len(orders))]
+        place.greet()
+        if pairs is None:
+            couples = [sums[n : n + 2] for n in range(0, len(sums), 2)]
+            for couple in couples:
+                for i in range(max(s.n1 for s in couple)):
+                    for s in couple:
+                        if i < s.n1:
+                            s.start(i)
+
+            def core(couple):
+                for i in range(max(s.n1 for s in couple)):
+                    for s in couple:
+                        if i < s.n1:
+                            s.stage_core(i)
+
+            def one(couple):
+                for i in range(max(s.n2 for s in couple)):
+                    for s in couple:
+                        if i < s.n2:
+                            s.stage_one(from_far(s.n2)[i])
+
+            def two(couple):
+                for s in couple:
+                    s.stage_two()
+
+            for stage in (core, one, two):
+                for couple in couples:
+                    stage(couple)
+            for s, out in zip(sums, outs):
+                s.stage_three(out)
+        else:
+            total = RowSum(plan, 4, pair_ref, refs)
+            ks = from_far(plan.wide)
+            for one in sums:
+                for i in range(one.n1 - 1):
+                    one.start(i)
+            total.start(ks[:-1])
+            for one in sums:
+                one.start(one.n1 - 1)
+            total.start(ks[-1:])
+            for one in sums:
+                for i in range(one.n1 - 1):
+                    one.stage_core(i)
+            for k in ks[:-1]:
+                total.stage_over(k)
+            for one in sums:
+                one.stage_core(one.n1 - 1)
+            total.stage_dests(0, 2)
+            for k2 in from_far(sums[0].n2):
+                sums[0].stage_one(k2)
+            total.stage_dests(2, 3)
+            sums[0].stage_two()
+            for one in sums[1:]:
+                for k2 in from_far(one.n2):
+                    one.stage_one(k2)
+            total.stage_dests(3, 4)
+            for one in sums[1:]:
+                one.stage_two()
+            pair_out[...] = total.result()
+            for one, out in zip(sums, outs):
+                one.stage_three(out)
+            total.drain()
+        for s in sums:
+            s.drain()
+
+    operands, anywhere = list(parts), pl.BlockSpec(memory_space=pl.ANY)
+    out_shape = [jax.ShapeDtypeStruct((rows, width), jnp.float32)]
+    scratch = []
+    for n, axes in enumerate(orders):
+        scratch += WholeSum.scratch(place.sizes, axes, rows, cuts[n + 1] - cuts[n], parts[0].dtype, len(parts))
+    if pairs is not None:
+        plan = Plan(ep_count, True)
+        operands.append(pairs)
+        out_shape.append(jax.ShapeDtypeStruct(pairs.shape[1:], pairs.dtype))
+        scratch += RowSum.scratch(plan, pairs.shape[1], pairs.shape[2], pairs.dtype, 4)
+    got = pl.pallas_call(
         kernel,
-        out_shape=jax.ShapeDtypeStruct((rows, width), jnp.float32),
-        in_specs=[pl.BlockSpec(memory_space=pl.ANY)],
-        out_specs=pl.BlockSpec(memory_space=pltpu.VMEM),
-        scratch_shapes=[blocks(*full), blocks(*full), blocks(groups - 1, long, wide), blocks(long, wide - 1),
-                        blocks(long - 1),
-                        sem(full), sem(full), sem((groups - 1, long, wide)), sem((groups - 1, long, wide)),
-                        sem((long, wide - 1)), sem((long, wide - 1)), sem((long - 1,)), sem((long - 1,)), sem(full)],
+        out_shape=tuple(out_shape),
+        in_specs=[anywhere] * len(operands),
+        out_specs=tuple(pl.BlockSpec(memory_space=pltpu.VMEM) for _ in out_shape),
+        scratch_shapes=scratch,
         compiler_params=pltpu.CompilerParams(
             collective_id=collective_id, has_side_effects=True, vmem_limit_bytes=VMEM_MOST),
-        name="scatter_whole",
-    )(parts)
+        name="scatter_whole" if pairs is None else "scatter_pairs",
+    )(*operands)
+    return got[0] if pairs is None else got
 
 
 def visible_bias(shape, first_key, start, first_query):
@@ -712,7 +897,7 @@
 
 def finish_kernel(
     x_ref, gain_ref, res_ref, hid_ref, q_ref, kv_ref, cos_ref, sin_ref, wq_ref, wk_ref, wv_ref,
-    dw_ref, out_ref, gain_out, acc,
+    dq_ref, dk_ref, dv_ref, out_ref, gain_out, acc,
 ):
     step = pl.program_id(0)
 
@@ -731,8 +916,8 @@
         inner_right(grads[0], wq_ref[...]) + inner_right(grads[1], wk_ref[...]) + inner_right(grads[2], wv_ref[...])
     )
     hidden = hid_ref[...]
-    for i in range(3):
-        dw_ref[i] = inner_left(hidden, grads[i]).astype(jnp.bfloat16)
+    for ref, grad in zip((dq_ref, dk_ref, dv_ref), grads):
+        ref[...] = inner_left(hidden, grad).astype(jnp.bfloat16)
 
     @pl.when(step == pl.num_programs(0) - 1)
     def _():
@@ -751,7 +936,9 @@
     return pl.pallas_call(
         finish_kernel,
         out_shape=(
-            jax.ShapeDtypeStruct((3, width, width), jnp.bfloat16),
+            jax.ShapeDtypeStruct((width, width), jnp.bfloat16),
+            jax.ShapeDtypeStruct((width, width), jnp.bfloat16),
+            jax.ShapeDtypeStruct((width, width), jnp.bfloat16),
             jax.ShapeDtypeStruct((rows, width), jnp.bfloat16),
             jax.ShapeDtypeStruct((1, width), jnp.float32),
         ),
@@ -759,7 +946,7 @@
         in_specs=[whole_spec(rows, width), whole_spec(1, width), whole_spec(rows, width), whole_spec(rows, width),
                   pl.BlockSpec((rows, tile), lambda i: (0, i)), pl.BlockSpec((rows, 2 * tile), lambda i: (0, i)),
                   whole_spec(rows, HEAD), whole_spec(rows, HEAD), column, column, column],
-        out_specs=(pl.BlockSpec((3, width, tile), lambda i: (0, 0, i)), whole_spec(rows, width), whole_spec(1, width)),
+        out_specs=(column, column, column, whole_spec(rows, width), whole_spec(1, width)),
         scratch_shapes=[pltpu.VMEM((rows, width), jnp.float32)],
         cost_estimate=pl.CostEstimate(flops=12 * rows * width * width, bytes_accessed=12 * width * width, transcendentals=0),
         name="finish",
@@ -918,7 +1105,7 @@
     back, given, flat_in, pre_grad, lift_grad, middle, result_grad = run_experts(
         places, arrived, grads_all, rank, share, expert_gate, expert_up, expert_down, capacity
     )
-    back_sum = scatter_rows(back, False, 3, 2)
+    back_sum = scatter_rows(back, False, 3)
     given, back_sum = lax.optimization_barrier((given, back_sum))
     routed = wide(lax.psum_scatter(given, "ep", scatter_dimension=0))
     group_count = lax.axis_size("grp")
@@ -959,16 +1146,19 @@
     pair_parts, query_lin_grad = attend_back(
         info, queries, mixed_grad, mixed, start[None, :], log_total, cosine, sine, pairs
     )
-    pair_grads = scatter_rows(pair_parts, True, 4, 2)
-
     by_device = lambda v: low(v).reshape(device_count, width // device_count, -1)
-    early = jnp.concatenate(
-        [by_device(inner_left(ffn_low, shared_pre_grad)), by_device(inner_left(ffn_low, shared_lift_grad)),
-         by_device(inner_left(grad_low, shared_mid)), by_device(inner_left(mixed_low, mixer_grad_low))], axis=2
-    )
-    early_sum = scatter_whole(early, 5)
-
-    weight_grads, tokens_grad, mixer_gain_grad = finish(
+    early = [
+        by_device(part)
+        for part in (inner_left(ffn_low, shared_pre_grad), inner_left(ffn_low, shared_lift_grad),
+                     inner_left(grad_low, shared_mid), inner_left(mixed_low, mixer_grad_low))
+    ]
+    if ep_count > 16:
+        pair_grads = scatter_rows(pair_parts, True, 4)
+        early_sum = scatter_whole(early, 5)
+    else:
+        early_sum, pair_grads = scatter_whole(early, 5, pair_parts)
+
+    query_part, key_part, value_part, tokens_grad, mixer_gain_grad = finish(
         tokens[0], mixer_gain, residual_grad, hidden_low, query_lin_grad, pair_grads, cosine, sine,
         query_weight, key_weight, value_weight,
     )
@@ -980,10 +1170,7 @@
          jnp.broadcast_to(squares[None, :], (width, 3))], axis=1
     )
     extras = jnp.pad(extras, ((0, 0), (0, HEAD - extras.shape[1])))
-    late = jnp.concatenate(
-        [by_device(weight_grads[0]), by_device(weight_grads[1]), by_device(weight_grads[2]), by_device(extras)], axis=2
-    )
-    late_sum = scatter_whole(late, 6)
+    late_sum = scatter_whole([by_device(v) for v in (query_part, key_part, value_part, extras)], 6)
     extra_sum = late_sum[:, 3 * width :]
     entry_count = rows * device_count * width
     stream_rms = jnp.sqrt(extra_sum[0, expert_count + 2 : expert_count + 5] / entry_count)

time: 865 us -> 765 us (0.88)
  Pallas kernels: 703 us -> 626 us
  other arithmetic: 36 us -> 22.1 us
    pallas_call x5 -> x4, Pallas kernels: 422 us -> 343 us  [the longest x2 241 us: scatter_whole(): pl.pallas_call(kernel, out_shape=tuple(out_shape), in_specs=[anywhere] *...]
    concatenate x2 -> x0, other arithmetic: 14.1 us -> none  [the longest x1 9.4 us: local(): jnp.concatenate([by_device(weight_grads[0]), by_device(weight_grads[1]),...]
  transfers between devices with their start and end apart: 5 -> 5, of which waited for: 0 -> 0; matrix products, arithmetic and copies ran while one was open for 10% -> 10% of each run, Pallas kernels for 54% -> 57%
where the time goes in v3:
time: 765 us; the launch traced here: 761 us
  Pallas kernels  626 us (82%)
  matrix products  67.4 us (9%)
  local copies, waits for them, and re-layouts  28.7 us (4%)
  other arithmetic  22.1 us (3%)
  between operations  17 us (2%)
    pallas_call x2, Pallas kernels, scatter_whole(): pl.pallas_call(kernel, out_shape=tuple(out_shape), in_specs=[anywhere] *...  241 us
    pallas_call x2, Pallas kernels, gather_rows(): pl.pallas_call(functools.partial(gather_kernel, plan, pieces), out_shape=...  184 us
    pallas_call x1, Pallas kernels, scatter_rows(): pl.pallas_call(kernel, out_shape=jax.ShapeDtypeStruct((rows, width), part...  87.2 us
    pallas_call x1, Pallas kernels, run_experts(): pl.pallas_call(experts_kernel, out_shape=(shape(count, rows, side), shape...  73.6 us
    dot_general x9, matrix products, inner_left(): lax.dot_general(left_op, right_op, (((0,), (0,)), ((), ())), preferred_el...  50.3 us
  transfers between devices with their start and end apart: 5, of which 0 were waited for; matrix products, arithmetic and copies ran while one was open for 10% of the time, Pallas kernels for 57%

profile of v3, /device:TPU:0, one launch (start us, length us, event | category | flops | bytes accessed | tf_op | source)
XLA Modules:
  0.0 761.5 jit_solution(4135018151828021881)
XLA Ops:
  8.6 1.3 broadcast_in_dim.107.gain_ref
  10.6 8.6 %project.1 = (bf16[256,1280]{1,0:T(8,128)(2,1)}, bf16[256,1280]{1,0:T(8,128)(2,1)}, bf16[256,2560]{1,0:T(8,128)(2,1)}) custom-call(bf16[256,1280]{1,0:T(8,128)(2,1)} %bitcast.99, f32[1,1280]{1,0:T(1,128)} %broadcast_in_dim.107.gain_ref, f32[256,128]{1,0:T(8,128)} %pad_maximum_fusion.1.cos_ref, f32[256,128]{1,0:T(8,128)} %pad_maximum_fusion.2.sin_ref, ...), custom_call_target="tpu_custom_call" | custom-call | flops 2516582400 | bytes 9830400 | tf_op jit(solution)/shard_map/project/pallas_call | solution.py:725
  19.2 34.8 %gather_rows.2.kv_ref = bf16[16,256,2560]{2,1,0:T(8,128)(2,1)} custom-call(bf16[256,2560]{1,0:T(8,128)(2,1)} %get-tuple-element.43.x_ref), custom_call_target="tpu_custom_call" | custom-call | tf_op jit(solution)/shard_map/gather_rows/pallas_call | solution.py:233
  58.3 7.9 %attend.1 = (f32[10,128,256]{2,1,0:T(8,128)}, bf16[256,1280]{1,0:T(8,128)(2,1)}, f32[10,1,256]{2,1,0:T(1,128)}) custom-call(s32[2]{0:T(128)} %pad_add_fusion.info, bf16[256,1280]{1,0:T(8,128)(2,1)} %get-tuple-element.42.q_ref, s32[1,256]{1,0:T(1,128)} %bitcast.104, bf16[16,256,2560]{2,1,0:T(8,128)(2,1)} %gather_rows.2.kv_ref), custom_call_target="tpu_custom_call" | custom-call | flops 3019898880 | bytes 11796480 | tf_op jit(solution)/shard_map/attend/pallas_call | solution.py:783
  66.2 3.9 multiply_reduce_fusion.5
  70.1 1.0 copy-done.2
  72.8 1.0 concatenate.18.x_ref
  73.8 148.7 %gather_rows.3.x_ref = bf16[16,256,1408]{2,1,0:T(8,128)(2,1)} custom-call(bf16[256,1408]{1,0:T(8,128)(2,1)} %concatenate.18.x_ref), custom_call_target="tpu_custom_call" | custom-call | tf_op jit(solution)/shard_map/gather_rows/pallas_call | solution.py:233
  222.6 2.6 select_reduce_fusion
  226.0 2.0 copy.60.rank_col
  229.2 73.6 %run_experts.1 = (bf16[16,256,1408]{2,1,0:T(8,128)(2,1)}, bf16[16,256,1280]{2,1,0:T(8,128)(2,1)}, bf16[3072,1280]{1,0:T(8,128)(2,1)}, bf16[3072,896]{1,0:T(8,128...) custom-call(s32[2]{0:T(128)} %pad_add_fusion.1.where_ref, ...), custom_call_target="tpu_custom_call" | custom-call | flops 56371445760 | bytes 62914560 | tf_op jit(solution)/shard_map/run_experts/pallas_call | solution.py:1010
  302.8 8.4 %fusion.7 = bf16[896,640]{1,0:T(8,128)(2,1)S(1)} fusion(bf16[3072,896]{1,0:T(8,128)(2,1)} %get-tuple-element.66, bf16[3072,1280]{1,0:T(8,128)(2,1)} %get-tuple-element.67), kind=kOutput, calls=%fused_computation.21 | convolution fusion | flops 3523788800 | bytes 10584064 | tf_op jit(solution)/shard_map/dot_general | solution.py:26
  311.2 4.5 fusion.10
  315.7 1.5 pad_maximum_fusion
  317.3 13.3 %convolution_convert_fusion.1 = bf16[1280,896]{1,0:T(8,128)(2,1)} fusion(bf16[3072,1280]{1,0:T(8,128)(2,1)} %get-tuple-element.63, bf16[3072,896]{1,0:T(8,128)(2,1)} %get-tuple-element.65), kind=kOutput, calls=%fused_computation.5 | convolution fusion | flops 7047577600 | bytes 15663104 | tf_op jit(solution)/shard_map/dot_general | solution.py:26
  330.7 13.4 %convolution_convert_fusion.2 = bf16[1280,896]{1,0:T(8,128)(2,1)} fusion(bf16[3072,1280]{1,0:T(8,128)(2,1)} %get-tuple-element.63, bf16[3072,896]{1,0:T(8,128)(2,1)} %get-tuple-element.64), kind=kOutput, calls=%fused_computation.6 | convolution fusion | flops 7047577600 | bytes 15663104 | tf_op jit(solution)/shard_map/dot_general | solution.py:26
  344.1 87.2 %scatter_rows.1 = bf16[256,1408]{1,0:T(8,128)(2,1)} custom-call(bf16[16,256,1408]{2,1,0:T(8,128)(2,1)} %get-tuple-element.48.p_ref), custom_call_target="tpu_custom_call" | custom-call | tf_op jit(solution)/shard_map/scatter_rows/pallas_call | solution.py:430
  431.4 1.1 copy-done.1
  433.2 0.8 fusion.33
  434.9 0.8 fusion.34
  436.7 1.9 multiply_convert_fusion.1
  439.4 0.8 fusion.4
  440.2 3.2 copy.61
  443.4 3.3 convolution_convert_fusion.5
  446.7 2.3 convolution_convert_fusion.4
  449.0 0.9 fusion.35
  450.5 0.9 copy-done.12
  451.4 0.9 fusion.5
  452.9 1.3 multiply_reduce_fusion.2
  456.0 2.9 convolution_convert_fusion
  458.9 1.1 copy-done.32
  459.9 2.0 convolution_convert_fusion.6.g_ref
  461.9 9.8 %attend_back.1 = (bf16[16,256,2560]{2,1,0:T(8,128)(2,1)}, bf16[256,1280]{1,0:T(8,128)(2,1)}) custom-call(s32[2]{0:T(128)} %pad_add_fusion.info, bf16[256,1280]{1,0:T(8,128)(2,1)} %get-tuple-element.42.q_ref, bf16[256,1280]{1,0:T(8,128)(2,1)} %convolution_convert_fusion.6.g_ref, f32[10,128,256]{2,1,0:T(8,128)} %get-tuple-element.52.mixed_ref, ...), custom_call_target="tpu_custom_call" | custom-call | flops 7549747200 | bytes 23592960 | tf_op jit(solution)/shard_map/attend_back/pallas_call | solution.py:862
  471.7 162.9 %scatter_pairs.1 = (f32[40,3968]{1,0:T(8,128)}, bf16[256,2560]{1,0:T(8,128)(2,1)}) custom-call(bf16[32,40,896]{2,1,0:T(8,128)(2,1)} %bitcast.92, bf16[32,40,896]{2,1,0:T(8,128)(2,1)} %bitcast.93, bf16[32,40,896]{2,1,0:T(8,128)(2,1)} %bitcast.91, bf16[32,40,1280]{2,1,0:T(8,128)(2,1)} %bitcast.90, bf16[16,256,2560]{2,1,0:T(8,128)(2,1)} %get-tuple-element.55.refs_4_), custom_call_target="tpu_custom_call" | custom-call | tf_op jit(solution)/shard_map/scatter_pairs/pallas_call | solution.py:672
  634.6 1.6 slice.72
  636.2 1.8 slice_bitcast_fusion
  638.0 1.5 convolution_convert_fusion.7
  639.6 14.3 %finish.1 = (bf16[1280,1280]{1,0:T(8,128)(2,1)}, bf16[1280,1280]{1,0:T(8,128)(2,1)}, bf16[1280,1280]{1,0:T(8,128)(2,1)}, bf16[256,1280]{1,0:T(8,128)(2,1)}, f32[1,1280]{1,0:T(1,128)}) custom-call(bf16[256,1280]{1,0:T(8,128)(2,1)} %bitcast.100, f32[1,1280]{1,0:T(1,128)} %broadcast_in_dim.107.gain_ref, f32[256,1280]{1,0:T(8,128)} %copy-done.7, ...), custom_call_target="tpu_custom_call" | custom-call | flops 5033164800 | bytes 19660800 | tf_op jit(solution)/shard_map/finish/pallas_call | solution.py:936
  654.6 2.8 bitcast_convert_fusion
  657.4 2.8 bitcast_convert_fusion.1
  660.2 2.9 bitcast_convert_fusion.2
  663.1 4.1 multiply_reduce_fusion
  667.2 2.0 maximum_convert_fusion
  669.6 0.8 pad.5.clone
  670.4 78.2 %scatter_whole.1 = f32[40,3968]{1,0:T(8,128)} custom-call(bf16[32,40,1280]{2,1,0:T(8,128)(2,1)} %bitcast.95, bf16[32,40,1280]{2,1,0:T(8,128)(2,1)} %bitcast.96, bf16[32,40,1280]{2,1,0:T(8,128)(2,1)} %bitcast.97, bf16[32,40,128]{2,1,0:T(8,128)(2,1)} %bitcast.98), custom_call_target="tpu_custom_call" | custom-call | tf_op jit(solution)/shard_map/scatter_whole/pallas_call | solution.py:672
  748.6 2.0 fusion.31
  751.3 1.5 slice_reduce_fusion
  752.8 1.3 sqrt_bitcast_fusion
  (116 shorter events, 16.4 us)
Async XLA Ops:
  7.2 222.0 %all-gather.3.cloned.1.call-start = ((), (), s32[]{:S(2)}) async-start(), calls=%async_computation.8 | async-start | bytes 11141120 | tf_op jit(solution)/shard_map/all_gather | solution.py:1077
  19.2 34.9 %copy-start.33 = (s32[1,4]{1,0:T(1,128)S(1)}, s32[1,4]{1,0:T(1,128)}, u32[]{:S(2)}) copy-start(s32[1,4]{1,0:T(1,128)} %param.18) | copy-start | bytes 52
  19.2 38.3 %copy-start.28 = (s32[1,256,7]{1,0,2:T(1,128)S(1)}, s32[1,256,7]{1,0,2:T(1,128)}, u32[]{:S(2)}) copy-start(s32[1,256,7]{1,0,2:T(1,128)} %param.19) | copy-start | bytes 21508
  54.0 600.5 %reduce-scatter.11.cloned.1.call-start = ((), (), s32[]{:S(2)}) async-start(), calls=%async_computation.7 | async-start | bytes 3440640 | tf_op jit(solution)/shard_map/reduce_scatter | solution.py:1118
  54.4 3.9 copy-start.29
  58.3 7.9 %copy-start.19 = (bf16[1,256,1280]{2,1,0:T(8,128)(2,1)S(1)}, bf16[1,256,1280]{2,1,0:T(8,128)(2,1)}, u32[]{:S(2)}) copy-start(bf16[1,256,1280]{2,1,0:T(8,128)(2,1)} %param.17) | copy-start | bytes 1966084
  66.2 5.0 copy-start.22
  66.2 5.1 copy-start.20
  70.1 1.0 copy-start.2
  70.1 2.6 copy-start.30
  70.1 2.6 copy-start.25
  71.4 151.2 %copy-start = (bf16[256,1280]{1,0:T(8,128)(2,1)}, bf16[256,1280]{1,0:T(8,128)(2,1)S(1)}, u32[]{:S(2)}) copy-start(bf16[256,1280]{1,0:T(8,128)(2,1)S(1)} %multiply_convert_fusion) | copy-start | bytes 1966084
  302.8 8.4 %copy-start.34 = (bf16[3072,1280]{1,0:T(8,128)(2,1)S(1)}, bf16[3072,1280]{1,0:T(8,128)(2,1)}, u32[]{:S(2)}) copy-start(bf16[3072,1280]{1,0:T(8,128)(2,1)} %get-tuple-element.67) | copy-start | bytes 23592964
  302.8 8.4 %copy-start.35 = (bf16[3072,896]{1,0:T(8,128)(2,1)S(1)}, bf16[3072,896]{1,0:T(8,128)(2,1)}, u32[]{:S(2)}) copy-start(bf16[3072,896]{1,0:T(8,128)(2,1)} %get-tuple-element.66) | copy-start | bytes 16515076
  317.3 340.1 %reduce-scatter.9.cloned.1.call-start = ((), (), s32[]{:S(2)}) async-start(), calls=%async_computation.6 | async-start | bytes 3440640 | tf_op jit(solution)/shard_map/reduce_scatter | solution.py:1118
  330.6 329.5 %reduce-scatter.7.cloned.1.call-start = ((), (), s32[]{:S(2)}) async-start(), calls=%async_computation.5 | async-start | bytes 3440640 | tf_op jit(solution)/shard_map/reduce_scatter | solution.py:1118
  344.1 319.0 %reduce-scatter.5.cloned.1.call-start = ((), (), s32[]{:S(2)}) async-start(), calls=%async_computation.4 | async-start | bytes 11141120 | tf_op jit(solution)/shard_map/reduce_scatter | solution.py:1110
  431.4 1.1 copy-start.1
  431.4 1.9 copy-start.9
  433.2 1.6 copy-start.11
  434.9 1.1 copy-start.5
  434.9 1.9 copy-start.13
  438.6 0.8 copy-start.16
  446.7 2.3 copy-start.10
  446.7 2.3 copy-start.18
  449.0 1.2 copy-start.8
  449.0 1.3 copy-start.15
  449.0 2.4 copy-start.12
  451.4 0.9 copy-start.27
  451.4 1.5 copy-start.3
  451.4 1.5 copy-start.21
  451.4 1.5 copy-start.23
  451.4 1.5 copy-start.26
  452.9 1.9 copy-start.31
  452.9 1.9 copy-start.6
  454.8 1.2 copy-start.14
  456.0 2.9 copy-start.7
  456.0 3.9 copy-start.32
  660.2 2.9 copy-start.4
  660.2 2.9 copy-start.17
  663.1 6.2 copy-start.24
Sparse Core Ops, SparseCore 0:
  54.2 160.0 all-gather.2
  317.4 47.5 reduce-scatter.10
  367.4 33.9 reduce-scatter.8
  403.5 33.9 reduce-scatter.6
  442.0 156.0 reduce-scatter.4

commit v4 on v3

--- a/solution.py
+++ b/solution.py
@@ -680,6 +680,130 @@
         name="scatter_whole" if pairs is None else "scatter_pairs",
     )(*operands)
     return got[0] if pairs is None else got
+
+
+def scatter_experts(parts, lefts, rights, collective_id):
+    ep_count, rows, width = parts.shape
+    flat, tall = lefts[0].shape
+    ff = rights[0].shape[1]
+    half, depth = tall // 2, flat // 3
+    plan, pieces = Plan(ep_count, False), 4
+    place = Place(lax.axis_size("grp"), ep_count)
+    left_of = [0, 0, 1]
+    hooks = (4, 5, 6, 7, 10, 11, 12, 13, 16, 17)
+    kinds, units = len(rights), 2 * len(rights)
+    steps = units * 3
+
+    def kernel(p_ref, in_ref, og_ref, pre_ref, lift_ref, mid_ref, out_ref, w0, w1, w2, acc, left, right, gone, came,
+               ls, rs, gs, cs, *scratch):
+        left_refs, right_refs, outs = (in_ref, og_ref), (pre_ref, lift_ref, mid_ref), (w0, w1, w2)
+        place.locate()
+        total = RowSum(plan, pieces, p_ref, scratch)
+        g = place.at["x"]
+        place.greet()
+
+        def fetch(kind, step):
+            chunk, slot = step % 3, step % 2
+            mine = (step >= 3 * kinds).astype(jnp.int32)
+            first = pl.multiple_of(jnp.where(mine == 1, g, 1 - g) * half, HEAD)
+            at = pl.ds(pl.multiple_of(chunk * depth, depth), depth)
+            return (pltpu.make_async_copy(left_refs[left_of[kind]].at[at, pl.ds(first, half)], left.at[slot], ls.at[slot]),
+                    pltpu.make_async_copy(right_refs[kind].at[at, :], right.at[slot], rs.at[slot]))
+
+        def per_kind(step, go):
+            for kind in range(kinds):
+                run_if((step // 3) % kinds == kind, lambda kind=kind: go(kind))
+
+        def begin(step):
+            def go(kind):
+                for copy in fetch(kind, step):
+                    copy.start()
+            per_kind(step, go)
+
+        def away(kind):
+            return send(gone.at[kind], came.at[kind], gs.at[kind], cs.at[kind], place.dev(x=place.back("x", 1)))
+
+        def meet(n):
+            q, distance = n // plan.long, plan.long - 1 - n % plan.long
+            for d in sorted({-distance, distance}):
+                total.dest(d, q)
+
+        ks = from_far(plan.wide)
+        total.start(ks)
+        begin(jnp.int32(0))
+        for k in ks[:-1]:
+            total.stage_over(k)
+
+        @pl.loop(0, steps)
+        def _(step):
+            run_if(step + 1 < steps, lambda: begin(step + 1))
+
+            def ready(kind):
+                for copy in fetch(kind, step):
+                    copy.wait()
+            per_kind(step, ready)
+            slot = step % 2
+            product = inner_left(left[slot], right[slot])
+            fresh = step % 3 == 0
+
+            @pl.when(fresh)
+            def _():
+                acc[...] = product
+
+            @pl.when(jnp.logical_not(fresh))
+            def _():
+                acc[...] += product
+
+            def done(kind):
+                @pl.when(step < 3 * kinds)
+                def _():
+                    gone[kind] = acc[...].astype(jnp.bfloat16)
+                    away(kind).start()
+
+                @pl.when(step >= 3 * kinds)
+                def _():
+                    outs[kind][...] = acc[...]
+
+            run_if(step % 3 == 2, lambda: per_kind(step, done))
+            for n, at in enumerate(hooks):
+                run_if(step == at, lambda n=n: meet(n))
+
+        for n in range(len(hooks), pieces * plan.long):
+            meet(n)
+        out_ref[...] = total.result()
+        for kind in range(kinds):
+            away(kind).wait_recv()
+            piece = 32
+
+            @pl.loop(0, half // piece)
+            def _(i, kind=kind):
+                at = pl.ds(pl.multiple_of(i * piece, piece), piece)
+                outs[kind][at, :] = outs[kind][at, :] + came[kind, at, :].astype(jnp.float32)
+
+        for kind in range(kinds):
+            away(kind).wait_send()
+        total.drain()
+
+    anywhere = pl.BlockSpec(memory_space=pl.ANY)
+    sem = lambda n: pltpu.SemaphoreType.DMA((n,))
+    outs = [jax.ShapeDtypeStruct((rows, width), parts.dtype)] + [jax.ShapeDtypeStruct((half, ff), jnp.float32)] * kinds
+    return pl.pallas_call(
+        kernel,
+        out_shape=tuple(outs),
+        in_specs=[anywhere] * 6,
+        out_specs=tuple(pl.BlockSpec(memory_space=pltpu.VMEM) for _ in outs),
+        scratch_shapes=[
+            pltpu.VMEM((half, ff), jnp.float32),
+            pltpu.VMEM((2, depth, half), jnp.bfloat16),
+            pltpu.VMEM((2, depth, ff), jnp.bfloat16),
+            pltpu.VMEM((kinds, half, ff), jnp.bfloat16),
+            pltpu.VMEM((kinds, half, ff), jnp.bfloat16),
+            sem(2), sem(2), sem(kinds), sem(kinds),
+        ] + RowSum.scratch(plan, rows, width, parts.dtype, pieces),
+        compiler_params=pltpu.CompilerParams(
+            collective_id=collective_id, has_side_effects=True, vmem_limit_bytes=VMEM_MOST),
+        name="scatter_experts",
+    )(parts, *lefts, *rights)
 
 
 def visible_bias(shape, first_key, start, first_query):
@@ -1105,20 +1229,23 @@
     back, given, flat_in, pre_grad, lift_grad, middle, result_grad = run_experts(
         places, arrived, grads_all, rank, share, expert_gate, expert_up, expert_down, capacity
     )
-    back_sum = scatter_rows(back, False, 3)
-    given, back_sum = lax.optimization_barrier((given, back_sum))
     routed = wide(lax.psum_scatter(given, "ep", scatter_dimension=0))
     group_count = lax.axis_size("grp")
-    split = width // group_count
-    own_down_grad = jnp.concatenate(
-        [low(inner_left(middle, result_grad[:, i * split : (i + 1) * split])) for i in range(group_count)], axis=0
-    )
-    own_gate_grad = low(inner_left(flat_in, pre_grad))
-    own_up_grad = low(inner_left(flat_in, lift_grad))
-    over_groups = lambda v: wide(lax.psum_scatter(v, "grp", scatter_dimension=0, tiled=True))[None]
-    gate_sum = over_groups(own_gate_grad)
-    up_sum = over_groups(own_up_grad)
-    down_sum = over_groups(own_down_grad)
+    if group_count == 2:
+        back_sum, gate_sum, up_sum, down_sum = scatter_experts(
+            back, (flat_in, result_grad), (pre_grad, lift_grad, middle), 3
+        )
+        gate_sum, up_sum, down_sum = gate_sum[None], up_sum[None], down_sum.T[None]
+    else:
+        back_sum = scatter_rows(back, False, 3)
+        split = width // group_count
+        own_down_grad = jnp.concatenate(
+            [low(inner_left(middle, result_grad[:, i * split : (i + 1) * split])) for i in range(group_count)], axis=0
+        )
+        over_groups = lambda v: wide(lax.psum_scatter(v, "grp", scatter_dimension=0, tiled=True))[None]
+        gate_sum = over_groups(low(inner_left(flat_in, pre_grad)))
+        up_sum = over_groups(low(inner_left(flat_in, lift_grad)))
+        down_sum = over_groups(own_down_grad)
 
     shared_pre = dot(ffn_low, shared_gate)
     shared_lift = dot(ffn_low, shared_up)

time: 765 us -> 746 us (0.975)
  matrix products: 67.4 us -> 31.9 us
  Pallas kernels: 626 us -> 647 us
  other arithmetic: 22.1 us -> 12.9 us
    pallas_call x1, Pallas kernels: 87.2 us -> 130 us  [scatter_experts(): pl.pallas_call(kernel, out_shape=tuple(outs), in_specs=[anywhere] * 6, ou...]
    dot_general x9 -> x5, matrix products: 50.3 us -> 10.3 us  [inner_left(): lax.dot_general(left_op, right_op, (((0,), (0,)), ((), ())), preferred_el...]
    pallas_call x2, Pallas kernels: 241 us -> 216 us  [scatter_whole(): pl.pallas_call(kernel, out_shape=tuple(out_shape), in_specs=[anywhere] *...]
    broadcast_in_dim x3 -> x0, other arithmetic: 8.53 us -> none  [local(): wide(lax.psum_scatter(v, 'grp', scatter_dimension=0, tiled=True))[None]]
    unnamed x75 -> x82, local copies, waits for them, and re-layouts: 10.2 us -> 16.1 us
  transfers between devices with their start and end apart: 5 -> 2, of which waited for: 0 -> 0; matrix products, arithmetic and copies ran while one was open for 10% -> 7% of each run, Pallas kernels for 57% -> 62%
where the time goes in v4:
time: 746 us; the launch traced here: 743 us
  Pallas kernels  647 us (87%)
  local copies, waits for them, and re-layouts  33.7 us (5%)
  matrix products  31.9 us (4%)
  between operations  17.4 us (2%)
  other arithmetic  12.9 us (2%)
    pallas_call x2, Pallas kernels, scatter_whole(): pl.pallas_call(kernel, out_shape=tuple(out_shape), in_specs=[anywhere] *...  216 us
    pallas_call x2, Pallas kernels, gather_rows(): pl.pallas_call(functools.partial(gather_kernel, plan, pieces), out_shape=...  187 us
    pallas_call x1, Pallas kernels, scatter_experts(): pl.pallas_call(kernel, out_shape=tuple(outs), in_specs=[anywhere] * 6, ou...  130 us
    pallas_call x1, Pallas kernels, run_experts(): pl.pallas_call(experts_kernel, out_shape=(shape(count, rows, side), shape...  73.4 us
    unnamed x82, local copies, waits for them, and re-layouts  16.1 us
  transfers between devices with their start and end apart: 2, of which 0 were waited for; matrix products, arithmetic and copies ran while one was open for 7% of the time, Pallas kernels for 62%

profile of v4, /device:TPU:0, one launch (start us, length us, event | category | flops | bytes accessed | tf_op | source)
XLA Modules:
  0.0 742.6 jit_solution(10897623392316365560)
XLA Ops:
  7.8 0.8 pad_maximum_fusion.cos_ref
  8.6 1.3 broadcast_in_dim.98.gain_ref
  10.6 8.7 %project.1 = (bf16[256,1280]{1,0:T(8,128)(2,1)}, bf16[256,1280]{1,0:T(8,128)(2,1)}, bf16[256,2560]{1,0:T(8,128)(2,1)}) custom-call(bf16[256,1280]{1,0:T(8,128)(2,1)} %bitcast.92, f32[1,1280]{1,0:T(1,128)} %broadcast_in_dim.98.gain_ref, f32[256,128]{1,0:T(8,128)} %pad_maximum_fusion.cos_ref, f32[256,128]{1,0:T(8,128)} %pad_maximum_fusion.1.sin_ref, ...), custom_call_target="tpu_custom_call" | custom-call | flops 2516582400 | bytes 9830400 | tf_op jit(solution)/shard_map/project/pallas_call | solution.py:849
  19.3 34.8 %gather_rows.2.kv_ref = bf16[16,256,2560]{2,1,0:T(8,128)(2,1)} custom-call(bf16[256,2560]{1,0:T(8,128)(2,1)} %get-tuple-element.45.x_ref), custom_call_target="tpu_custom_call" | custom-call | tf_op jit(solution)/shard_map/gather_rows/pallas_call | solution.py:233
  58.3 7.9 %attend.1 = (f32[10,128,256]{2,1,0:T(8,128)}, bf16[256,1280]{1,0:T(8,128)(2,1)}, f32[10,1,256]{2,1,0:T(1,128)}) custom-call(s32[2]{0:T(128)} %pad_add_fusion.info, bf16[256,1280]{1,0:T(8,128)(2,1)} %get-tuple-element.44.q_ref, s32[1,256]{1,0:T(1,128)} %bitcast.97, bf16[16,256,2560]{2,1,0:T(8,128)(2,1)} %gather_rows.2.kv_ref), custom_call_target="tpu_custom_call" | custom-call | flops 3019898880 | bytes 11796480 | tf_op jit(solution)/shard_map/attend/pallas_call | solution.py:907
  66.3 4.0 multiply_reduce_fusion.5
  70.3 1.0 copy-done.3
  72.1 0.8 subtract_convert_fusion
  72.9 1.0 concatenate.15.x_ref
  74.0 152.4 %gather_rows.3.x_ref = bf16[16,256,1408]{2,1,0:T(8,128)(2,1)} custom-call(bf16[256,1408]{1,0:T(8,128)(2,1)} %concatenate.15.x_ref), custom_call_target="tpu_custom_call" | custom-call | tf_op jit(solution)/shard_map/gather_rows/pallas_call | solution.py:233
  226.4 2.5 select_reduce_fusion
  229.7 2.0 copy.63.rank_col
  232.9 73.4 %run_experts.1 = (bf16[16,256,1408]{2,1,0:T(8,128)(2,1)}, bf16[16,256,1280]{2,1,0:T(8,128)(2,1)}, bf16[3072,1280]{1,0:T(8,128)(2,1)}, bf16[3072,896]{1,0:T(8,128...) custom-call(s32[2]{0:T(128)} %pad_add_fusion.1.where_ref, ...), custom_call_target="tpu_custom_call" | custom-call | flops 56371445760 | bytes 62914560 | tf_op jit(solution)/shard_map/run_experts/pallas_call | solution.py:1134
  306.3 1.0 copy-done.1
  307.4 0.8 copy-done.10
  308.2 0.8 fusion.23
  309.0 0.8 copy-done.12
  309.8 0.8 fusion.24
  310.9 0.8 copy-done.13
  311.7 1.9 multiply_convert_fusion.1
  313.6 0.8 copy-done.18
  314.3 0.8 fusion
  315.1 3.4 copy.64
  318.5 3.3 convolution_convert_fusion.3
  321.8 2.3 convolution_convert_fusion.2
  324.5 2.0 fusion.25
  326.5 129.9 %scatter_experts.1 = (bf16[256,1408]{1,0:T(8,128)(2,1)}, f32[640,896]{1,0:T(8,128)}, f32[640,896]{1,0:T(8,128)}, f32[640,896]{1,0:T(8,128)}) custom-call(bf16[16,256,1408]{2,1,0:T(8,128)(2,1)} %get-tuple-element.50.p_ref, bf16[3072,1280]{1,0:T(8,128)(2,1)} %get-tuple-element.51.in_ref, bf16[3072,1280]{1,0:T(8,128)(2,1)} %get-tuple-element.52.og_ref, ...), custom_call_target="tpu_custom_call" | custom-call | tf_op jit(solution)/shard_map/scatter_experts/pallas_call | solution.py:790
  456.4 1.1 multiply_reduce_fusion.6
  457.6 3.3 fusion.1
  461.0 2.3 multiply_reduce_fusion.2
  465.0 2.7 convolution_convert_fusion
  468.3 1.9 convolution_convert_fusion.4.g_ref
  470.2 9.1 %attend_back.1 = (bf16[16,256,2560]{2,1,0:T(8,128)(2,1)}, bf16[256,1280]{1,0:T(8,128)(2,1)}) custom-call(s32[2]{0:T(128)} %pad_add_fusion.info, bf16[256,1280]{1,0:T(8,128)(2,1)} %get-tuple-element.44.q_ref, bf16[256,1280]{1,0:T(8,128)(2,1)} %convolution_convert_fusion.4.g_ref, f32[10,128,256]{2,1,0:T(8,128)} %get-tuple-element.58.mixed_ref, ...), custom_call_target="tpu_custom_call" | custom-call | flops 7549747200 | bytes 23592960 | tf_op jit(solution)/shard_map/attend_back/pallas_call | solution.py:986
  479.3 145.6 %scatter_pairs.1 = (f32[40,3968]{1,0:T(8,128)}, bf16[256,2560]{1,0:T(8,128)(2,1)}) custom-call(bf16[32,40,896]{2,1,0:T(8,128)(2,1)} %bitcast.82, bf16[32,40,896]{2,1,0:T(8,128)(2,1)} %bitcast.83, bf16[32,40,896]{2,1,0:T(8,128)(2,1)} %bitcast.81, bf16[32,40,1280]{2,1,0:T(8,128)(2,1)} %bitcast.80, bf16[16,256,2560]{2,1,0:T(8,128)(2,1)} %get-tuple-element.61.refs_4_), custom_call_target="tpu_custom_call" | custom-call | tf_op jit(solution)/shard_map/scatter_pairs/pallas_call | solution.py:672
  624.9 1.6 slice.66
  626.5 3.2 copy.67
  629.8 0.8 slice_bitcast_fusion
  630.5 1.2 convolution_convert_fusion.5
  631.8 14.4 %finish.1 = (bf16[1280,1280]{1,0:T(8,128)(2,1)}, bf16[1280,1280]{1,0:T(8,128)(2,1)}, bf16[1280,1280]{1,0:T(8,128)(2,1)}, bf16[256,1280]{1,0:T(8,128)(2,1)}, f32[1,1280]{1,0:T(1,128)}) custom-call(bf16[256,1280]{1,0:T(8,128)(2,1)} %bitcast.93, f32[1,1280]{1,0:T(1,128)} %broadcast_in_dim.98.gain_ref, f32[256,1280]{1,0:T(8,128)} %copy-done.8, ...), custom_call_target="tpu_custom_call" | custom-call | flops 5033164800 | bytes 19660800 | tf_op jit(solution)/shard_map/finish/pallas_call | solution.py:1060
  647.0 4.1 multiply_reduce_fusion
  651.0 2.1 maximum_convert_fusion
  653.5 0.8 pad.5.clone
  654.3 70.4 %scatter_whole.1 = f32[40,3968]{1,0:T(8,128)} custom-call(bf16[32,40,1280]{2,1,0:T(8,128)(2,1)} %bitcast.85, bf16[32,40,1280]{2,1,0:T(8,128)(2,1)} %bitcast.86, bf16[32,40,1280]{2,1,0:T(8,128)(2,1)} %bitcast.87, bf16[32,40,128]{2,1,0:T(8,128)(2,1)} %bitcast.91), custom_call_target="tpu_custom_call" | custom-call | tf_op jit(solution)/shard_map/scatter_whole/pallas_call | solution.py:672
  724.7 2.0 fusion.21
  727.4 1.5 slice_reduce_fusion
  728.9 1.3 sqrt_bitcast_fusion
  730.8 3.3 copy.78
  734.2 1.4 copy.79
  (106 shorter events, 11.3 us)
Async XLA Ops:
  7.2 225.7 %all-gather.3.cloned.1.call-start = ((), (), s32[]{:S(2)}) async-start(), calls=%async_computation.2 | async-start | bytes 11141120 | tf_op jit(solution)/shard_map/all_gather | solution.py:1201
  19.3 34.9 %copy-start.37 = (s32[1,4]{1,0:T(1,128)S(1)}, s32[1,4]{1,0:T(1,128)}, u32[]{:S(2)}) copy-start(s32[1,4]{1,0:T(1,128)} %param.18) | copy-start | bytes 52
  19.3 38.2 %copy-start.32 = (s32[1,256,7]{1,0,2:T(1,128)S(1)}, s32[1,256,7]{1,0,2:T(1,128)}, u32[]{:S(2)}) copy-start(s32[1,256,7]{1,0,2:T(1,128)} %param.19) | copy-start | bytes 21508
  54.1 592.9 %reduce-scatter.2.cloned.1.call-start = ((), (), s32[]{:S(2)}) async-start(), calls=%async_computation.1 | async-start | bytes 11141120 | tf_op jit(solution)/shard_map/reduce_scatter | solution.py:1232
  54.4 3.9 copy-start.33
  58.3 7.9 %copy-start.21 = (bf16[1,256,1280]{2,1,0:T(8,128)(2,1)S(1)}, bf16[1,256,1280]{2,1,0:T(8,128)(2,1)}, u32[]{:S(2)}) copy-start(bf16[1,256,1280]{2,1,0:T(8,128)(2,1)} %param.17) | copy-start | bytes 1966084
  66.3 5.0 copy-start.25
  66.3 5.2 copy-start.23
  70.3 1.1 copy-start.3
  70.3 2.7 copy-start.34
  70.3 2.6 copy-start.28
  71.5 154.9 %copy-start = (bf16[256,1280]{1,0:T(8,128)(2,1)}, bf16[256,1280]{1,0:T(8,128)(2,1)S(1)}, u32[]{:S(2)}) copy-start(bf16[256,1280]{1,0:T(8,128)(2,1)S(1)} %multiply_convert_fusion) | copy-start | bytes 1966084
  306.3 1.1 copy-start.1
  306.3 1.9 copy-start.10
  308.2 1.6 copy-start.12
  309.8 1.1 copy-start.6
  309.8 1.9 copy-start.13
  313.6 0.8 copy-start.18
  313.6 8.3 %copy-start.17 = (bf16[256,896]{1,0:T(8,128)(2,1)}, bf16[256,896]{1,0:T(8,128)(2,1)S(1)}, u32[]{:S(2)}) copy-start(bf16[256,896]{1,0:T(8,128)(2,1)S(1)} %get-tuple-element.146) | copy-start | bytes 1376260
  321.8 2.3 copy-start.11
  321.8 2.7 copy-start.20
  457.5 3.4 copy-start.30
  457.5 3.4 copy-start.4
  457.5 3.4 copy-start.15
  457.6 3.4 copy-start.24
  457.6 3.4 copy-start.26
  457.6 3.4 copy-start.29
  461.0 2.9 copy-start.35
  461.0 2.9 copy-start.7
  463.9 1.1 copy-start.14
  465.0 2.7 copy-start.8
  465.0 3.3 copy-start.36
  626.5 3.2 copy-start.22
  626.5 4.0 copy-start.2
  626.5 4.0 copy-start.16
  626.5 4.0 copy-start.31
  631.8 15.2 %copy-start.5 = (f32[256,1280]{1,0:T(8,128)S(1)}, f32[256,1280]{1,0:T(8,128)}, u32[]{:S(2)}) copy-start(f32[256,1280]{1,0:T(8,128)} %copy-done.3) | copy-start | bytes 3932164
  631.8 15.2 %copy-start.19 = (bf16[256,896]{1,0:T(8,128)(2,1)S(1)}, bf16[256,896]{1,0:T(8,128)(2,1)}, u32[]{:S(2)}) copy-start(bf16[256,896]{1,0:T(8,128)(2,1)} %copy-done.18) | copy-start | bytes 1376260
  646.9 6.2 copy-start.27
  730.8 3.3 copy-start.9
Sparse Core Ops, SparseCore 0:
  54.2 161.2 all-gather.2
  306.5 158.9 reduce-scatter.1

commit v5 on v4

--- a/solution.py
+++ b/solution.py
@@ -290,7 +290,7 @@
         n, wide = plan.planes(), plan.wide
         blocks = lambda *lead: pltpu.VMEM(lead + (rows, width), dtype)
         sem = lambda *lead: pltpu.SemaphoreType.DMA(lead + (pieces,))
-        return [blocks(n, wide), blocks(n, wide), blocks(n, wide - 1), blocks(n), blocks(n),
+        return [blocks(n, wide), blocks(n, wide), blocks(n, wide - 1), blocks(n), blocks(1 if plan.window else n),
                 sem(n, wide), sem(n, wide), sem(n, wide), sem(n, wide), sem(n), sem(n), sem(n), sem(n, wide)]
 
     def __init__(self, plan, pieces, p_ref, scratch):
@@ -298,7 +298,8 @@
         (self.held, self.rcb, self.rbb, self.r_hi, self.r_lo,
          self.sc, self.rc, self.sb, self.rb, self.sa, self.rhi, self.rlo, self.ld) = scratch
         self.a, self.b, self.c = plan.place()
-        self.rows = p_ref.shape[1] // pieces
+        self.ready = len(p_ref.shape) == 4
+        self.rows = p_ref.shape[-2] // pieces
         self.order = sorted(plan.steps, key=lambda d: -abs(d))
 
     def part(self, q):
@@ -319,8 +320,9 @@
     def cross(self, d, k, q):
         p, i, b0, c = self.plan, self.plan.plane(self.a, d), self.source(k), self.c
         real = p.inside(self.a - d)
+        at = (i, k) if self.ready else (p.slot(self.a - d, b0, 1 - c),)
         return (both(real, p.need(d, self.b, c, b0, 1 - c)), lambda: send(
-            self.p_ref.at[p.slot(self.a - d, b0, 1 - c), self.part(q)], self.rcb.at[i, k, self.part(q)],
+            self.p_ref.at[at + (self.part(q),)], self.rcb.at[i, k, self.part(q)],
             self.sc.at[i, k, q], self.rc.at[i, k, q], self.dev(self.a, self.b, 1 - c)),
             both(real, p.need(d, self.b, 1 - c, b0, c)))
 
@@ -348,8 +350,9 @@
 
     def first(self, d, k, q):
         i = self.plan.plane(self.a, d)
-        cond, go = self.load(d, k, q)
-        run_if(cond, lambda: go().wait())
+        if not self.ready:
+            cond, go = self.load(d, k, q)
+            run_if(cond, lambda: go().wait())
         _, come_go, come = self.cross(d, k, q)
 
         def take():
@@ -566,96 +569,64 @@
                     self.hop(2, key).wait_send()
 
 
-def scatter_whole(parts, collective_id, pairs=None):
+def pieces_of(sources, low, high):
+    pieces, first = [], 0
+    for ref in sources:
+        begin, end = max(low, first), min(high, first + ref.shape[2])
+        if begin < end:
+            pieces.append((ref, begin - first, begin - low, end - begin))
+        first += ref.shape[2]
+    return pieces
+
+
+def scatter_whole(parts, collective_id):
     rows = parts[0].shape[1]
     width = sum(part.shape[2] for part in parts)
     groups, ep_count = lax.axis_size("grp"), lax.axis_size("ep")
     place = Place(groups, ep_count)
     tiles = width // HEAD
     cuts = [0, tiles // 2 * HEAD, width]
-    orders = ["xba", "xba" if pairs is not None else "bxa"]
+    orders = ["xba", "bxa"]
 
     def kernel(*refs):
         sources, refs = refs[: len(parts)], refs[len(parts) :]
-        if pairs is not None:
-            pair_ref, refs = refs[0], refs[1:]
         out_ref, refs = refs[0], refs[1:]
-        if pairs is not None:
-            pair_out, refs = refs[0], refs[1:]
         place.locate()
         sums = []
         for n, axes in enumerate(orders):
-            low, high, first, pieces = cuts[n], cuts[n + 1], 0, []
-            for ref in sources:
-                begin, end = max(low, first), min(high, first + ref.shape[2])
-                if begin < end:
-                    pieces.append((ref, begin - first, begin - low, end - begin))
-                first += ref.shape[2]
+            pieces = pieces_of(sources, cuts[n], cuts[n + 1])
             sums.append(WholeSum(place, axes, pieces, refs[:14]))
             refs = refs[14:]
         outs = [out_ref.at[:, pl.ds(cuts[n], cuts[n + 1] - cuts[n])] for n in range(len(orders))]
         place.greet()
-        if pairs is None:
-            couples = [sums[n : n + 2] for n in range(0, len(sums), 2)]
+        couples = [sums[n : n + 2] for n in range(0, len(sums), 2)]
+        for couple in couples:
+            for i in range(max(s.n1 for s in couple)):
+                for s in couple:
+                    if i < s.n1:
+                        s.start(i)
+
+        def core(couple):
+            for i in range(max(s.n1 for s in couple)):
+                for s in couple:
+                    if i < s.n1:
+                        s.stage_core(i)
+
+        def one(couple):
+            for i in range(max(s.n2 for s in couple)):
+                for s in couple:
+                    if i < s.n2:
+                        s.stage_one(from_far(s.n2)[i])
+
+        def two(couple):
+            for s in couple:
+                s.stage_two()
+
+        for stage in (core, one, two):
             for couple in couples:
-                for i in range(max(s.n1 for s in couple)):
-                    for s in couple:
-                        if i < s.n1:
-                            s.start(i)
-
-            def core(couple):
-                for i in range(max(s.n1 for s in couple)):
-                    for s in couple:
-                        if i < s.n1:
-                            s.stage_core(i)
-
-            def one(couple):
-                for i in range(max(s.n2 for s in couple)):
-                    for s in couple:
-                        if i < s.n2:
-                            s.stage_one(from_far(s.n2)[i])
-
-            def two(couple):
-                for s in couple:
-                    s.stage_two()
-
-            for stage in (core, one, two):
-                for couple in couples:
-                    stage(couple)
-            for s, out in zip(sums, outs):
-                s.stage_three(out)
-        else:
-            total = RowSum(plan, 4, pair_ref, refs)
-            ks = from_far(plan.wide)
-            for one in sums:
-                for i in range(one.n1 - 1):
-                    one.start(i)
-            total.start(ks[:-1])
-            for one in sums:
-                one.start(one.n1 - 1)
-            total.start(ks[-1:])
-            for one in sums:
-                for i in range(one.n1 - 1):
-                    one.stage_core(i)
-            for k in ks[:-1]:
-                total.stage_over(k)
-            for one in sums:
-                one.stage_core(one.n1 - 1)
-            total.stage_dests(0, 2)
-            for k2 in from_far(sums[0].n2):
-                sums[0].stage_one(k2)
-            total.stage_dests(2, 3)
-            sums[0].stage_two()
-            for one in sums[1:]:
-                for k2 in from_far(one.n2):
-                    one.stage_one(k2)
-            total.stage_dests(3, 4)
-            for one in sums[1:]:
-                one.stage_two()
-            pair_out[...] = total.result()
-            for one, out in zip(sums, outs):
-                one.stage_three(out)
-            total.drain()
+                stage(couple)
+        for s, out in zip(sums, outs):
+            s.stage_three(out)
         for s in sums:
             s.drain()
 
@@ -664,11 +635,6 @@
     scratch = []
     for n, axes in enumerate(orders):
         scratch += WholeSum.scratch(place.sizes, axes, rows, cuts[n + 1] - cuts[n], parts[0].dtype, len(parts))
-    if pairs is not None:
-        plan = Plan(ep_count, True)
-        operands.append(pairs)
-        out_shape.append(jax.ShapeDtypeStruct(pairs.shape[1:], pairs.dtype))
-        scratch += RowSum.scratch(plan, pairs.shape[1], pairs.shape[2], pairs.dtype, 4)
     got = pl.pallas_call(
         kernel,
         out_shape=tuple(out_shape),
@@ -677,9 +643,9 @@
         scratch_shapes=scratch,
         compiler_params=pltpu.CompilerParams(
             collective_id=collective_id, has_side_effects=True, vmem_limit_bytes=VMEM_MOST),
-        name="scatter_whole" if pairs is None else "scatter_pairs",
+        name="scatter_whole",
     )(*operands)
-    return got[0] if pairs is None else got
+    return got[0]
 
 
 def scatter_experts(parts, lefts, rights, collective_id):
@@ -1149,6 +1115,161 @@
     )(places, arrived, grads, rank[:, None, :], rank[:, :, None], share[:, None, :], gate, up, down)
 
 
+def attend_back_sum(queries, grads, mixed, start, total, cosine, sine, pairs, parts, collective_id):
+    rows, width = queries.shape
+    ep_count = pairs.shape[0]
+    part_rows, part_width = parts[0].shape[1], sum(part.shape[2] for part in parts)
+    plan, pieces = Plan(ep_count, True), 4
+    place = Place(lax.axis_size("grp"), ep_count)
+    n, wide = plan.planes(), plan.wide
+    cuts = [0, part_width // HEAD // 2 * HEAD, part_width]
+
+    def kernel(q_ref, g_ref, mixed_ref, start_ref, total_ref, cos_ref, sin_ref, pair_ref, *refs):
+        sources, refs = refs[: len(parts)], refs[len(parts) :]
+        out_ref, pair_out, dq_ref, bias, acc, term, kv, staged, kv_sem = refs[:9]
+        refs = refs[9:]
+        place.locate()
+        sums = []
+        for i in range(2):
+            sums.append(WholeSum(place, "xba", pieces_of(sources, cuts[i], cuts[i + 1]), refs[:14]))
+            refs = refs[14:]
+        sum_rows = RowSum(plan, pieces, staged, refs)
+        a, b, c = sum_rows.a, sum_rows.b, sum_rows.c
+        me = plan.slot(a, b, c)
+        order, ks = sum_rows.order, from_far(wide)
+        turns = [(k, d) for k in ks for d in order]
+
+        def block(turn, other):
+            k, d = turns[turn]
+            b0, c0 = sum_rows.source(k), jnp.where(other, 1 - c, c)
+            there = both(plan.inside(a - d), plan.need(d, b, c, b0, c0))
+            return there, plan.slot(a - d, b0, c0)
+
+        def fetch(turn, other):
+            there, slot = block(turn, other)
+            held = jnp.where(other, 0, 1)
+            return there, lambda: pltpu.make_async_copy(pair_ref.at[slot], kv.at[held], kv_sem.at[held])
+
+        def begin(turn, other):
+            there, go = fetch(turn, other)
+            run_if(there, lambda: go().start())
+
+        def compute(turn, other, target):
+            there, slot = block(turn, other)
+            held = 0 if other else 1
+
+            def work():
+                fetch(turn, other)[1]().wait()
+                bias[...] = visible_bias((rows, rows), slot * rows, start_ref[...], me * rows)
+
+                @pl.loop(0, HEADS, unroll=2)
+                def _(h):
+                    early, late, at = lanes(2 * h * HEAD), lanes((2 * h + 1) * HEAD), lanes(h * HEAD)
+                    keys, values = kv[held, :, early], kv[held, :, late]
+                    own, grad = q_ref[:, at], g_ref[:, at]
+                    probs = jnp.exp(inner_right(keys, own) + bias[...] - total_ref[h])
+                    score_grad = (probs * (inner_right(values, grad) - term[h])).astype(jnp.bfloat16)
+                    target[:, late] = jnp.dot(
+                        probs.astype(jnp.bfloat16), grad, preferred_element_type=jnp.float32
+                    ).astype(jnp.bfloat16)
+                    target[:, early] = jnp.dot(
+                        score_grad, own, preferred_element_type=jnp.float32
+                    ).astype(jnp.bfloat16)
+                    acc[h] += inner_left(keys, score_grad)
+
+            run_if(there, work)
+
+        def turn_of(turn):
+            k, d = turns[turn]
+            i = plan.plane(a, d)
+            compute(turn, True, staged.at[i, k])
+            if turn + 1 < len(turns):
+                begin(turn + 1, True)
+            cond = sum_rows.cross(d, k, 0)[0]
+            for q in range(pieces):
+                run_if(cond, lambda q=q: sum_rows.cross(d, k, q)[1]().start())
+            compute(turn, False, sum_rows.held.at[i, k])
+            if turn + 1 < len(turns):
+                begin(turn + 1, False)
+
+        def pass_on(turn):
+            k, d = turns[turn]
+
+            @pl.loop(0, pieces)
+            def _(q):
+                sum_rows.first(d, k, q)
+                cond, go = sum_rows.over(d, k, q)
+                run_if(cond, lambda: go().start())
+
+        begin(0, True)
+        begin(0, False)
+        acc[...] = jnp.zeros_like(acc)
+        for h in range(HEADS):
+            grad = g_ref[:, h * HEAD : (h + 1) * HEAD].astype(jnp.float32).T
+            term[h] = jnp.sum(grad * mixed_ref[h], axis=0, keepdims=True)
+        place.greet()
+        far = (wide - 1) * len(order)
+        for one in sums:
+            for i in range(one.n1 - 1):
+                one.start(i)
+        turn_of(0)
+        for one in sums:
+            for i in range(one.n1 - 1):
+                one.stage_core(i)
+        for one in sums:
+            one.start(one.n1 - 1)
+        for turn in range(1, len(turns)):
+            turn_of(turn)
+            if turn <= far:
+                pass_on(turn - 1)
+            if turn == far:
+                for one in sums:
+                    one.stage_core(one.n1 - 1)
+        for h in range(HEADS):
+            back = turned(acc[h].T * HEAD ** (-0.5), cos_ref[...], -sin_ref[...])
+            dq_ref[:, h * HEAD : (h + 1) * HEAD] = back.astype(jnp.bfloat16)
+        sum_rows.stage_dests(0, 2)
+        for k2 in from_far(sums[0].n2):
+            sums[0].stage_one(k2)
+        sum_rows.stage_dests(2, 3)
+        sums[0].stage_two()
+        for k2 in from_far(sums[1].n2):
+            sums[1].stage_one(k2)
+        sum_rows.stage_dests(3, 4)
+        sums[1].stage_two()
+        pair_out[...] = sum_rows.result()
+        for i, one in enumerate(sums):
+            one.stage_three(out_ref.at[:, pl.ds(cuts[i], cuts[i + 1] - cuts[i])])
+        sum_rows.drain()
+        for one in sums:
+            one.drain()
+
+    anywhere, near = pl.BlockSpec(memory_space=pl.ANY), pl.BlockSpec(memory_space=pltpu.VMEM)
+    scratch = [
+        pltpu.VMEM((rows, rows), jnp.float32),
+        pltpu.VMEM((HEADS, HEAD, rows), jnp.float32),
+        pltpu.VMEM((HEADS, 1, rows), jnp.float32),
+        pltpu.VMEM((2, rows, 2 * width), jnp.bfloat16),
+        pltpu.VMEM((n, wide, rows, 2 * width), jnp.bfloat16),
+        pltpu.SemaphoreType.DMA((2,)),
+    ]
+    for i in range(2):
+        scratch += WholeSum.scratch(place.sizes, "xba", part_rows, cuts[i + 1] - cuts[i], parts[0].dtype, len(parts))
+    scratch += RowSum.scratch(plan, rows, 2 * width, pairs.dtype, pieces)
+    return pl.pallas_call(
+        kernel,
+        out_shape=(jax.ShapeDtypeStruct((part_rows, part_width), jnp.float32),
+                   jax.ShapeDtypeStruct((rows, 2 * width), pairs.dtype),
+                   jax.ShapeDtypeStruct((rows, width), jnp.bfloat16)),
+        in_specs=[near] * 7 + [anywhere] * (1 + len(parts)),
+        out_specs=(near, near, near),
+        scratch_shapes=scratch,
+        compiler_params=pltpu.CompilerParams(
+            collective_id=collective_id, has_side_effects=True, vmem_limit_bytes=VMEM_MOST),
+        name="attend_back_sum",
+    )(queries, grads, mixed, start, total, cosine, sine, pairs, *parts)
+
+
 def local(
     tokens,
     doc_lengths,
@@ -1270,9 +1391,6 @@
     residual_grad = grad_out + residual_part
     mixer_grad_low = low(residual_grad)
     mixed_grad = low(inner_right(mixer_grad_low, output_weight))
-    pair_parts, query_lin_grad = attend_back(
-        info, queries, mixed_grad, mixed, start[None, :], log_total, cosine, sine, pairs
-    )
     by_device = lambda v: low(v).reshape(device_count, width // device_count, -1)
     early = [
         by_device(part)
@@ -1280,10 +1398,15 @@
                      inner_left(grad_low, shared_mid), inner_left(mixed_low, mixer_grad_low))
     ]
     if ep_count > 16:
+        pair_parts, query_lin_grad = attend_back(
+            info, queries, mixed_grad, mixed, start[None, :], log_total, cosine, sine, pairs
+        )
         pair_grads = scatter_rows(pair_parts, True, 4)
         early_sum = scatter_whole(early, 5)
     else:
-        early_sum, pair_grads = scatter_whole(early, 5, pair_parts)
+        early_sum, pair_grads, query_lin_grad = attend_back_sum(
+            queries, mixed_grad, mixed, start[None, :], log_total, cosine, sine, pairs, early, 5
+        )
 
     query_part, key_part, value_part, tokens_grad, mixer_gain_grad = finish(
         tokens[0], mixer_gain, residual_grad, hidden_low, query_lin_grad, pair_grads, cosine, sine,

time: 746 us -> 743 us (level)
    pallas_call x2 -> x1, Pallas kernels: 216 us -> 74.5 us  [scatter_whole(): pl.pallas_call(kernel, out_shape=tuple(out_shape), in_specs=[anywhere] *...]
    pallas_call x1, Pallas kernels: 9.11 us -> 145 us  [attend_back_sum(): pl.pallas_call(kernel, out_shape=(jax.ShapeDtypeStruct((part_rows, part_w...]
    pallas_call x1, Pallas kernels: 130 us -> 122 us  [scatter_experts(): pl.pallas_call(kernel, out_shape=tuple(outs), in_specs=[anywhere] * 6, ou...]
  transfers between devices with their start and end apart: 2 -> 2, of which waited for: 0 -> 0; matrix products, arithmetic and copies ran while one was open for 7% -> 7% of each run, Pallas kernels for 62% -> 61%
where the time goes in v5:
time: 743 us; the launch traced here: 736 us
  Pallas kernels  640 us (86%)
  local copies, waits for them, and re-layouts  34.1 us (5%)
  matrix products  32.1 us (4%)
  between operations  17.3 us (2%)
  other arithmetic  12.8 us (2%)
    pallas_call x2, Pallas kernels, gather_rows(): pl.pallas_call(functools.partial(gather_kernel, plan, pieces), out_shape=...  194 us
    pallas_call x1, Pallas kernels, attend_back_sum(): pl.pallas_call(kernel, out_shape=(jax.ShapeDtypeStruct((part_rows, part_w...  145 us
    pallas_call x1, Pallas kernels, scatter_experts(): pl.pallas_call(kernel, out_shape=tuple(outs), in_specs=[anywhere] * 6, ou...  122 us
    pallas_call x1, Pallas kernels, scatter_whole(): pl.pallas_call(kernel, out_shape=tuple(out_shape), in_specs=[anywhere] *...  74.5 us
    pallas_call x1, Pallas kernels, run_experts(): pl.pallas_call(experts_kernel, out_shape=(shape(count, rows, side), shape...  73.4 us
    unnamed x82, local copies, waits for them, and re-layouts  16.4 us
  transfers between devices with their start and end apart: 2, of which 0 were waited for; matrix products, arithmetic and copies ran while one was open for 7% of the time, Pallas kernels for 61%

profile of v5, /device:TPU:0, one launch (start us, length us, event | category | flops | bytes accessed | tf_op | source)
XLA Modules:
  0.0 735.9 jit_solution(7811549409425054945)
XLA Ops:
  7.8 0.8 pad_maximum_fusion.cos_ref
  8.6 1.3 broadcast_in_dim.98.gain_ref
  9.9 0.8 pad_maximum_fusion.1.sin_ref
  10.6 8.7 %project.1 = (bf16[256,1280]{1,0:T(8,128)(2,1)}, bf16[256,1280]{1,0:T(8,128)(2,1)}, bf16[256,2560]{1,0:T(8,128)(2,1)}) custom-call(bf16[256,1280]{1,0:T(8,128)(2,1)} %bitcast.92, f32[1,1280]{1,0:T(1,128)} %broadcast_in_dim.98.gain_ref, f32[256,128]{1,0:T(8,128)} %pad_maximum_fusion.cos_ref, f32[256,128]{1,0:T(8,128)} %pad_maximum_fusion.1.sin_ref, ...), custom_call_target="tpu_custom_call" | custom-call | flops 2516582400 | bytes 9830400 | tf_op jit(solution)/shard_map/project/pallas_call | solution.py:815
  19.3 34.8 %gather_rows.2.kv_ref.pair_ref = bf16[16,256,2560]{2,1,0:T(8,128)(2,1)} custom-call(bf16[256,2560]{1,0:T(8,128)(2,1)} %get-tuple-element.44.x_ref), custom_call_target="tpu_custom_call" | custom-call | tf_op jit(solution)/shard_map/gather_rows/pallas_call | solution.py:233
  58.3 7.9 %attend.1 = (f32[10,128,256]{2,1,0:T(8,128)}, bf16[256,1280]{1,0:T(8,128)(2,1)}, f32[10,1,256]{2,1,0:T(1,128)}) custom-call(s32[2]{0:T(128)} %pad_add_fusion.info, bf16[256,1280]{1,0:T(8,128)(2,1)} %get-tuple-element.43.q_ref, s32[1,256]{1,0:T(1,128)} %bitcast.97, bf16[16,256,2560]{2,1,0:T(8,128)(2,1)} %gather_rows.2.kv_ref.pair_ref), custom_call_target="tpu_custom_call" | custom-call | flops 3019898880 | bytes 11796480 | tf_op jit(solution)/shard_map/attend/pallas_call | solution.py:873
  66.2 3.9 multiply_reduce_fusion.5
  70.2 1.0 copy-done.3
  72.0 0.8 subtract_convert_fusion
  72.8 1.0 concatenate.15.x_ref
  73.8 158.8 %gather_rows.3.x_ref = bf16[16,256,1408]{2,1,0:T(8,128)(2,1)} custom-call(bf16[256,1408]{1,0:T(8,128)(2,1)} %concatenate.15.x_ref), custom_call_target="tpu_custom_call" | custom-call | tf_op jit(solution)/shard_map/gather_rows/pallas_call | solution.py:233
  232.7 2.5 select_reduce_fusion
  236.0 2.0 copy.63.rank_col
  239.2 73.4 %run_experts.1 = (bf16[16,256,1408]{2,1,0:T(8,128)(2,1)}, bf16[16,256,1280]{2,1,0:T(8,128)(2,1)}, bf16[3072,1280]{1,0:T(8,128)(2,1)}, bf16[3072,896]{1,0:T(8,128...) custom-call(s32[2]{0:T(128)} %pad_add_fusion.1.where_ref, ...), custom_call_target="tpu_custom_call" | custom-call | flops 56371445760 | bytes 62914560 | tf_op jit(solution)/shard_map/run_experts/pallas_call | solution.py:1100
  312.7 1.0 copy-done.1
  313.7 0.8 copy-done.10
  314.5 0.8 fusion.23
  315.3 0.8 copy-done.12
  316.1 0.8 fusion.24
  317.3 1.2 copy-done.13
  318.4 1.9 multiply_convert_fusion.1
  320.3 0.8 copy-done.18
  321.1 0.8 fusion
  321.9 3.4 copy.64
  325.4 3.4 convolution_convert_fusion.3
  328.7 2.3 convolution_convert_fusion.2
  331.3 2.0 fusion.25
  333.3 121.8 %scatter_experts.1 = (bf16[256,1408]{1,0:T(8,128)(2,1)}, f32[640,896]{1,0:T(8,128)}, f32[640,896]{1,0:T(8,128)}, f32[640,896]{1,0:T(8,128)}) custom-call(bf16[16,256,1408]{2,1,0:T(8,128)(2,1)} %get-tuple-element.49.p_ref, bf16[3072,1280]{1,0:T(8,128)(2,1)} %get-tuple-element.50.in_ref, bf16[3072,1280]{1,0:T(8,128)(2,1)} %get-tuple-element.51.og_ref, ...), custom_call_target="tpu_custom_call" | custom-call | tf_op jit(solution)/shard_map/scatter_experts/pallas_call | solution.py:756
  455.1 1.1 multiply_reduce_fusion.6
  456.3 3.3 fusion.1
  459.7 2.3 multiply_reduce_fusion.2
  463.7 2.8 convolution_convert_fusion
  467.0 1.9 convolution_convert_fusion.4.g_ref
  468.9 145.3 %attend_back_sum.1 = (f32[40,3968]{1,0:T(8,128)}, bf16[256,2560]{1,0:T(8,128)(2,1)}, bf16[256,1280]{1,0:T(8,128)(2,1)}) custom-call(bf16[256,1280]{1,0:T(8,128)(2,1)} %get-tuple-element.43.q_ref, bf16[256,1280]{1,0:T(8,128)(2,1)} %convolution_convert_fusion.4.g_ref, f32[10,128,256]{2,1,0:T(8,128)} %get-tuple-element.57.mixed_ref, s32[1,256]{1,0:T(1,128)} %bitcast.98, ...), custom_call_target="tpu_custom_call" | custom-call | tf_op jit(solution)/shard_map/attend_back_sum/pallas_call | solution.py:1259
  614.2 1.6 slice.66
  615.9 3.2 copy.67
  619.1 0.8 slice_bitcast_fusion
  619.8 1.2 convolution_convert_fusion.5
  621.1 14.4 %finish.1 = (bf16[1280,1280]{1,0:T(8,128)(2,1)}, bf16[1280,1280]{1,0:T(8,128)(2,1)}, bf16[1280,1280]{1,0:T(8,128)(2,1)}, bf16[256,1280]{1,0:T(8,128)(2,1)}, f32[1,1280]{1,0:T(1,128)}) custom-call(bf16[256,1280]{1,0:T(8,128)(2,1)} %bitcast.93, f32[1,1280]{1,0:T(1,128)} %broadcast_in_dim.98.gain_ref, f32[256,1280]{1,0:T(8,128)} %copy-done.8, ...), custom_call_target="tpu_custom_call" | custom-call | flops 5033164800 | bytes 19660800 | tf_op jit(solution)/shard_map/finish/pallas_call | solution.py:1026
  636.2 4.1 multiply_reduce_fusion
  640.3 2.0 maximum_convert_fusion
  642.7 0.8 pad.5.clone
  643.5 74.5 %scatter_whole.1 = f32[40,3968]{1,0:T(8,128)} custom-call(bf16[32,40,1280]{2,1,0:T(8,128)(2,1)} %bitcast.85, bf16[32,40,1280]{2,1,0:T(8,128)(2,1)} %bitcast.86, bf16[32,40,1280]{2,1,0:T(8,128)(2,1)} %bitcast.87, bf16[32,40,128]{2,1,0:T(8,128)(2,1)} %bitcast.91), custom_call_target="tpu_custom_call" | custom-call | tf_op jit(solution)/shard_map/scatter_whole/pallas_call | solution.py:638
  718.0 2.0 fusion.21
  720.7 1.5 slice_reduce_fusion
  722.2 1.3 sqrt_bitcast_fusion
  724.1 3.3 copy.78
  727.4 1.4 copy.79
  (105 shorter events, 10.4 us)
Async XLA Ops:
  7.2 232.0 %all-gather.3.cloned.1.call-start = ((), (), s32[]{:S(2)}) async-start(), calls=%async_computation.2 | async-start | bytes 11141120 | tf_op jit(solution)/shard_map/all_gather | solution.py:1322
  19.3 34.9 %copy-start.37 = (s32[1,4]{1,0:T(1,128)S(1)}, s32[1,4]{1,0:T(1,128)}, u32[]{:S(2)}) copy-start(s32[1,4]{1,0:T(1,128)} %param.18) | copy-start | bytes 52
  19.3 38.3 %copy-start.33 = (s32[1,256,7]{1,0,2:T(1,128)S(1)}, s32[1,256,7]{1,0,2:T(1,128)}, u32[]{:S(2)}) copy-start(s32[1,256,7]{1,0,2:T(1,128)} %param.19) | copy-start | bytes 21508
  54.1 582.1 %reduce-scatter.2.cloned.1.call-start = ((), (), s32[]{:S(2)}) async-start(), calls=%async_computation.1 | async-start | bytes 11141120 | tf_op jit(solution)/shard_map/reduce_scatter | solution.py:1353
  54.4 3.9 copy-start.30
  58.3 7.9 %copy-start.21 = (bf16[1,256,1280]{2,1,0:T(8,128)(2,1)S(1)}, bf16[1,256,1280]{2,1,0:T(8,128)(2,1)}, u32[]{:S(2)}) copy-start(bf16[1,256,1280]{2,1,0:T(8,128)(2,1)} %param.17) | copy-start | bytes 1966084
  66.2 5.0 copy-start.25
  66.2 5.2 copy-start.23
  70.1 1.0 copy-start.3
  70.1 2.6 copy-start.34
  70.2 2.6 copy-start.28
  71.4 161.3 %copy-start = (bf16[256,1280]{1,0:T(8,128)(2,1)}, bf16[256,1280]{1,0:T(8,128)(2,1)S(1)}, u32[]{:S(2)}) copy-start(bf16[256,1280]{1,0:T(8,128)(2,1)S(1)} %multiply_convert_fusion) | copy-start | bytes 1966084
  312.6 1.1 copy-start.1
  312.6 1.9 copy-start.10
  314.5 1.6 copy-start.12
  316.1 1.1 copy-start.6
  316.1 2.3 copy-start.13
  320.3 0.8 copy-start.18
  320.3 8.4 %copy-start.17 = (bf16[256,896]{1,0:T(8,128)(2,1)}, bf16[256,896]{1,0:T(8,128)(2,1)S(1)}, u32[]{:S(2)}) copy-start(bf16[256,896]{1,0:T(8,128)(2,1)S(1)} %get-tuple-element.144) | copy-start | bytes 1376260
  328.7 2.3 copy-start.11
  328.7 2.6 copy-start.20
  456.2 3.4 copy-start.31
  456.2 3.4 copy-start.4
  456.2 3.4 copy-start.15
  456.2 3.4 copy-start.24
  456.2 3.4 copy-start.26
  456.3 3.4 copy-start.29
  459.7 2.9 copy-start.35
  459.7 2.9 copy-start.7
  462.6 1.1 copy-start.14
  463.7 2.8 copy-start.8
  463.7 3.4 copy-start.36
  615.8 3.2 copy-start.22
  615.8 4.0 copy-start.2
  615.8 4.0 copy-start.16
  615.8 4.0 copy-start.32
  621.1 15.1 %copy-start.5 = (f32[256,1280]{1,0:T(8,128)S(1)}, f32[256,1280]{1,0:T(8,128)}, u32[]{:S(2)}) copy-start(f32[256,1280]{1,0:T(8,128)} %copy-done.3) | copy-start | bytes 3932164
  621.1 15.1 %copy-start.19 = (bf16[256,896]{1,0:T(8,128)(2,1)S(1)}, bf16[256,896]{1,0:T(8,128)(2,1)}, u32[]{:S(2)}) copy-start(bf16[256,896]{1,0:T(8,128)(2,1)} %copy-done.18) | copy-start | bytes 1376260
  636.2 6.2 copy-start.27
  724.1 3.3 copy-start.9
Sparse Core Ops, SparseCore 0:
  54.2 161.6 all-gather.2
  312.8 151.7 reduce-scatter.1

commit v6 on v5

--- a/solution.py
+++ b/solution.py
@@ -40,6 +40,7 @@
 
 
 MESH = pl.DeviceIdType.MESH
+COUPLES = 2
 VMEM_MOST = 64 * 1024 * 1024 - 65536
 
 
@@ -118,7 +119,7 @@
         pl.semaphore_wait(barrier, self.wide + 2 - ends)
 
 
-def gather_kernel(plan, pieces, x_ref, out_ref, ra, sa_up, sa_dn, rb, sb, rc, sc, own):
+def gather_kernel(plan, pieces, beside, x_ref, out_ref, ra, sa_up, sa_dn, rb, sb, rc, sc, own):
     a, b, c = plan.place()
     steps, wide = plan.steps, plan.wide
     at = {d: i for i, d in enumerate(steps)}
@@ -177,6 +178,8 @@
     keep.start()
     far = max(abs(d) for d in steps)
     for step in range(1, far + 3):
+        beside(step - 1)
+
         @pl.loop(0, pieces)
         def _(q, step=step):
             for d in (step, -step):
@@ -231,7 +234,7 @@
     n, wide = len(plan.steps), plan.wide
     sem = pltpu.SemaphoreType.DMA
     return pl.pallas_call(
-        functools.partial(gather_kernel, plan, pieces),
+        functools.partial(gather_kernel, plan, pieces, lambda n: None),
         out_shape=jax.ShapeDtypeStruct((ep_count,) + block.shape, block.dtype),
         in_specs=[pl.BlockSpec(memory_space=pltpu.VMEM)],
         out_specs=pl.BlockSpec(memory_space=pl.ANY),
@@ -240,6 +243,69 @@
         compiler_params=pltpu.CompilerParams(collective_id=collective_id, has_side_effects=True),
         name="gather_rows",
     )(block)
+
+
+def gather_shared(block, grads, gate, up, down, collective_id, pieces=4):
+    ep_count = lax.axis_size("ep")
+    plan = Plan(ep_count, False)
+    n, wide = len(plan.steps), plan.wide
+    rows, width = grads.shape
+    ff = gate.shape[1]
+    sem = pltpu.SemaphoreType.DMA
+    stages = max(plan.steps) + 2
+    tiles = ff // HEAD
+
+    def kernel(x_ref, g_ref, wg_ref, wu_ref, wd_ref, out_ref, shared_ref, back_ref, dg_ref, du_ref, dd_ref, *sems):
+        dot = lambda left, right: jnp.dot(left, right, preferred_element_type=jnp.float32)
+
+        def tile(i):
+            at = pl.ds(pl.multiple_of(i * HEAD, HEAD), HEAD)
+            x, g = x_ref[:, :width], g_ref[...]
+            w_gate, w_up, w_down = wg_ref[:, at], wu_ref[:, at], wd_ref[at, :]
+            silu, slope = silu_parts(dot(x, w_gate))
+            lift = dot(x, w_up)
+            mid = (silu * lift).astype(jnp.bfloat16)
+            mid_grad = inner_right(g, w_down)
+            pre_grad = (mid_grad * lift * slope).astype(jnp.bfloat16)
+            lift_grad = (mid_grad * silu).astype(jnp.bfloat16)
+            out = dot(mid, w_down)
+            back = inner_right(pre_grad, w_gate) + inner_right(lift_grad, w_up)
+
+            @pl.when(i == 0)
+            def _():
+                shared_ref[...] = out
+                back_ref[...] = back
+
+            @pl.when(i > 0)
+            def _():
+                shared_ref[...] += out
+                back_ref[...] += back
+
+            dg_ref[:, at] = inner_left(x, pre_grad).astype(jnp.bfloat16)
+            du_ref[:, at] = inner_left(x, lift_grad).astype(jnp.bfloat16)
+            dd_ref[:, at] = inner_left(g, mid).astype(jnp.bfloat16)
+
+        def beside(stage):
+            pl.loop(tiles * stage // stages, tiles * (stage + 1) // stages)(tile)
+
+        gather_kernel(plan, pieces, beside, x_ref, out_ref, *sems)
+
+    near = pl.BlockSpec(memory_space=pltpu.VMEM)
+    return pl.pallas_call(
+        kernel,
+        out_shape=(
+            jax.ShapeDtypeStruct((ep_count,) + block.shape, block.dtype),
+            jax.ShapeDtypeStruct((rows, width), jnp.float32),
+            jax.ShapeDtypeStruct((rows, width), jnp.float32),
+        ) + (jax.ShapeDtypeStruct((width, ff), jnp.bfloat16),) * 3,
+        in_specs=[near] * 5,
+        out_specs=(pl.BlockSpec(memory_space=pl.ANY),) + (near,) * 5,
+        scratch_shapes=[sem((n, pieces)), sem((n, pieces)), sem((n, pieces)), sem((n, wide, pieces)),
+                        sem((n, wide, pieces)), sem((n, wide, pieces)), sem((n, wide, pieces)), sem],
+        compiler_params=pltpu.CompilerParams(
+            collective_id=collective_id, has_side_effects=True, vmem_limit_bytes=VMEM_MOST),
+        name="gather_shared",
+    )(block, grads, gate, up, down)
 
 
 def add_rows(dst, others, out=None):
@@ -585,8 +651,9 @@
     groups, ep_count = lax.axis_size("grp"), lax.axis_size("ep")
     place = Place(groups, ep_count)
     tiles = width // HEAD
-    cuts = [0, tiles // 2 * HEAD, width]
-    orders = ["xba", "bxa"]
+    count = 2 * COUPLES
+    cuts = [tiles * n // count * HEAD for n in range(count + 1)]
+    orders = ["xba", "bxa"] * COUPLES
 
     def kernel(*refs):
         sources, refs = refs[: len(parts)], refs[len(parts) :]
@@ -622,9 +689,12 @@
             for s in couple:
                 s.stage_two()
 
-        for stage in (core, one, two):
-            for couple in couples:
-                stage(couple)
+        core(couples[0])
+        for n, couple in enumerate(couples):
+            one(couple)
+            if n + 1 < len(couples):
+                core(couples[n + 1])
+            two(couple)
         for s, out in zip(sums, outs):
             s.stage_three(out)
         for s in sums:
@@ -1122,7 +1192,8 @@
     plan, pieces = Plan(ep_count, True), 4
     place = Place(lax.axis_size("grp"), ep_count)
     n, wide = plan.planes(), plan.wide
-    cuts = [0, part_width // HEAD // 2 * HEAD, part_width]
+    cuts = [0, part_width // HEAD * 3 // 4 * HEAD, part_width]
+    orders = ("xba", "bxa")
 
     def kernel(q_ref, g_ref, mixed_ref, start_ref, total_ref, cos_ref, sin_ref, pair_ref, *refs):
         sources, refs = refs[: len(parts)], refs[len(parts) :]
@@ -1131,7 +1202,7 @@
         place.locate()
         sums = []
         for i in range(2):
-            sums.append(WholeSum(place, "xba", pieces_of(sources, cuts[i], cuts[i + 1]), refs[:14]))
+            sums.append(WholeSum(place, orders[i], pieces_of(sources, cuts[i], cuts[i + 1]), refs[:14]))
             refs = refs[14:]
         sum_rows = RowSum(plan, pieces, staged, refs)
         a, b, c = sum_rows.a, sum_rows.b, sum_rows.c
@@ -1203,41 +1274,39 @@
 
         begin(0, True)
         begin(0, False)
+        place.greet()
+        for i in range(max(one.n1 for one in sums)):
+            for one in sums:
+                if i < one.n1:
+                    one.start(i)
         acc[...] = jnp.zeros_like(acc)
         for h in range(HEADS):
             grad = g_ref[:, h * HEAD : (h + 1) * HEAD].astype(jnp.float32).T
             term[h] = jnp.sum(grad * mixed_ref[h], axis=0, keepdims=True)
-        place.greet()
         far = (wide - 1) * len(order)
         for one in sums:
             for i in range(one.n1 - 1):
-                one.start(i)
-        turn_of(0)
-        for one in sums:
-            for i in range(one.n1 - 1):
                 one.stage_core(i)
-        for one in sums:
-            one.start(one.n1 - 1)
-        for turn in range(1, len(turns)):
+        first, second = sums
+        ones = {far - 1: (second, 1), far: (first, 1), far + 1: (second, 0), far + 2: (first, 0)}
+        for turn in range(len(turns)):
             turn_of(turn)
-            if turn <= far:
-                pass_on(turn - 1)
-            if turn == far:
+            if turn == 0:
                 for one in sums:
                     one.stage_core(one.n1 - 1)
+            elif turn <= far:
+                pass_on(turn - 1)
+            if turn in ones:
+                one, part = ones[turn]
+                for k2 in from_far(one.n2)[:-1] if part else [0]:
+                    one.stage_one(k2)
         for h in range(HEADS):
             back = turned(acc[h].T * HEAD ** (-0.5), cos_ref[...], -sin_ref[...])
             dq_ref[:, h * HEAD : (h + 1) * HEAD] = back.astype(jnp.bfloat16)
-        sum_rows.stage_dests(0, 2)
-        for k2 in from_far(sums[0].n2):
-            sums[0].stage_one(k2)
-        sum_rows.stage_dests(2, 3)
-        sums[0].stage_two()
-        for k2 in from_far(sums[1].n2):
-            sums[1].stage_one(k2)
-        sum_rows.stage_dests(3, 4)
-        sums[1].stage_two()
+        second.stage_two()
+        sum_rows.stage_dests(0, pieces)
         pair_out[...] = sum_rows.result()
+        first.stage_two()
         for i, one in enumerate(sums):
             one.stage_three(out_ref.at[:, pl.ds(cuts[i], cuts[i + 1] - cuts[i])])
         sum_rows.drain()
@@ -1254,7 +1323,7 @@
         pltpu.SemaphoreType.DMA((2,)),
     ]
     for i in range(2):
-        scratch += WholeSum.scratch(place.sizes, "xba", part_rows, cuts[i + 1] - cuts[i], parts[0].dtype, len(parts))
+        scratch += WholeSum.scratch(place.sizes, orders[i], part_rows, cuts[i + 1] - cuts[i], parts[0].dtype, len(parts))
     scratch += RowSum.scratch(plan, rows, 2 * width, pairs.dtype, pieces)
     return pl.pallas_call(
         kernel,
@@ -1336,7 +1405,9 @@
     side = width + 2 * HEAD if 2 * expert_count > HEAD else width + HEAD
     pad = jnp.zeros((rows, side - width - 2 * expert_count), jnp.bfloat16)
     sent = jnp.concatenate([ffn_low, probs_high, probs_rest, pad], axis=1)
-    arrived = gather_rows(sent, False, 2)
+    arrived, shared_out, ffn_grad, shared_gate_part, shared_up_part, shared_down_part = gather_shared(
+        sent, grad_low, shared_gate, shared_up, shared_down, 2
+    )
 
     own = experts[None, None, :] == ep_index
     high = arrived[:, :, width : width + expert_count]
@@ -1368,17 +1439,7 @@
         up_sum = over_groups(low(inner_left(flat_in, lift_grad)))
         down_sum = over_groups(own_down_grad)
 
-    shared_pre = dot(ffn_low, shared_gate)
-    shared_lift = dot(ffn_low, shared_up)
-    shared_silu, shared_slope = silu_parts(shared_pre)
-    shared_mid = low(shared_silu * shared_lift)
-    shared_out = dot(shared_mid, shared_down)
     grad_out = wide(grad_low)
-    shared_mid_grad = inner_right(grad_low, shared_down)
-    shared_pre_grad = low(shared_mid_grad * shared_lift * shared_slope)
-    shared_lift_grad = low(shared_mid_grad * shared_silu)
-    ffn_grad = inner_right(shared_pre_grad, shared_gate) + inner_right(shared_lift_grad, shared_up)
-
     layer_out = residual + shared_out + routed
     gate_back = wide(back_sum[:, width : width + expert_count]) + wide(
         back_sum[:, width + expert_count : width + 2 * expert_count]
@@ -1394,8 +1455,7 @@
     by_device = lambda v: low(v).reshape(device_count, width // device_count, -1)
     early = [
         by_device(part)
-        for part in (inner_left(ffn_low, shared_pre_grad), inner_left(ffn_low, shared_lift_grad),
-                     inner_left(grad_low, shared_mid), inner_left(mixed_low, mixer_grad_low))
+        for part in (shared_gate_part, shared_up_part, shared_down_part, inner_left(mixed_low, mixer_grad_low))
     ]
     if ep_count > 16:
         pair_parts, query_lin_grad = attend_back(

time: 743 us -> 735 us (0.989)
  waiting for transfers between devices: 0.04 us -> 19.3 us
  matrix products: 32.1 us -> 13 us
  local copies, waits for them, and re-layouts: 34.1 us -> 25.6 us
    reduce_scatter x1, waiting for transfers between devices: 0.01 us -> 19.3 us  [local(): routed = wide(lax.psum_scatter(given, 'ep', scatter_dimension=0))]
    unnamed x82 -> x52, local copies, waits for them, and re-layouts: 16.4 us -> 11 us
  transfers between devices with their start and end apart: 2 -> 2, of which waited for: 0 -> 1; matrix products, arithmetic and copies ran while one was open for 7% -> 3% of each run, Pallas kernels for 61% -> 40%
where the time goes in v6:
time: 735 us; the launch traced here: 729 us
  Pallas kernels  637 us (87%)
  local copies, waits for them, and re-layouts  25.6 us (3%)
  waiting for transfers between devices  19.3 us (3%)
  between operations  17.4 us (2%)
  other arithmetic  16.6 us (2%)
  matrix products  13 us (2%)
    pallas_call x1, Pallas kernels, gather_shared(): pl.pallas_call(kernel, out_shape=(jax.ShapeDtypeStruct((ep_count,) + bloc...  162 us
    pallas_call x1, Pallas kernels, attend_back_sum(): pl.pallas_call(kernel, out_shape=(jax.ShapeDtypeStruct((part_rows, part_w...  143 us
    pallas_call x1, Pallas kernels, scatter_experts(): pl.pallas_call(kernel, out_shape=tuple(outs), in_specs=[anywhere] * 6, ou...  125 us
    pallas_call x1, Pallas kernels, run_experts(): pl.pallas_call(experts_kernel, out_shape=(shape(count, rows, side), shape...  73.5 us
    pallas_call x1, Pallas kernels, scatter_whole(): pl.pallas_call(kernel, out_shape=tuple(out_shape), in_specs=[anywhere] *...  67.4 us
    pallas_call x1, Pallas kernels, gather_rows(): pl.pallas_call(functools.partial(gather_kernel, plan, pieces, lambda n: N...  34.8 us
    reduce_scatter x1, waiting for transfers between devices, local(): routed = wide(lax.psum_scatter(given, 'ep', scatter_dimension=0))  19.3 us
  transfers between devices with their start and end apart: 2, of which 1 were waited for; matrix products, arithmetic and copies ran while one was open for 3% of the time, Pallas kernels for 40%

profile of v6, /device:TPU:0, one launch (start us, length us, event | category | flops | bytes accessed | tf_op | source)
XLA Modules:
  0.0 728.8 jit_solution(13165026952301905054)
XLA Ops:
  7.3 1.3 broadcast_in_dim.98.gain_ref
  8.6 0.5 fusion.7
  9.1 0.8 pad_maximum_fusion.cos_ref
  9.9 0.8 pad_maximum_fusion.1.sin_ref
  10.6 8.6 %project.1 = (bf16[256,1280]{1,0:T(8,128)(2,1)}, bf16[256,1280]{1,0:T(8,128)(2,1)}, bf16[256,2560]{1,0:T(8,128)(2,1)}) custom-call(bf16[256,1280]{1,0:T(8,128)(2,1)} %bitcast.71, f32[1,1280]{1,0:T(1,128)} %broadcast_in_dim.98.gain_ref, f32[256,128]{1,0:T(8,128)} %pad_maximum_fusion.cos_ref, f32[256,128]{1,0:T(8,128)} %pad_maximum_fusion.1.sin_ref, ...), custom_call_target="tpu_custom_call" | custom-call | flops 2516582400 | bytes 9830400 | tf_op jit(solution)/shard_map/project/pallas_call | solution.py:885
  19.2 34.8 %gather_rows.1.kv_ref.pair_ref = bf16[16,256,2560]{2,1,0:T(8,128)(2,1)} custom-call(bf16[256,2560]{1,0:T(8,128)(2,1)} %get-tuple-element.50.x_ref), custom_call_target="tpu_custom_call" | custom-call | tf_op jit(solution)/shard_map/gather_rows/pallas_call | solution.py:236
  54.4 0.5 slice.56
  57.7 0.6 pad_add_fusion.info
  58.3 7.9 %attend.1 = (f32[10,128,256]{2,1,0:T(8,128)}, bf16[256,1280]{1,0:T(8,128)(2,1)}, f32[10,1,256]{2,1,0:T(1,128)}) custom-call(s32[2]{0:T(128)} %pad_add_fusion.info, bf16[256,1280]{1,0:T(8,128)(2,1)} %get-tuple-element.49.q_ref, s32[1,256]{1,0:T(1,128)} %bitcast.76, bf16[16,256,2560]{2,1,0:T(8,128)(2,1)} %gather_rows.1.kv_ref.pair_ref), custom_call_target="tpu_custom_call" | custom-call | flops 3019898880 | bytes 11796480 | tf_op jit(solution)/shard_map/attend/pallas_call | solution.py:943
  66.1 3.9 multiply_reduce_fusion.5
  70.2 0.6 copy-done.11
  70.8 0.4 fusion.15
  71.4 0.8 subtract_convert_fusion
  72.2 1.0 concatenate.15.x_ref
  73.3 161.6 %gather_shared.1 = (bf16[16,256,1408]{2,1,0:T(8,128)(2,1)}, f32[256,1280]{1,0:T(8,128)}, f32[256,1280]{1,0:T(8,128)}, bf16[1280,896]{1,0:T(8,128)(2,1)}, bf16[12...) custom-call(bf16[256,1408]{1,0:T(8,128)(2,1)} %concatenate.15.x_ref, bf16[256,1280]{1,0:T(8,128)(2,1)} %bitcast.60, ...), custom_call_target="tpu_custom_call" | custom-call | tf_op jit(solution)/shard_map/gather_shared/pallas_call | solution.py:294
  234.9 2.5 select_reduce_fusion
  237.4 0.6 broadcast_in_dim.108.share_row
  238.2 0.6 copy.59.rank_row
  238.8 2.0 copy.60.rank_col
  240.8 0.6 pad_add_fusion.1.where_ref
  241.4 73.5 %run_experts.1 = (bf16[16,256,1408]{2,1,0:T(8,128)(2,1)}, bf16[16,256,1280]{2,1,0:T(8,128)(2,1)}, bf16[3072,1280]{1,0:T(8,128)(2,1)}, bf16[3072,896]{1,0:T(8,128...) custom-call(s32[2]{0:T(128)} %pad_add_fusion.1.where_ref, ...), custom_call_target="tpu_custom_call" | custom-call | flops 56371445760 | bytes 62914560 | tf_op jit(solution)/shard_map/run_experts/pallas_call | solution.py:1170
  314.9 125.3 %scatter_experts.1 = (bf16[256,1408]{1,0:T(8,128)(2,1)}, f32[640,896]{1,0:T(8,128)}, f32[640,896]{1,0:T(8,128)}, f32[640,896]{1,0:T(8,128)}) custom-call(bf16[16,256,1408]{2,1,0:T(8,128)(2,1)} %get-tuple-element.58.p_ref, bf16[3072,1280]{1,0:T(8,128)(2,1)} %get-tuple-element.59.in_ref, bf16[3072,1280]{1,0:T(8,128)(2,1)} %get-tuple-element.60.og_ref, ...), custom_call_target="tpu_custom_call" | custom-call | tf_op jit(solution)/shard_map/scatter_experts/pallas_call | solution.py:826
  440.2 3.2 copy.63
  443.4 1.1 multiply_reduce_fusion.6
  444.5 1.9 convolution_convert_fusion.2
  446.4 2.0 convolution_add_fusion
  448.4 19.3 %reduce-scatter.2.cloned.1.call-done = bf16[1,256,1280]{2,1,0:T(8,128)(2,1)} async-done(((bf16[16,256,1280]{2,1,0:T(8,128)(2,1)}), bf16[1,256,1280]{2,1,0:T(8,128)(2,1)}) %reduce-scatter.2.cloned.1.call-update) | async-done | bytes 655376 | tf_op jit(solution)/shard_map/reduce_scatter | solution.py:1424
  467.7 3.8 multiply_reduce_fusion.4
  471.5 0.4 fusion.res_ref
  471.9 1.5 copy-done.21
  473.5 1.9 convolution_convert_fusion.1.g_ref
  475.4 2.8 convolution_convert_fusion
  478.2 143.4 %attend_back_sum.1 = (f32[40,3968]{1,0:T(8,128)}, bf16[256,2560]{1,0:T(8,128)(2,1)}, bf16[256,1280]{1,0:T(8,128)(2,1)}) custom-call(bf16[256,1280]{1,0:T(8,128)(2,1)} %get-tuple-element.49.q_ref, bf16[256,1280]{1,0:T(8,128)(2,1)} %convolution_convert_fusion.1.g_ref, f32[10,128,256]{2,1,0:T(8,128)} %get-tuple-element.66.mixed_ref, s32[1,256]{1,0:T(1,128)} %bitcast.77, ...), custom_call_target="tpu_custom_call" | custom-call | tf_op jit(solution)/shard_map/attend_back_sum/pallas_call | solution.py:1328
  621.6 1.6 slice.66
  623.2 1.8 slice_bitcast_fusion
  625.0 0.7 broadcast_in_dim.112
  625.7 14.3 %finish.1 = (bf16[1280,1280]{1,0:T(8,128)(2,1)}, bf16[1280,1280]{1,0:T(8,128)(2,1)}, bf16[1280,1280]{1,0:T(8,128)(2,1)}, bf16[256,1280]{1,0:T(8,128)(2,1)}, f32[1,1280]{1,0:T(1,128)}) custom-call(bf16[256,1280]{1,0:T(8,128)(2,1)} %bitcast.72, f32[1,1280]{1,0:T(1,128)} %broadcast_in_dim.98.gain_ref, f32[256,1280]{1,0:T(8,128)} %copy-done.5, ...), custom_call_target="tpu_custom_call" | custom-call | flops 5033164800 | bytes 19660800 | tf_op jit(solution)/shard_map/finish/pallas_call | solution.py:1096
  640.0 0.7 convert_bitcast_fusion.1
  640.7 2.0 maximum_convert_fusion
  642.9 0.2 copy.66
  643.1 0.8 pad.5.clone
  643.9 67.4 %scatter_whole.1 = f32[40,3968]{1,0:T(8,128)} custom-call(bf16[32,40,1280]{2,1,0:T(8,128)(2,1)} %bitcast.61, bf16[32,40,1280]{2,1,0:T(8,128)(2,1)} %bitcast.62, bf16[32,40,1280]{2,1,0:T(8,128)(2,1)} %bitcast.63, bf16[32,40,128]{2,1,0:T(8,128)(2,1)} %bitcast.70), custom_call_target="tpu_custom_call" | custom-call | tf_op jit(solution)/shard_map/scatter_whole/pallas_call | solution.py:708
  711.4 1.3 sqrt_bitcast_fusion
  712.7 1.5 slice_reduce_fusion
  714.2 2.0 fusion.14
  716.2 0.7 copy.62
  716.8 3.3 copy.74
  720.2 1.4 copy.75
  (67 shorter events, 1.3 us)
Async XLA Ops:
  7.2 234.2 %all-gather.3.cloned.1.call-start = ((), (), s32[]{:S(2)}) async-start(), calls=%async_computation.2 | async-start | bytes 11141120 | tf_op jit(solution)/shard_map/all_gather | solution.py:1391
  19.2 34.9 %copy-start.22 = (s32[1,4]{1,0:T(1,128)S(1)}, s32[1,4]{1,0:T(1,128)}, u32[]{:S(2)}) copy-start(s32[1,4]{1,0:T(1,128)} %param.18) | copy-start | bytes 52
  19.2 38.3 %copy-start.18 = (s32[1,256,7]{1,0,2:T(1,128)S(1)}, s32[1,256,7]{1,0,2:T(1,128)}, u32[]{:S(2)}) copy-start(s32[1,256,7]{1,0,2:T(1,128)} %param.19) | copy-start | bytes 21508
  54.0 413.7 %reduce-scatter.2.cloned.1.call-start = ((), (), s32[]{:S(2)}) async-start(), calls=%async_computation.1 | async-start | bytes 11141120 | tf_op jit(solution)/shard_map/reduce_scatter | solution.py:1424
  54.4 3.9 copy-start.17
  58.3 7.9 %copy-start.9 = (bf16[1,256,1280]{2,1,0:T(8,128)(2,1)S(1)}, bf16[1,256,1280]{2,1,0:T(8,128)(2,1)}, u32[]{:S(2)}) copy-start(bf16[1,256,1280]{2,1,0:T(8,128)(2,1)} %param.17) | copy-start | bytes 1966084
  66.1 3.9 copy-start.13
  70.0 1.2 copy-start
  70.0 1.2 copy-start.19
  70.0 0.8 copy-start.11
  70.0 1.2 copy-start.15
  70.8 1.4 copy-start.2
  440.2 3.2 copy-start.8
  440.2 4.3 copy-start.3
  440.2 6.2 copy-start.12
  446.4 21.3 %copy-start.1 = (f32[256,1280]{1,0:T(8,128)S(1)}, f32[256,1280]{1,0:T(8,128)}, u32[]{:S(2)}) copy-start(f32[256,1280]{1,0:T(8,128)} %copy-done) | copy-start | bytes 3932164
  446.4 21.3 %copy-start.14 = (f32[1280]{0:T(1024)S(1)}, f32[1280]{0:T(1024)}, u32[]{:S(2)}) copy-start(f32[1280]{0:T(1024)} %param.26) | copy-start | bytes 15364
  446.4 21.3 %copy-start.16 = (f32[256]{0:T(256)S(1)}, f32[256]{0:T(256)}, u32[]{:S(2)}) copy-start(f32[256]{0:T(256)} %copy-done.15) | copy-start | bytes 3076
  467.7 3.8 copy-start.20
  467.7 3.8 copy-start.4
  471.5 1.9 copy-start.21
  473.5 1.9 copy-start.5
  473.5 1.9 copy-start.7
  625.7 17.1 %copy-start.10 = (bf16[1280,16]{0,1:T(8,128)(2,1)S(1)}, bf16[1280,16]{0,1:T(8,128)(2,1)}, u32[]{:S(2)}) copy-start(bf16[1280,16]{0,1:T(8,128)(2,1)} %convolution_convert_fusion.2) | copy-start | bytes 122884
  711.4 4.8 slice-start
  716.8 3.3 copy-start.6
Sparse Core Ops, SparseCore 0:
  54.2 161.0 all-gather.2
  315.0 152.6 reduce-scatter.1

commit v7 on v6

--- a/solution.py
+++ b/solution.py
@@ -440,6 +440,11 @@
         def _(q):
             for d in self.order:
                 self.dest(d, q)
+
+    def stage_dest(self, d, low, high):
+        @pl.loop(low, high)
+        def _(q):
+            self.dest(d, q)
 
     def dest(self, d, q):
         p, a, b, steps = self.plan, self.a, self.b, self.plan.steps
@@ -1208,7 +1213,7 @@
         a, b, c = sum_rows.a, sum_rows.b, sum_rows.c
         me = plan.slot(a, b, c)
         order, ks = sum_rows.order, from_far(wide)
-        turns = [(k, d) for k in ks for d in order]
+        turns = [(k, d) for d in order for k in ks]
 
         def block(turn, other):
             k, d = turns[turn]
@@ -1275,36 +1280,45 @@
         begin(0, True)
         begin(0, False)
         place.greet()
-        for i in range(max(one.n1 for one in sums)):
-            for one in sums:
-                if i < one.n1:
-                    one.start(i)
+        first, second = sums
+        for one in sums:
+            for i in range(one.n1 - 1):
+                one.start(i)
         acc[...] = jnp.zeros_like(acc)
         for h in range(HEADS):
             grad = g_ref[:, h * HEAD : (h + 1) * HEAD].astype(jnp.float32).T
             term[h] = jnp.sum(grad * mixed_ref[h], axis=0, keepdims=True)
-        far = (wide - 1) * len(order)
         for one in sums:
             for i in range(one.n1 - 1):
                 one.stage_core(i)
-        first, second = sums
-        ones = {far - 1: (second, 1), far: (first, 1), far + 1: (second, 0), far + 2: (first, 0)}
+        last = len(turns) - 1
         for turn in range(len(turns)):
             turn_of(turn)
+            if turns[turn][0]:
+                pass_on(turn)
             if turn == 0:
                 for one in sums:
+                    one.start(one.n1 - 1)
+            if turn == last - 3:
+                for one in sums:
                     one.stage_core(one.n1 - 1)
-            elif turn <= far:
-                pass_on(turn - 1)
-            if turn in ones:
-                one, part = ones[turn]
-                for k2 in from_far(one.n2)[:-1] if part else [0]:
-                    one.stage_one(k2)
+                for k2 in from_far(second.n2)[:-1]:
+                    second.stage_one(k2)
+            if turn == last - 2:
+                sum_rows.stage_dest(order[0], 0, 2)
+            if turn == last - 1:
+                for k2 in from_far(first.n2)[:-1]:
+                    first.stage_one(k2)
+                second.stage_one(0)
+                sum_rows.stage_dest(order[0], 2, 3)
+        sum_rows.stage_dest(order[0], 3, pieces)
+        first.stage_one(0)
         for h in range(HEADS):
             back = turned(acc[h].T * HEAD ** (-0.5), cos_ref[...], -sin_ref[...])
             dq_ref[:, h * HEAD : (h + 1) * HEAD] = back.astype(jnp.bfloat16)
         second.stage_two()
-        sum_rows.stage_dests(0, pieces)
+        for d in order[1:]:
+            sum_rows.stage_dest(d, 0, pieces)
         pair_out[...] = sum_rows.result()
         first.stage_two()
         for i, one in enumerate(sums):
@@ -1421,7 +1435,7 @@
     back, given, flat_in, pre_grad, lift_grad, middle, result_grad = run_experts(
         places, arrived, grads_all, rank, share, expert_gate, expert_up, expert_down, capacity
     )
-    routed = wide(lax.psum_scatter(given, "ep", scatter_dimension=0))
+    routed = lax.psum_scatter(given, "ep", scatter_dimension=0)
     group_count = lax.axis_size("grp")
     if group_count == 2:
         back_sum, gate_sum, up_sum, down_sum = scatter_experts(
@@ -1440,7 +1454,6 @@
         down_sum = over_groups(own_down_grad)
 
     grad_out = wide(grad_low)
-    layer_out = residual + shared_out + routed
     gate_back = wide(back_sum[:, width : width + expert_count]) + wide(
         back_sum[:, width + expert_count : width + 2 * expert_count]
     )
@@ -1468,6 +1481,8 @@
             queries, mixed_grad, mixed, start[None, :], log_total, cosine, sine, pairs, early, 5
         )
 
+    routed, pair_grads = lax.optimization_barrier((routed, pair_grads))
+    layer_out = residual + shared_out + wide(routed)
     query_part, key_part, value_part, tokens_grad, mixer_gain_grad = finish(
         tokens[0], mixer_gain, residual_grad, hidden_low, query_lin_grad, pair_grads, cosine, sine,
         query_weight, key_weight, value_weight,

time: 735 us -> 699 us (0.951)
  Pallas kernels: 637 us -> 615 us
  waiting for transfers between devices: 19.3 us -> 0.04 us
    reduce_scatter x1, waiting for transfers between devices: 19.3 us -> 0.01 us  [local(): routed = lax.psum_scatter(given, 'ep', scatter_dimension=0)]
    pallas_call x1, Pallas kernels: 143 us -> 128 us  [attend_back_sum(): pl.pallas_call(kernel, out_shape=(jax.ShapeDtypeStruct((part_rows, part_w...]
  transfers between devices with their start and end apart: 2 -> 2, of which waited for: 1 -> 0; matrix products, arithmetic and copies ran while one was open for 3% -> 5% of each run, Pallas kernels for 40% -> 61%
where the time goes in v7:
time: 699 us; the launch traced here: 686 us
  Pallas kernels  615 us (88%)
  local copies, waits for them, and re-layouts  25.5 us (4%)
  between operations  17.5 us (3%)
  other arithmetic  14.7 us (2%)
  matrix products  13 us (2%)
    pallas_call x1, Pallas kernels, gather_shared(): pl.pallas_call(kernel, out_shape=(jax.ShapeDtypeStruct((ep_count,) + bloc...  162 us
    pallas_call x1, Pallas kernels, attend_back_sum(): pl.pallas_call(kernel, out_shape=(jax.ShapeDtypeStruct((part_rows, part_w...  128 us
    pallas_call x1, Pallas kernels, scatter_experts(): pl.pallas_call(kernel, out_shape=tuple(outs), in_specs=[anywhere] * 6, ou...  122 us
    pallas_call x1, Pallas kernels, run_experts(): pl.pallas_call(experts_kernel, out_shape=(shape(count, rows, side), shape...  73.5 us
    pallas_call x1, Pallas kernels, scatter_whole(): pl.pallas_call(kernel, out_shape=tuple(out_shape), in_specs=[anywhere] *...  64.4 us
    pallas_call x1, Pallas kernels, gather_rows(): pl.pallas_call(functools.partial(gather_kernel, plan, pieces, lambda n: N...  34.8 us
    pallas_call x1, Pallas kernels, finish(): pl.pallas_call(finish_kernel, out_shape=(jax.ShapeDtypeStruct((width, wid...  14.4 us
  transfers between devices with their start and end apart: 2, of which 0 were waited for; matrix products, arithmetic and copies ran while one was open for 5% of the time, Pallas kernels for 61%

profile of v7, /device:TPU:0, one launch (start us, length us, event | category | flops | bytes accessed | tf_op | source)
XLA Modules:
  0.0 685.9 jit_solution(13113246112592810215)
XLA Ops:
  7.3 1.3 broadcast_in_dim.98.gain_ref
  8.6 0.5 fusion.7
  9.1 0.8 pad_maximum_fusion.cos_ref
  9.9 0.8 pad_maximum_fusion.1.sin_ref
  10.6 8.6 %project.1 = (bf16[256,1280]{1,0:T(8,128)(2,1)}, bf16[256,1280]{1,0:T(8,128)(2,1)}, bf16[256,2560]{1,0:T(8,128)(2,1)}) custom-call(bf16[256,1280]{1,0:T(8,128)(2,1)} %bitcast.65, f32[1,1280]{1,0:T(1,128)} %broadcast_in_dim.98.gain_ref, f32[256,128]{1,0:T(8,128)} %pad_maximum_fusion.cos_ref, f32[256,128]{1,0:T(8,128)} %pad_maximum_fusion.1.sin_ref, ...), custom_call_target="tpu_custom_call" | custom-call | flops 2516582400 | bytes 9830400 | tf_op jit(solution)/shard_map/project/pallas_call | solution.py:890
  19.2 34.8 %gather_rows.1.kv_ref.pair_ref = bf16[16,256,2560]{2,1,0:T(8,128)(2,1)} custom-call(bf16[256,2560]{1,0:T(8,128)(2,1)} %get-tuple-element.52.x_ref), custom_call_target="tpu_custom_call" | custom-call | tf_op jit(solution)/shard_map/gather_rows/pallas_call | solution.py:236
  54.4 0.5 slice.56
  57.7 0.6 pad_add_fusion.info
  58.3 7.9 %attend.1 = (f32[10,128,256]{2,1,0:T(8,128)}, bf16[256,1280]{1,0:T(8,128)(2,1)}, f32[10,1,256]{2,1,0:T(1,128)}) custom-call(s32[2]{0:T(128)} %pad_add_fusion.info, bf16[256,1280]{1,0:T(8,128)(2,1)} %get-tuple-element.51.q_ref, s32[1,256]{1,0:T(1,128)} %bitcast.71, bf16[16,256,2560]{2,1,0:T(8,128)(2,1)} %gather_rows.1.kv_ref.pair_ref), custom_call_target="tpu_custom_call" | custom-call | flops 3019898880 | bytes 11796480 | tf_op jit(solution)/shard_map/attend/pallas_call | solution.py:948
  66.1 3.9 multiply_reduce_fusion.5
  70.2 0.6 copy-done.13
  70.8 0.4 fusion.15
  71.4 0.8 subtract_convert_fusion
  72.2 1.0 concatenate.15.x_ref
  73.3 161.7 %gather_shared.1 = (bf16[16,256,1408]{2,1,0:T(8,128)(2,1)}, f32[256,1280]{1,0:T(8,128)}, f32[256,1280]{1,0:T(8,128)}, bf16[1280,896]{1,0:T(8,128)(2,1)}, bf16[12...) custom-call(bf16[256,1408]{1,0:T(8,128)(2,1)} %concatenate.15.x_ref, bf16[256,1280]{1,0:T(8,128)(2,1)} %bitcast.54, ...), custom_call_target="tpu_custom_call" | custom-call | tf_op jit(solution)/shard_map/gather_shared/pallas_call | solution.py:294
  235.0 2.5 select_reduce_fusion
  237.5 0.6 broadcast_in_dim.108.share_row
  238.3 0.6 copy.59.rank_row
  238.9 2.0 copy.60.rank_col
  240.9 0.6 pad_add_fusion.1.where_ref
  241.5 73.5 %run_experts.1 = (bf16[16,256,1408]{2,1,0:T(8,128)(2,1)}, bf16[16,256,1280]{2,1,0:T(8,128)(2,1)}, bf16[3072,1280]{1,0:T(8,128)(2,1)}, bf16[3072,896]{1,0:T(8,128...) custom-call(s32[2]{0:T(128)} %pad_add_fusion.1.where_ref, ...), custom_call_target="tpu_custom_call" | custom-call | flops 56371445760 | bytes 62914560 | tf_op jit(solution)/shard_map/run_experts/pallas_call | solution.py:1175
  315.0 122.1 %scatter_experts.1 = (bf16[256,1408]{1,0:T(8,128)(2,1)}, f32[640,896]{1,0:T(8,128)}, f32[640,896]{1,0:T(8,128)}, f32[640,896]{1,0:T(8,128)}) custom-call(bf16[16,256,1408]{2,1,0:T(8,128)(2,1)} %get-tuple-element.60.p_ref, bf16[3072,1280]{1,0:T(8,128)(2,1)} %get-tuple-element.61.in_ref, bf16[3072,1280]{1,0:T(8,128)(2,1)} %get-tuple-element.62.og_ref, ...), custom_call_target="tpu_custom_call" | custom-call | tf_op jit(solution)/shard_map/scatter_experts/pallas_call | solution.py:831
  437.1 1.2 multiply_reduce_fusion.6
  438.4 2.7 multiply_reduce_fusion.2
  441.1 0.6 broadcast_in_dim.112
  441.7 3.2 copy.63
  445.0 0.4 fusion.res_ref
  445.4 0.7 copy-done.8
  446.1 2.8 convolution_convert_fusion
  448.9 0.6 copy-done.24
  449.5 1.9 convolution_convert_fusion.1.g_ref
  451.4 127.7 %attend_back_sum.1 = (f32[40,3968]{1,0:T(8,128)}, bf16[256,2560]{1,0:T(8,128)(2,1)}, bf16[256,1280]{1,0:T(8,128)(2,1)}) custom-call(bf16[256,1280]{1,0:T(8,128)(2,1)} %get-tuple-element.51.q_ref, bf16[256,1280]{1,0:T(8,128)(2,1)} %convolution_convert_fusion.1.g_ref, f32[10,128,256]{2,1,0:T(8,128)} %get-tuple-element.67.mixed_ref, s32[1,256]{1,0:T(1,128)} %bitcast.72, ...), custom_call_target="tpu_custom_call" | custom-call | tf_op jit(solution)/shard_map/attend_back_sum/pallas_call | solution.py:1342
  579.1 1.7 slice.66
  580.8 1.8 slice_bitcast_fusion
  582.6 1.2 convolution_convert_fusion.2
  583.9 14.4 %finish.1 = (bf16[1280,1280]{1,0:T(8,128)(2,1)}, bf16[1280,1280]{1,0:T(8,128)(2,1)}, bf16[1280,1280]{1,0:T(8,128)(2,1)}, bf16[256,1280]{1,0:T(8,128)(2,1)}, f32[1,1280]{1,0:T(1,128)}) custom-call(bf16[256,1280]{1,0:T(8,128)(2,1)} %bitcast.66, f32[1,1280]{1,0:T(1,128)} %broadcast_in_dim.98.gain_ref, f32[256,1280]{1,0:T(8,128)} %copy-done.6, ...), custom_call_target="tpu_custom_call" | custom-call | flops 5033164800 | bytes 19660800 | tf_op jit(solution)/shard_map/finish/pallas_call | solution.py:1101
  598.3 0.7 convert_bitcast_fusion.1
  599.0 1.8 multiply_reduce_fusion.4
  600.8 2.0 maximum_convert_fusion
  603.0 0.2 copy.66
  603.2 0.8 pad.5.clone
  604.0 64.4 %scatter_whole.1 = f32[40,3968]{1,0:T(8,128)} custom-call(bf16[32,40,1280]{2,1,0:T(8,128)(2,1)} %bitcast.55, bf16[32,40,1280]{2,1,0:T(8,128)(2,1)} %bitcast.56, bf16[32,40,1280]{2,1,0:T(8,128)(2,1)} %bitcast.57, bf16[32,40,128]{2,1,0:T(8,128)(2,1)} %bitcast.64), custom_call_target="tpu_custom_call" | custom-call | tf_op jit(solution)/shard_map/scatter_whole/pallas_call | solution.py:713
  668.4 1.3 sqrt_bitcast_fusion
  669.8 1.5 slice_reduce_fusion
  671.3 2.0 fusion.14
  673.2 0.7 copy.62
  673.9 3.3 copy.74
  677.2 1.4 copy.75
  (73 shorter events, 1.3 us)
Async XLA Ops:
  7.2 234.3 %all-gather.3.cloned.1.call-start = ((), (), s32[]{:S(2)}) async-start(), calls=%async_computation.2 | async-start | bytes 11141120 | tf_op jit(solution)/shard_map/all_gather | solution.py:1405
  19.2 34.9 %copy-start.25 = (s32[1,4]{1,0:T(1,128)S(1)}, s32[1,4]{1,0:T(1,128)}, u32[]{:S(2)}) copy-start(s32[1,4]{1,0:T(1,128)} %param.18) | copy-start | bytes 52
  19.2 38.3 %copy-start.21 = (s32[1,256,7]{1,0,2:T(1,128)S(1)}, s32[1,256,7]{1,0,2:T(1,128)}, u32[]{:S(2)}) copy-start(s32[1,256,7]{1,0,2:T(1,128)} %param.19) | copy-start | bytes 21508
  54.0 529.8 %reduce-scatter.2.cloned.1.call-start = ((), (), s32[]{:S(2)}) async-start(), calls=%async_computation.1 | async-start | bytes 11141120 | tf_op jit(solution)/shard_map/reduce_scatter | solution.py:1438
  54.4 3.9 copy-start.19
  58.3 7.9 %copy-start.11 = (bf16[1,256,1280]{2,1,0:T(8,128)(2,1)S(1)}, bf16[1,256,1280]{2,1,0:T(8,128)(2,1)}, u32[]{:S(2)}) copy-start(bf16[1,256,1280]{2,1,0:T(8,128)(2,1)} %param.17) | copy-start | bytes 1966084
  66.1 3.9 copy-start.14
  70.0 1.2 copy-start
  70.0 1.2 copy-start.22
  70.0 0.8 copy-start.13
  70.0 1.2 copy-start.17
  70.8 1.4 copy-start.3
  438.4 2.7 copy-start.20
  441.7 3.3 copy-start.23
  441.7 3.3 copy-start.1
  441.7 3.3 copy-start.5
  441.7 3.3 copy-start.15
  441.7 3.3 copy-start.18
  445.0 1.1 copy-start.8
  446.1 2.8 copy-start.6
  446.1 3.4 copy-start.24
  579.1 3.5 copy-start.4
  579.1 3.5 copy-start.9
  583.8 15.2 %copy-start.2 = (f32[256,1280]{1,0:T(8,128)S(1)}, f32[256,1280]{1,0:T(8,128)}, u32[]{:S(2)}) copy-start(f32[256,1280]{1,0:T(8,128)} %copy-done) | copy-start | bytes 3932164
  583.9 15.2 %copy-start.10 = (f32[256,1280]{1,0:T(8,128)S(1)}, f32[256,1280]{1,0:T(8,128)}, u32[]{:S(2)}) copy-start(f32[256,1280]{1,0:T(8,128)} %get-tuple-element.55) | copy-start | bytes 3932164
  583.9 15.1 %copy-start.12 = (bf16[1,256,1280]{2,1,0:T(8,128)(2,1)S(1)}, bf16[1,256,1280]{2,1,0:T(8,128)(2,1)}, u32[]{:S(2)}) copy-start(bf16[1,256,1280]{2,1,0:T(8,128)(2,1)} %reduce-scatter.2.cloned.1.call-done) | copy-start | bytes 1966084
  599.0 3.9 copy-start.16
  668.4 4.8 slice-start
  673.9 3.3 copy-start.7
Sparse Core Ops, SparseCore 0:
  54.2 154.2 all-gather.2
  315.2 147.1 reduce-scatter.1

commit v8 on v7

--- a/solution.py
+++ b/solution.py
@@ -1190,6 +1190,246 @@
     )(places, arrived, grads, rank[:, None, :], rank[:, :, None], share[:, None, :], gate, up, down)
 
 
+def gather_attend_kernel(plan, pieces, attention, x_ref, out_ref, ra, sa_up, sa_dn, rb, sb, rc, sc, own):
+    a, b, c = plan.place()
+    steps, wide = plan.steps, plan.wide
+    at = {d: i for i, d in enumerate(steps)}
+    rows = x_ref.shape[0] // pieces
+
+    def part(q):
+        return pl.ds(pl.multiple_of(q * rows, rows), rows)
+
+    def copy(q, src, slot, ssem, rsem, dev):
+        return pltpu.make_async_remote_copy(
+            src_ref=src, dst_ref=out_ref.at[slot, part(q)], send_sem=ssem, recv_sem=rsem,
+            device_id={"ep": dev}, device_id_type=MESH,
+        )
+
+    def hops(d, q):
+        i = at[d]
+        slot = plan.slot(a - d, b, c)
+        src = x_ref.at[part(q)] if d == 0 else out_ref.at[slot, part(q)]
+        real = plan.inside(a - d)
+        out = []
+        if d >= 0 and d + 1 in at:
+            out.append((both(real, a + 1 < plan.long), lambda: copy(
+                q, src, slot, sa_up.at[i, q], ra.at[at[d + 1], q], plan.slot(a + 1, b, c))))
+        if d <= 0 and d - 1 in at:
+            out.append((both(real, a > 0), lambda: copy(
+                q, src, slot, sa_dn.at[i, q], ra.at[at[d - 1], q], plan.slot(a - 1, b, c))))
+        for k in range(1, wide):
+            to = (b + k) % wide
+            out.append((both(real, plan.need_pair(d, to, b)), lambda k=k, to=to: copy(
+                q, src, slot, sb.at[i, k, q], rb.at[i, k, q], plan.slot(a, to, c))))
+        out.append((both(real, plan.need(d, b, 1 - c, b, c)), lambda: copy(
+            q, src, slot, sc.at[i, 0, q], rc.at[i, 0, q], plan.slot(a, b, 1 - c))))
+        return out
+
+    def cross(d, k, q):
+        i = at[d]
+        b0 = (b + wide - k) % wide
+        slot = plan.slot(a - d, b0, c)
+        real = plan.inside(a - d)
+        come = lambda: copy(q, x_ref.at[part(q)], slot, sb.at[i, k, q], rb.at[i, k, q], plan.slot(a, b, c))
+        go = lambda: copy(q, out_ref.at[slot, part(q)], slot, sc.at[i, k, q], rc.at[i, k, q],
+                          plan.slot(a, b, 1 - c))
+        return (both(real, plan.need_pair(d, b, b0)), come,
+                both(real, plan.need(d, b, 1 - c, b0, c)), go)
+
+    plan.greet(a, b, c)
+    keep = pltpu.make_async_copy(x_ref, out_ref.at[plan.slot(a, b, c)], own)
+
+    @pl.loop(0, pieces)
+    def _(q):
+        for cond, go in hops(0, q):
+            @when(cond)
+            def _(go=go):
+                go().start()
+
+    keep.start()
+    far = max(abs(d) for d in steps)
+
+    def arrive(d, k):
+        b0 = (b + wide - k) % wide
+        slot = plan.slot(a - d, b0, 1 - c)
+
+        @pl.loop(0, pieces)
+        def _(q):
+            copy(q, x_ref.at[part(q)], slot, sc.at[at[d], k, q], rc.at[at[d], k, q], plan.slot(a, b, c)).wait_recv()
+
+    work = attention(a, b, c, arrive)
+    work.own()
+    for step in range(1, far + 2):
+        @pl.loop(0, pieces)
+        def _(q, step=step):
+            for d in (step, -step):
+                if d in at:
+                    @when(plan.inside(a - d))
+                    def _(d=d):
+                        slot = plan.slot(a - d, b, c)
+                        copy(q, x_ref.at[part(q)], slot, sa_up.at[0, q], ra.at[at[d], q],
+                             plan.slot(a, b, c)).wait_recv()
+                        for cond, go in hops(d, q):
+                            @when(cond)
+                            def _(go=go):
+                                go().start()
+            for d in (step - 1,):
+                if d in at:
+                    for k in range(1, wide):
+                        came, come, goes, go = cross(d, k, q)
+                        @when(came)
+                        def _(come=come):
+                            come().wait_recv()
+                        @when(goes)
+                        def _(go=go):
+                            go().start()
+            work.beside(step, q)
+
+    work.rest()
+    keep.wait()
+
+    @pl.loop(0, pieces)
+    def _(q):
+        for d in steps:
+            i = at[d]
+            real = plan.inside(a - d)
+            for cond, go in hops(d, q):
+                @when(cond)
+                def _(go=go):
+                    go().wait_send()
+            for k in range(1, wide):
+                came, come, goes, go = cross(d, k, q)
+                @when(goes)
+                def _(go=go):
+                    go().wait_send()
+
+
+class Attention:
+    def __init__(self, plan, a, b, c, arrive, x_ref, pair_ref, q_ref, start_ref, mixed_ref, low_ref, total_ref,
+                 bias, top, norm, kv, kv_sem):
+        self.plan, self.a, self.b, self.c, self.arrive = plan, a, b, c, arrive
+        self.x_ref, self.pair_ref, self.q_ref, self.start_ref = x_ref, pair_ref, q_ref, start_ref
+        self.mixed_ref, self.low_ref, self.total_ref = mixed_ref, low_ref, total_ref
+        self.bias, self.top, self.norm, self.kv, self.kv_sem = bias, top, norm, kv, kv_sem
+        self.turns = [(0, 0, True), (1, 0, False), (1, 0, True), (0, 1, False), (0, 1, True), (2, 0, False), (2, 0, True),
+                      (1, 1, False), (1, 1, True), (2, 1, False), (2, 1, True)]
+
+    def block(self, n):
+        d, k, other = self.turns[n]
+        b0, c0 = (self.b + self.plan.wide - k) % self.plan.wide, 1 - self.c if other else self.c
+        there = both(self.plan.inside(self.a - d), self.plan.need(d, self.b, self.c, b0, c0))
+        return there, self.plan.slot(self.a - d, b0, c0)
+
+    def copy(self, n):
+        return pltpu.make_async_copy(self.pair_ref.at[self.block(n)[1]], self.kv.at[n % 2], self.kv_sem.at[n % 2])
+
+    def fetch(self, n):
+        if n < len(self.turns):
+            d, k, other = self.turns[n]
+
+            def go():
+                if other:
+                    self.arrive(d, k)
+                self.copy(n).start()
+
+            run_if(self.block(n)[0], go)
+
+    def use(self, n):
+        def go():
+            self.copy(n).wait()
+            self.step(self.kv.at[n % 2], self.block(n)[1])
+
+        run_if(self.block(n)[0], go)
+
+    def step(self, pair, slot):
+        rows = self.q_ref.shape[0]
+        me = self.plan.slot(self.a, self.b, self.c)
+        self.bias[...] = visible_bias((rows, rows), slot * rows, self.start_ref[...], me * rows)
+
+        @pl.loop(0, HEADS)
+        def _(h):
+            keys, values = pair[:, lanes(2 * h * HEAD)], pair[:, lanes((2 * h + 1) * HEAD)]
+            scores = inner_right(keys, self.q_ref[:, lanes(h * HEAD)]) + self.bias[...]
+            old = self.top[h]
+            new = jnp.maximum(old, jnp.max(scores, axis=0, keepdims=True))
+            weights = jnp.exp(scores - new)
+            shrink = jnp.exp(old - new)
+            self.top[h] = new
+            self.norm[h] = self.norm[h] * shrink + jnp.sum(weights, axis=0, keepdims=True)
+            self.mixed_ref[h] = self.mixed_ref[h] * shrink + inner_left(values, weights.astype(jnp.bfloat16))
+
+    def own(self):
+        self.top[...] = jnp.full_like(self.top, masked_value)
+        self.norm[...] = jnp.zeros_like(self.norm)
+        self.mixed_ref[...] = jnp.zeros_like(self.mixed_ref)
+        self.step(self.x_ref, self.plan.slot(self.a, self.b, self.c))
+        self.fetch(0)
+        self.use(0)
+
+    def beside(self, step, q):
+        if step == 1:
+            return
+        if step == 2:
+            run_if(q == 0, lambda: self.fetch(1))
+        first = 4 * step - 7
+        for i in range(4):
+            def go(n=first + i):
+                self.fetch(n + 1)
+                self.use(n)
+
+            run_if(q == 2 * i + 1, go)
+
+    def rest(self):
+        self.fetch(10)
+        self.use(9)
+        self.use(10)
+        for h in range(HEADS):
+            mixed = self.mixed_ref[h] / self.norm[h]
+            self.mixed_ref[h] = mixed
+            self.low_ref[:, h * HEAD : (h + 1) * HEAD] = mixed.T.astype(jnp.bfloat16)
+            self.total_ref[h] = self.top[h] + jnp.log(self.norm[h])
+
+
+def gather_attend(block, queries, start, collective_id):
+    ep_count, pieces = lax.axis_size("ep"), 8
+    plan = Plan(ep_count, True)
+    n, wide = len(plan.steps), plan.wide
+    rows, width = queries.shape
+    sem = pltpu.SemaphoreType.DMA
+
+    def kernel(x_ref, q_ref, start_ref, out_ref, mixed_ref, low_ref, total_ref, bias, top, norm, kv, kv_sem, *sems):
+        def attention(a, b, c, arrive):
+            return Attention(plan, a, b, c, arrive, x_ref, out_ref, q_ref, start_ref, mixed_ref, low_ref, total_ref,
+                             bias, top, norm, kv, kv_sem)
+
+        gather_attend_kernel(plan, pieces, attention, x_ref, out_ref, *sems)
+
+    near = pl.BlockSpec(memory_space=pltpu.VMEM)
+    return pl.pallas_call(
+        kernel,
+        out_shape=(
+            jax.ShapeDtypeStruct((ep_count,) + block.shape, block.dtype),
+            jax.ShapeDtypeStruct((HEADS, HEAD, rows), jnp.float32),
+            jax.ShapeDtypeStruct((rows, width), jnp.bfloat16),
+            jax.ShapeDtypeStruct((HEADS, 1, rows), jnp.float32),
+        ),
+        in_specs=[near] * 3,
+        out_specs=(pl.BlockSpec(memory_space=pl.ANY), near, near, near),
+        scratch_shapes=[
+            pltpu.VMEM((rows, rows), jnp.float32),
+            pltpu.VMEM((HEADS, 1, rows), jnp.float32),
+            pltpu.VMEM((HEADS, 1, rows), jnp.float32),
+            pltpu.VMEM((2,) + block.shape, block.dtype),
+            sem((2,)),
+            sem((n, pieces)), sem((n, pieces)), sem((n, pieces)), sem((n, wide, pieces)),
+            sem((n, wide, pieces)), sem((n, wide, pieces)), sem((n, wide, pieces)), sem,
+        ],
+        compiler_params=pltpu.CompilerParams(
+            collective_id=collective_id, has_side_effects=True, vmem_limit_bytes=VMEM_MOST),
+        name="gather_attend",
+    )(block, queries, start)
+
+
 def attend_back_sum(queries, grads, mixed, start, total, cosine, sine, pairs, parts, collective_id):
     rows, width = queries.shape
     ep_count = pairs.shape[0]
@@ -1238,7 +1478,7 @@
                 fetch(turn, other)[1]().wait()
                 bias[...] = visible_bias((rows, rows), slot * rows, start_ref[...], me * rows)
 
-                @pl.loop(0, HEADS, unroll=2)
+                @pl.loop(0, HEADS)
                 def _(h):
                     early, late, at = lanes(2 * h * HEAD), lanes((2 * h + 1) * HEAD), lanes(h * HEAD)
                     keys, values = kv[held, :, early], kv[held, :, late]
@@ -1400,10 +1640,13 @@
     hidden_low, queries, own_pairs = project(
         tokens[0], mixer_gain, cosine, sine, query_weight, key_weight, value_weight
     )
-    pairs = gather_rows(own_pairs, True, 1, 8)
+    if ep_count > 16:
+        pairs = gather_rows(own_pairs, True, 1, 8)
+        mixed, mixed_low, log_total = attend(info, queries, start[None, :], pairs)
+    else:
+        pairs, mixed, mixed_low, log_total = gather_attend(own_pairs, queries, start[None, :], 1)
     grad_later, pairs = lax.optimization_barrier((grad_low, pairs))
     grads_all = lax.all_gather(grad_later, "ep", axis=0, tiled=False)
-    mixed, mixed_low, log_total = attend(info, queries, start[None, :], pairs)
     mixer_out = dot(mixed_low, output_weight)
     residual = stream + mixer_out
     ffn_low = low(normed(residual, ffn_gain))

time: 699 us -> 716 us (1.024); the launches traced: 686 us -> 712 us
  Pallas kernels: 615 us -> 643 us
    pallas_call x1, Pallas kernels: 128 us -> 144 us  [attend_back_sum(): pl.pallas_call(kernel, out_shape=(jax.ShapeDtypeStruct((part_rows, part_w...]
    pallas_call x1, Pallas kernels: 162 us -> 174 us  [gather_shared(): pl.pallas_call(kernel, out_shape=(jax.ShapeDtypeStruct((ep_count,) + bloc...]
    pallas_call x2 -> x1, Pallas kernels: 42.7 us -> 36.2 us  [gather_attend(): pl.pallas_call(kernel, out_shape=(jax.ShapeDtypeStruct((ep_count,) + bloc...]
  transfers between devices with their start and end apart: 2 -> 2, of which waited for: 0 -> 0; matrix products, arithmetic and copies ran while one was open for 5% -> 4% of each run, Pallas kernels for 61% -> 63%
where the time goes in v8:
time: 716 us; the launch traced here: 712 us
  Pallas kernels  643 us (90%)
  local copies, waits for them, and re-layouts  25.6 us (4%)
  other arithmetic  15.1 us (2%)
  between operations  14.8 us (2%)
  matrix products  13.2 us (2%)
    pallas_call x1, Pallas kernels, gather_shared(): pl.pallas_call(kernel, out_shape=(jax.ShapeDtypeStruct((ep_count,) + bloc...  174 us
    pallas_call x1, Pallas kernels, attend_back_sum(): pl.pallas_call(kernel, out_shape=(jax.ShapeDtypeStruct((part_rows, part_w...  144 us
    pallas_call x1, Pallas kernels, scatter_experts(): pl.pallas_call(kernel, out_shape=tuple(outs), in_specs=[anywhere] * 6, ou...  127 us
    pallas_call x1, Pallas kernels, run_experts(): pl.pallas_call(experts_kernel, out_shape=(shape(count, rows, side), shape...  73.5 us
    pallas_call x1, Pallas kernels, scatter_whole(): pl.pallas_call(kernel, out_shape=tuple(out_shape), in_specs=[anywhere] *...  64.1 us
    pallas_call x1, Pallas kernels, gather_attend(): pl.pallas_call(kernel, out_shape=(jax.ShapeDtypeStruct((ep_count,) + bloc...  36.2 us
    pallas_call x1, Pallas kernels, finish(): pl.pallas_call(finish_kernel, out_shape=(jax.ShapeDtypeStruct((width, wid...  14.4 us
  transfers between devices with their start and end apart: 2, of which 0 were waited for; matrix products, arithmetic and copies ran while one was open for 4% of the time, Pallas kernels for 63%

profile of v8, /device:TPU:0, one launch (start us, length us, event | category | flops | bytes accessed | tf_op | source)
XLA Modules:
  0.0 711.6 jit_solution(14287007349162361028)
XLA Ops:
  7.3 1.3 broadcast_in_dim.97.gain_ref
  8.6 0.5 fusion.7
  9.1 0.8 pad_maximum_fusion.cos_ref
  9.9 0.8 reduce-window.8
  10.7 0.6 select_reduce_fusion.1
  11.3 0.8 pad_maximum_fusion.1.sin_ref
  12.1 8.6 %project.1 = (bf16[256,1280]{1,0:T(8,128)(2,1)}, bf16[256,1280]{1,0:T(8,128)(2,1)}, bf16[256,2560]{1,0:T(8,128)(2,1)}) custom-call(bf16[256,1280]{1,0:T(8,128)(2,1)} %bitcast.63, f32[1,1280]{1,0:T(1,128)} %broadcast_in_dim.97.gain_ref, f32[256,128]{1,0:T(8,128)} %pad_maximum_fusion.cos_ref, f32[256,128]{1,0:T(8,128)} %pad_maximum_fusion.1.sin_ref, ...), custom_call_target="tpu_custom_call" | custom-call | flops 2516582400 | bytes 9830400 | tf_op jit(solution)/shard_map/project/pallas_call | solution.py:890
  20.7 36.2 %gather_attend.1 = (bf16[16,256,2560]{2,1,0:T(8,128)(2,1)}, f32[10,128,256]{2,1,0:T(8,128)}, bf16[256,1280]{1,0:T(8,128)(2,1)}, f32[10,1,256]{2,1,0:T(1,128)}) custom-call(bf16[256,2560]{1,0:T(8,128)(2,1)} %get-tuple-element.52.x_ref, bf16[256,1280]{1,0:T(8,128)(2,1)} %get-tuple-element.53.q_ref, s32[1,256]{1,0:T(1,128)} %bitcast.69), custom_call_target="tpu_custom_call" | custom-call | tf_op jit(solution)/shard_map/gather_attend/pallas_call | solution.py:1408
  57.0 0.7 copy.68
  57.9 4.0 multiply_reduce_fusion.5
  62.1 0.6 copy-done.12
  62.7 0.4 fusion.15
  63.3 0.8 subtract_convert_fusion
  64.1 1.0 concatenate.15.x_ref
  65.1 174.4 %gather_shared.1 = (bf16[16,256,1408]{2,1,0:T(8,128)(2,1)}, f32[256,1280]{1,0:T(8,128)}, f32[256,1280]{1,0:T(8,128)}, bf16[1280,896]{1,0:T(8,128)(2,1)}, bf16[12...) custom-call(bf16[256,1408]{1,0:T(8,128)(2,1)} %concatenate.15.x_ref, bf16[256,1280]{1,0:T(8,128)(2,1)} %bitcast.52, ...), custom_call_target="tpu_custom_call" | custom-call | tf_op jit(solution)/shard_map/gather_shared/pallas_call | solution.py:294
  239.6 2.5 select_reduce_fusion
  242.0 0.6 broadcast_in_dim.108.share_row
  242.8 0.6 copy.59.rank_row
  243.4 2.0 copy.60.rank_col
  245.4 0.6 pad_add_fusion.where_ref
  246.0 73.5 %run_experts.1 = (bf16[16,256,1408]{2,1,0:T(8,128)(2,1)}, bf16[16,256,1280]{2,1,0:T(8,128)(2,1)}, bf16[3072,1280]{1,0:T(8,128)(2,1)}, bf16[3072,896]{1,0:T(8,128...) custom-call(s32[2]{0:T(128)} %pad_add_fusion.where_ref, ...), custom_call_target="tpu_custom_call" | custom-call | flops 56371445760 | bytes 62914560 | tf_op jit(solution)/shard_map/run_experts/pallas_call | solution.py:1175
  319.5 127.3 %scatter_experts.1 = (bf16[256,1408]{1,0:T(8,128)(2,1)}, f32[640,896]{1,0:T(8,128)}, f32[640,896]{1,0:T(8,128)}, f32[640,896]{1,0:T(8,128)}) custom-call(bf16[16,256,1408]{2,1,0:T(8,128)(2,1)} %get-tuple-element.61.p_ref, bf16[3072,1280]{1,0:T(8,128)(2,1)} %get-tuple-element.62.in_ref, bf16[3072,1280]{1,0:T(8,128)(2,1)} %get-tuple-element.63.og_ref, ...), custom_call_target="tpu_custom_call" | custom-call | tf_op jit(solution)/shard_map/scatter_experts/pallas_call | solution.py:831
  446.8 1.1 multiply_reduce_fusion.6
  448.0 2.7 multiply_reduce_fusion.2
  450.7 0.6 broadcast_in_dim.112
  451.3 3.2 copy.63
  454.6 0.4 fusion.res_ref
  455.0 0.7 copy-done.8
  455.7 2.8 convolution_convert_fusion
  458.5 0.6 copy-done.21
  459.1 1.9 convolution_convert_fusion.1.g_ref
  461.0 144.1 %attend_back_sum.1 = (f32[40,3968]{1,0:T(8,128)}, bf16[256,2560]{1,0:T(8,128)(2,1)}, bf16[256,1280]{1,0:T(8,128)(2,1)}) custom-call(bf16[256,1280]{1,0:T(8,128)(2,1)} %get-tuple-element.53.q_ref, bf16[256,1280]{1,0:T(8,128)(2,1)} %convolution_convert_fusion.1.g_ref, f32[10,128,256]{2,1,0:T(8,128)} %get-tuple-element.68.mixed_ref, s32[1,256]{1,0:T(1,128)} %bitcast.70, ...), custom_call_target="tpu_custom_call" | custom-call | tf_op jit(solution)/shard_map/attend_back_sum/pallas_call | solution.py:1582
  605.1 1.7 slice.62
  606.8 1.8 slice_bitcast_fusion
  608.6 1.2 convolution_convert_fusion.2
  609.9 14.4 %finish.1 = (bf16[1280,1280]{1,0:T(8,128)(2,1)}, bf16[1280,1280]{1,0:T(8,128)(2,1)}, bf16[1280,1280]{1,0:T(8,128)(2,1)}, bf16[256,1280]{1,0:T(8,128)(2,1)}, f32[1,1280]{1,0:T(1,128)}) custom-call(bf16[256,1280]{1,0:T(8,128)(2,1)} %bitcast.64, f32[1,1280]{1,0:T(1,128)} %broadcast_in_dim.97.gain_ref, f32[256,1280]{1,0:T(8,128)} %copy-done.6, ...), custom_call_target="tpu_custom_call" | custom-call | flops 5033164800 | bytes 19660800 | tf_op jit(solution)/shard_map/finish/pallas_call | solution.py:1101
  624.3 0.7 convert_bitcast_fusion.1
  625.0 1.8 multiply_reduce_fusion.4
  626.8 2.0 maximum_convert_fusion
  628.9 0.2 copy.66
  629.2 0.8 pad.5.clone
  630.0 64.1 %scatter_whole.1 = f32[40,3968]{1,0:T(8,128)} custom-call(bf16[32,40,1280]{2,1,0:T(8,128)(2,1)} %bitcast.53, bf16[32,40,1280]{2,1,0:T(8,128)(2,1)} %bitcast.54, bf16[32,40,1280]{2,1,0:T(8,128)(2,1)} %bitcast.55, bf16[32,40,128]{2,1,0:T(8,128)(2,1)} %bitcast.62), custom_call_target="tpu_custom_call" | custom-call | tf_op jit(solution)/shard_map/scatter_whole/pallas_call | solution.py:713
  694.1 1.3 sqrt_bitcast_fusion
  695.5 1.5 slice_reduce_fusion
  697.0 2.0 fusion.14
  698.9 0.7 copy.62
  699.6 3.3 copy.74
  702.9 1.4 copy.75
  (62 shorter events, 1.1 us)
Async XLA Ops:
  7.2 238.8 %all-gather.3.cloned.1.call-start = ((), (), s32[]{:S(2)}) async-start(), calls=%async_computation.2 | async-start | bytes 11141120 | tf_op jit(solution)/shard_map/all_gather | solution.py:1649
  57.0 552.9 %reduce-scatter.2.cloned.1.call-start = ((), (), s32[]{:S(2)}) async-start(), calls=%async_computation.1 | async-start | bytes 11141120 | tf_op jit(solution)/shard_map/reduce_scatter | solution.py:1681
  57.9 4.0 copy-start.13
  61.9 1.2 copy-start
  61.9 1.2 copy-start.19
  61.9 0.8 copy-start.12
  61.9 1.2 copy-start.16
  62.7 1.4 copy-start.3
  447.9 2.7 copy-start.18
  451.3 3.3 copy-start.20
  451.3 3.3 copy-start.1
  451.3 3.3 copy-start.5
  451.3 3.3 copy-start.14
  451.3 3.3 copy-start.17
  454.6 1.1 copy-start.8
  455.7 2.8 copy-start.6
  455.7 3.4 copy-start.21
  605.1 3.5 copy-start.4
  605.1 3.5 copy-start.9
  609.8 15.1 %copy-start.2 = (f32[256,1280]{1,0:T(8,128)S(1)}, f32[256,1280]{1,0:T(8,128)}, u32[]{:S(2)}) copy-start(f32[256,1280]{1,0:T(8,128)} %copy-done) | copy-start | bytes 3932164
  609.8 15.1 %copy-start.10 = (f32[256,1280]{1,0:T(8,128)S(1)}, f32[256,1280]{1,0:T(8,128)}, u32[]{:S(2)}) copy-start(f32[256,1280]{1,0:T(8,128)} %get-tuple-element.55) | copy-start | bytes 3932164
  609.9 15.1 %copy-start.11 = (bf16[1,256,1280]{2,1,0:T(8,128)(2,1)S(1)}, bf16[1,256,1280]{2,1,0:T(8,128)(2,1)}, u32[]{:S(2)}) copy-start(bf16[1,256,1280]{2,1,0:T(8,128)(2,1)} %reduce-scatter.2.cloned.1.call-done) | copy-start | bytes 1966084
  625.0 3.9 copy-start.15
  694.1 4.8 slice-start
  699.6 3.3 copy-start.7
Sparse Core Ops, SparseCore 0:
  57.1 181.6 all-gather.2
  319.6 145.8 reduce-scatter.1

commit v9 on v8

--- a/solution.py
+++ b/solution.py
@@ -119,7 +119,7 @@
         pl.semaphore_wait(barrier, self.wide + 2 - ends)
 
 
-def gather_kernel(plan, pieces, beside, x_ref, out_ref, ra, sa_up, sa_dn, rb, sb, rc, sc, own):
+def gather_steps(plan, pieces, beside, greet, x_ref, out_ref, ra, sa_up, sa_dn, rb, sb, rc, sc, own):
     a, b, c = plan.place()
     steps, wide = plan.steps, plan.wide
     at = {d: i for i, d in enumerate(steps)}
@@ -165,7 +165,8 @@
         return (both(real, plan.need_pair(d, b, b0)), come,
                 both(real, plan.need(d, b, 1 - c, b0, c)), go)
 
-    plan.greet(a, b, c)
+    if greet:
+        plan.greet(a, b, c)
     keep = pltpu.make_async_copy(x_ref, out_ref.at[plan.slot(a, b, c)], own)
 
     @pl.loop(0, pieces)
@@ -176,6 +177,7 @@
                 go().start()
 
     keep.start()
+    yield
     far = max(abs(d) for d in steps)
     for step in range(1, far + 3):
         beside(step - 1)
@@ -228,6 +230,11 @@
                     go().wait_send()
 
 
+def gather_kernel(plan, pieces, beside, *refs):
+    for _ in gather_steps(plan, pieces, beside, True, *refs):
+        pass
+
+
 def gather_rows(block, window, collective_id, pieces=4):
     ep_count = lax.axis_size("ep")
     plan = Plan(ep_count, window)
@@ -731,7 +738,7 @@
     plan, pieces = Plan(ep_count, False), 4
     place = Place(lax.axis_size("grp"), ep_count)
     left_of = [0, 0, 1]
-    hooks = (4, 5, 6, 7, 10, 11, 12, 13, 16, 17)
+    hooks = (12, 13, 14, 15)
     kinds, units = len(rights), 2 * len(rights)
     steps = units * 3
 
@@ -1120,7 +1127,7 @@
 
 def experts_kernel(
     where_ref, x_ref, g_ref, rank_row, rank_col, share_row, wg_ref, wu_ref, wd_ref,
-    back_ref, routed_ref, in_ref, pre_ref, lift_ref, mid_ref, og_ref, grads,
+    back_ref, in_ref, pre_ref, lift_ref, mid_ref, og_ref, grads,
 ):
     blocks, rows, side = x_ref.shape
     capacity = in_ref.shape[0] // blocks
@@ -1159,8 +1166,8 @@
         hit = rank_col[i] == lax.broadcasted_iota(jnp.int32, (rows, capacity), 1)
         put = jnp.where(hit, 1.0, 0.0).astype(jnp.bfloat16)
         back_ref[i, :, :width] = dot(put, in_grad[at, :]).astype(jnp.bfloat16)
-        back_ref[i, :, width:] = dot(put, extra[at, :]).astype(jnp.bfloat16)
-        routed_ref[i] = dot(put, given[at, :]).astype(jnp.bfloat16)
+        back_ref[i, :, width:side] = dot(put, extra[at, :]).astype(jnp.bfloat16)
+        back_ref[i, :, side:] = dot(put, given[at, :]).astype(jnp.bfloat16)
 
 
 def run_experts(places, arrived, grads, rank, share, gate, up, down, capacity):
@@ -1174,14 +1181,14 @@
     shape = lambda *dims: jax.ShapeDtypeStruct(dims, jnp.bfloat16)
     return pl.pallas_call(
         experts_kernel,
-        out_shape=(shape(count, rows, side), shape(count, rows, width), shape(flat, width), shape(flat, ff),
+        out_shape=(shape(count, rows, side + width), shape(flat, width), shape(flat, ff),
                    shape(flat, ff), shape(flat, ff), shape(flat, width)),
         grid_spec=pltpu.PrefetchScalarGridSpec(
             num_scalar_prefetch=1,
             grid=(count // blocks,),
             in_specs=[lead(rows, side), lead(rows, width), lead(1, rows), lead(rows, 1), lead(1, rows),
                       once(1, width, ff), once(1, width, ff), once(1, ff, width)],
-            out_specs=(lead(rows, side), lead(rows, width), tall(width), tall(ff), tall(ff), tall(ff), tall(width)),
+            out_specs=(lead(rows, side + width), tall(width), tall(ff), tall(ff), tall(ff), tall(width)),
             scratch_shapes=[pltpu.VMEM((blocks * capacity, width), jnp.bfloat16)],
         ),
         compiler_params=pltpu.CompilerParams(vmem_limit_bytes=VMEM_MOST),
@@ -1190,7 +1197,7 @@
     )(places, arrived, grads, rank[:, None, :], rank[:, :, None], share[:, None, :], gate, up, down)
 
 
-def gather_attend_kernel(plan, pieces, attention, x_ref, out_ref, ra, sa_up, sa_dn, rb, sb, rc, sc, own):
+def gather_attend_steps(plan, pieces, attention, x_ref, out_ref, ra, sa_up, sa_dn, rb, sb, rc, sc, own):
     a, b, c = plan.place()
     steps, wide = plan.steps, plan.wide
     at = {d: i for i, d in enumerate(steps)}
@@ -1247,6 +1254,7 @@
                 go().start()
 
     keep.start()
+    yield
     far = max(abs(d) for d in steps)
 
     def arrive(d, k):
@@ -1390,44 +1398,51 @@
             self.total_ref[h] = self.top[h] + jnp.log(self.norm[h])
 
 
-def gather_attend(block, queries, start, collective_id):
+def gather_attend(block, grads, queries, start, collective_id):
     ep_count, pieces = lax.axis_size("ep"), 8
-    plan = Plan(ep_count, True)
-    n, wide = len(plan.steps), plan.wide
+    plan, other = Plan(ep_count, True), Plan(ep_count, False)
+    n, wide, more = len(plan.steps), plan.wide, len(other.steps)
     rows, width = queries.shape
     sem = pltpu.SemaphoreType.DMA
-
-    def kernel(x_ref, q_ref, start_ref, out_ref, mixed_ref, low_ref, total_ref, bias, top, norm, kv, kv_sem, *sems):
+    sems_of = lambda n, pieces: [sem((n, pieces))] * 3 + [sem((n, wide, pieces))] * 4 + [sem]
+
+    def kernel(x_ref, g_ref, q_ref, start_ref, out_ref, all_ref, mixed_ref, low_ref, total_ref, bias, top, norm, kv,
+               kv_sem, *sems):
         def attention(a, b, c, arrive):
             return Attention(plan, a, b, c, arrive, x_ref, out_ref, q_ref, start_ref, mixed_ref, low_ref, total_ref,
                              bias, top, norm, kv, kv_sem)
 
-        gather_attend_kernel(plan, pieces, attention, x_ref, out_ref, *sems)
+        keys = gather_attend_steps(plan, pieces, attention, x_ref, out_ref, *sems[:8])
+        rest = gather_steps(other, 4, lambda n: None, False, g_ref, all_ref, *sems[8:])
+        next(keys)
+        next(rest)
+        for part in (keys, rest):
+            for _ in part:
+                pass
 
     near = pl.BlockSpec(memory_space=pltpu.VMEM)
     return pl.pallas_call(
         kernel,
         out_shape=(
             jax.ShapeDtypeStruct((ep_count,) + block.shape, block.dtype),
+            jax.ShapeDtypeStruct((ep_count,) + grads.shape, grads.dtype),
             jax.ShapeDtypeStruct((HEADS, HEAD, rows), jnp.float32),
             jax.ShapeDtypeStruct((rows, width), jnp.bfloat16),
             jax.ShapeDtypeStruct((HEADS, 1, rows), jnp.float32),
         ),
-        in_specs=[near] * 3,
-        out_specs=(pl.BlockSpec(memory_space=pl.ANY), near, near, near),
+        in_specs=[near] * 4,
+        out_specs=(pl.BlockSpec(memory_space=pl.ANY), pl.BlockSpec(memory_space=pl.ANY), near, near, near),
         scratch_shapes=[
             pltpu.VMEM((rows, rows), jnp.float32),
             pltpu.VMEM((HEADS, 1, rows), jnp.float32),
             pltpu.VMEM((HEADS, 1, rows), jnp.float32),
             pltpu.VMEM((2,) + block.shape, block.dtype),
             sem((2,)),
-            sem((n, pieces)), sem((n, pieces)), sem((n, pieces)), sem((n, wide, pieces)),
-            sem((n, wide, pieces)), sem((n, wide, pieces)), sem((n, wide, pieces)), sem,
-        ],
+        ] + sems_of(n, pieces) + sems_of(more, 4),
         compiler_params=pltpu.CompilerParams(
             collective_id=collective_id, has_side_effects=True, vmem_limit_bytes=VMEM_MOST),
         name="gather_attend",
-    )(block, queries, start)
+    )(block, grads, queries, start)
 
 
 def attend_back_sum(queries, grads, mixed, start, total, cosine, sine, pairs, parts, collective_id):
@@ -1643,10 +1658,10 @@
     if ep_count > 16:
         pairs = gather_rows(own_pairs, True, 1, 8)
         mixed, mixed_low, log_total = attend(info, queries, start[None, :], pairs)
+        grad_later, pairs = lax.optimization_barrier((grad_low, pairs))
+        grads_all = lax.all_gather(grad_later, "ep", axis=0, tiled=False)
     else:
-        pairs, mixed, mixed_low, log_total = gather_attend(own_pairs, queries, start[None, :], 1)
-    grad_later, pairs = lax.optimization_barrier((grad_low, pairs))
-    grads_all = lax.all_gather(grad_later, "ep", axis=0, tiled=False)
+        pairs, grads_all, mixed, mixed_low, log_total = gather_attend(own_pairs, grad_low, queries, start[None, :], 1)
     mixer_out = dot(mixed_low, output_weight)
     residual = stream + mixer_out
     ffn_low = low(normed(residual, ffn_gain))
@@ -1675,18 +1690,19 @@
     rank = dot(low(chosen), earlier).astype(jnp.int32)
     rank = jnp.where(chosen, rank, -1)
     places = jnp.stack([ep_index, expert_count + ep_index]).astype(jnp.int32)
-    back, given, flat_in, pre_grad, lift_grad, middle, result_grad = run_experts(
+    back, flat_in, pre_grad, lift_grad, middle, result_grad = run_experts(
         places, arrived, grads_all, rank, share, expert_gate, expert_up, expert_down, capacity
     )
-    routed = lax.psum_scatter(given, "ep", scatter_dimension=0)
     group_count = lax.axis_size("grp")
     if group_count == 2:
         back_sum, gate_sum, up_sum, down_sum = scatter_experts(
             back, (flat_in, result_grad), (pre_grad, lift_grad, middle), 3
         )
         gate_sum, up_sum, down_sum = gate_sum[None], up_sum[None], down_sum.T[None]
+        routed = back_sum[:, side:]
     else:
-        back_sum = scatter_rows(back, False, 3)
+        back_sum = scatter_rows(back[:, :, :side], False, 3)
+        routed = lax.psum_scatter(back[:, :, side:], "ep", scatter_dimension=0)
         split = width // group_count
         own_down_grad = jnp.concatenate(
             [low(inner_left(middle, result_grad[:, i * split : (i + 1) * split])) for i in range(group_count)], axis=0

time: 716 us -> 745 us (1.041)
  Pallas kernels: 643 us -> 677 us
  between operations: 14.8 us -> 1.35 us
    pallas_call x1, Pallas kernels: 36.2 us -> 136 us  [gather_attend(): pl.pallas_call(kernel, out_shape=(jax.ShapeDtypeStruct((ep_count,) + bloc...]
    pallas_call x1, Pallas kernels: 174 us -> 86 us  [gather_shared(): pl.pallas_call(kernel, out_shape=(jax.ShapeDtypeStruct((ep_count,) + bloc...]
    pallas_call x1, Pallas kernels: 127 us -> 160 us  [scatter_experts(): pl.pallas_call(kernel, out_shape=tuple(outs), in_specs=[anywhere] * 6, ou...]
    pallas_call x1, Pallas kernels: 144 us -> 134 us  [attend_back_sum(): pl.pallas_call(kernel, out_shape=(jax.ShapeDtypeStruct((part_rows, part_w...]
  transfers between devices with their start and end apart: 2 -> 0, of which waited for: 0 -> 0; matrix products, arithmetic and copies ran while one was open for 4% -> 0% of each run, Pallas kernels for 63% -> 0%
where the time goes in v9:
time: 745 us; the launch traced here: 736 us
  Pallas kernels  677 us (91%)
  local copies, waits for them, and re-layouts  26.4 us (4%)
  other arithmetic  17.8 us (2%)
  matrix products  14.1 us (2%)
    pallas_call x1, Pallas kernels, scatter_experts(): pl.pallas_call(kernel, out_shape=tuple(outs), in_specs=[anywhere] * 6, ou...  160 us
    pallas_call x1, Pallas kernels, gather_attend(): pl.pallas_call(kernel, out_shape=(jax.ShapeDtypeStruct((ep_count,) + bloc...  136 us
    pallas_call x1, Pallas kernels, attend_back_sum(): pl.pallas_call(kernel, out_shape=(jax.ShapeDtypeStruct((part_rows, part_w...  134 us
    pallas_call x1, Pallas kernels, gather_shared(): pl.pallas_call(kernel, out_shape=(jax.ShapeDtypeStruct((ep_count,) + bloc...  86 us
    pallas_call x1, Pallas kernels, run_experts(): pl.pallas_call(experts_kernel, out_shape=(shape(count, rows, side + width...  73.2 us
    pallas_call x1, Pallas kernels, scatter_whole(): pl.pallas_call(kernel, out_shape=tuple(out_shape), in_specs=[anywhere] *...  64.4 us

profile of v9, /device:TPU:0, one launch (start us, length us, event | category | flops | bytes accessed | tf_op | source)
XLA Modules:
  0.0 736.3 jit_solution(1297616996477474991)
XLA Ops:
  0.6 0.6 pad_add_fusion.where_ref
  1.2 0.8 reduce-window.8
  2.1 0.5 iota_compare_fusion.3
  2.6 0.7 select_reduce_fusion.1
  3.2 1.3 broadcast_in_dim.97.gain_ref
  4.5 0.7 copy.68
  5.3 0.7 copy.57
  6.0 0.5 fusion.7
  6.5 0.8 pad_maximum_fusion.1.sin_ref
  7.3 0.8 pad_maximum_fusion.cos_ref
  8.0 8.7 %project.1 = (bf16[256,1280]{1,0:T(8,128)(2,1)}, bf16[256,1280]{1,0:T(8,128)(2,1)}, bf16[256,2560]{1,0:T(8,128)(2,1)}) custom-call(bf16[256,1280]{1,0:T(8,128)(2,1)} %bitcast.61, f32[1,1280]{1,0:T(1,128)} %broadcast_in_dim.97.gain_ref, f32[256,128]{1,0:T(8,128)} %pad_maximum_fusion.cos_ref, f32[256,128]{1,0:T(8,128)} %pad_maximum_fusion.1.sin_ref, ...), custom_call_target="tpu_custom_call" | custom-call | flops 2516582400 | bytes 9830400 | tf_op jit(solution)/shard_map/project/pallas_call | solution.py:897
  16.7 136.2 %gather_attend.1 = (bf16[16,256,2560]{2,1,0:T(8,128)(2,1)}, bf16[16,256,1280]{2,1,0:T(8,128)(2,1)}, f32[10,128,256]{2,1,0:T(8,128)}, bf16[256,1280]{1,0:T(8,128)(2,1)}, f32[10,1,256]{2,1,0:T(1,128)}) custom-call(bf16[256,2560]{1,0:T(8,128)(2,1)} %get-tuple-element.50.x_ref, bf16[256,1280]{1,0:T(8,128)(2,1)} %bitcast.49, ...), custom_call_target="tpu_custom_call" | custom-call | tf_op jit(solution)/shard_map/gather_attend/pallas_call | solution.py:1424
  152.9 4.0 multiply_reduce_fusion.5
  157.1 0.5 copy-done.8
  157.8 0.4 fusion.15
  158.4 0.8 subtract_convert_fusion
  159.2 1.0 concatenate.15.x_ref
  160.2 86.0 %gather_shared.1 = (bf16[16,256,1408]{2,1,0:T(8,128)(2,1)}, f32[256,1280]{1,0:T(8,128)}, f32[256,1280]{1,0:T(8,128)}, bf16[1280,896]{1,0:T(8,128)(2,1)}, bf16[12...) custom-call(bf16[256,1408]{1,0:T(8,128)(2,1)} %concatenate.15.x_ref, bf16[256,1280]{1,0:T(8,128)(2,1)} %bitcast.50, ...), custom_call_target="tpu_custom_call" | custom-call | tf_op jit(solution)/shard_map/gather_shared/pallas_call | solution.py:301
  246.3 2.6 select_reduce_fusion
  249.0 0.6 broadcast_in_dim.108.share_row
  249.6 0.6 copy.59.rank_row
  250.3 2.0 copy.60.rank_col
  252.2 73.2 %run_experts.1 = (bf16[16,256,2688]{2,1,0:T(8,128)(2,1)}, bf16[3072,1280]{1,0:T(8,128)(2,1)}, bf16[3072,896]{1,0:T(8,128)(2,1)}, bf16[3072,896]{1,0:T(8,128)(2,1...) custom-call(s32[2]{0:T(128)} %pad_add_fusion.where_ref, bf16[16,256,1408]{2,1,0:T(8,128)(2,1)} %get-tuple-element.54.x_ref, ...), custom_call_target="tpu_custom_call" | custom-call | flops 56371445760 | bytes 62914560 | tf_op jit(solution)/shard_map/run_experts/pallas_call | solution.py:1182
  325.4 159.9 %scatter_experts.1 = (bf16[256,2688]{1,0:T(8,128)(2,1)}, f32[640,896]{1,0:T(8,128)}, f32[640,896]{1,0:T(8,128)}, f32[640,896]{1,0:T(8,128)}) custom-call(bf16[16,256,2688]{2,1,0:T(8,128)(2,1)} %get-tuple-element.56.p_ref, bf16[3072,1280]{1,0:T(8,128)(2,1)} %get-tuple-element.57.in_ref, bf16[3072,1280]{1,0:T(8,128)(2,1)} %get-tuple-element.58.og_ref, ...), custom_call_target="tpu_custom_call" | custom-call | tf_op jit(solution)/shard_map/scatter_experts/pallas_call | solution.py:838
  485.3 1.1 multiply_reduce_fusion.6
  486.5 2.1 convolution_convert_fusion.2
  488.6 2.7 multiply_reduce_fusion.2
  491.4 2.1 slice.58
  493.9 0.6 broadcast_in_dim.112
  494.5 1.4 copy-done.18
  495.9 1.9 convolution_convert_fusion.1.g_ref
  497.8 3.2 copy.63
  501.0 2.7 convolution_convert_fusion
  503.7 134.1 %attend_back_sum.1 = (f32[40,3968]{1,0:T(8,128)}, bf16[256,2560]{1,0:T(8,128)(2,1)}, bf16[256,1280]{1,0:T(8,128)(2,1)}) custom-call(bf16[256,1280]{1,0:T(8,128)(2,1)} %get-tuple-element.51.q_ref, bf16[256,1280]{1,0:T(8,128)(2,1)} %convolution_convert_fusion.1.g_ref, f32[10,128,256]{2,1,0:T(8,128)} %get-tuple-element.64.mixed_ref, s32[1,256]{1,0:T(1,128)} %bitcast.67, ...), custom_call_target="tpu_custom_call" | custom-call | tf_op jit(solution)/shard_map/attend_back_sum/pallas_call | solution.py:1597
  637.9 3.7 multiply_reduce_fusion.4
  641.6 2.0 maximum_convert_fusion
  643.7 0.7 slice.66
  644.4 0.8 slice_bitcast_fusion
  645.2 14.3 %finish.1 = (bf16[1280,1280]{1,0:T(8,128)(2,1)}, bf16[1280,1280]{1,0:T(8,128)(2,1)}, bf16[1280,1280]{1,0:T(8,128)(2,1)}, bf16[256,1280]{1,0:T(8,128)(2,1)}, f32[1,1280]{1,0:T(1,128)}) custom-call(bf16[256,1280]{1,0:T(8,128)(2,1)} %bitcast.62, f32[1,1280]{1,0:T(1,128)} %broadcast_in_dim.97.gain_ref, f32[256,1280]{1,0:T(8,128)} %copy-done.4, ...), custom_call_target="tpu_custom_call" | custom-call | flops 5033164800 | bytes 19660800 | tf_op jit(solution)/shard_map/finish/pallas_call | solution.py:1108
  659.5 0.7 convert_bitcast_fusion.1
  660.5 0.8 pad.5.clone
  661.3 64.4 %scatter_whole.1 = f32[40,3968]{1,0:T(8,128)} custom-call(bf16[32,40,1280]{2,1,0:T(8,128)(2,1)} %bitcast.51, bf16[32,40,1280]{2,1,0:T(8,128)(2,1)} %bitcast.52, bf16[32,40,1280]{2,1,0:T(8,128)(2,1)} %bitcast.53, bf16[32,40,128]{2,1,0:T(8,128)(2,1)} %bitcast.60), custom_call_target="tpu_custom_call" | custom-call | tf_op jit(solution)/shard_map/scatter_whole/pallas_call | solution.py:720
  725.7 1.3 sqrt_bitcast_fusion
  727.1 1.5 slice_reduce_fusion
  728.6 2.0 fusion.14
  730.5 0.7 copy.62
  731.2 3.3 copy.74
  734.5 1.4 copy.75
  (51 shorter events, 1.5 us)
Async XLA Ops:
  152.9 4.0 copy-start.11
  156.9 1.3 copy-start
  156.9 1.3 copy-start.16
  156.9 0.8 copy-start.8
  156.9 0.9 copy-start.9
  156.9 1.3 copy-start.14
  157.8 1.4 copy-start.2
  488.6 4.8 copy-start.17
  488.6 4.9 copy-start.3
  488.6 4.9 copy-start.15
  491.4 2.1 copy-start.1
  491.4 2.1 copy-start.12
  493.5 2.4 copy-start.18
  493.9 7.1 copy-start.4
  497.8 3.2 copy-start.6
  637.9 5.8 copy-start.7
  645.2 15.0 %copy-start.10 = (bf16[1280,16]{0,1:T(8,128)(2,1)S(1)}, bf16[1280,16]{0,1:T(8,128)(2,1)}, u32[]{:S(2)}) copy-start(bf16[1280,16]{0,1:T(8,128)(2,1)} %convolution_convert_fusion.2) | copy-start | bytes 122884
  645.2 15.0 %copy-start.13 = (bf16[1280,1]{0,1:T(2,128)(2,1)S(1)}, bf16[1280,1]{0,1:T(2,128)(2,1)}, u32[]{:S(2)}) copy-start(bf16[1280,1]{0,1:T(2,128)(2,1)} %broadcast_in_dim.112) | copy-start | bytes 7684
  725.7 4.8 slice-start
  731.2 3.3 copy-start.5

commit v10 on v7

--- a/solution.py
+++ b/solution.py
@@ -921,7 +921,7 @@
     def _():
         bias[...] = visible_bias((rows, rows), block * rows, start_ref[...], me * rows)
 
-        @pl.loop(0, HEADS, unroll=2)
+        @pl.loop(0, HEADS, unroll=5)
         def _(h):
             keys, values = kv_ref[0, :, lanes(2 * h * HEAD)], kv_ref[0, :, lanes((2 * h + 1) * HEAD)]
             scores = inner_right(keys, q_ref[:, lanes(h * HEAD)]) + bias[...]
@@ -1061,10 +1061,13 @@
 
 
 def finish_kernel(
-    x_ref, gain_ref, res_ref, hid_ref, q_ref, kv_ref, cos_ref, sin_ref, wq_ref, wk_ref, wv_ref,
-    dq_ref, dk_ref, dv_ref, out_ref, gain_out, acc,
+    x_ref, gain_ref, res_ref, hid_ref, q_ref, kv_ref, cos_ref, sin_ref, wq_ref, wk_ref, wv_ref, *refs
 ):
+    carried = (len(refs) - 6) // 2
+    sums, (dq_ref, dk_ref, dv_ref, out_ref, gain_out), acc = refs[:carried], refs[carried : carried + 5], refs[-1]
     step = pl.program_id(0)
+    for n, (own, out) in enumerate(zip(sums, refs[carried + 5 : -1])):
+        out[...] = own[...].T if n == 2 else own[...]
 
     @pl.when(step == 0)
     def _():
@@ -1094,10 +1097,11 @@
         gain_out[...] = jnp.sum(grad * values * scale, axis=0, keepdims=True)
 
 
-def finish(tokens, gain, residual_grad, hidden, query_grad, pair_grads, cosine, sine, wq, wk, wv):
+def finish(tokens, gain, residual_grad, hidden, query_grad, pair_grads, cosine, sine, wq, wk, wv, sums):
     rows, width = tokens.shape
     tile = 2 * HEAD
     column = pl.BlockSpec((width, tile), lambda i: (0, i))
+    part = sums[0].shape[0] * tile // width if sums else 0
     return pl.pallas_call(
         finish_kernel,
         out_shape=(
@@ -1106,16 +1110,19 @@
             jax.ShapeDtypeStruct((width, width), jnp.bfloat16),
             jax.ShapeDtypeStruct((rows, width), jnp.bfloat16),
             jax.ShapeDtypeStruct((1, width), jnp.float32),
-        ),
+        ) + tuple(jax.ShapeDtypeStruct(v.shape[::-1] if n == 2 else v.shape, v.dtype) for n, v in enumerate(sums)),
         grid=(width // tile,),
         in_specs=[whole_spec(rows, width), whole_spec(1, width), whole_spec(rows, width), whole_spec(rows, width),
                   pl.BlockSpec((rows, tile), lambda i: (0, i)), pl.BlockSpec((rows, 2 * tile), lambda i: (0, i)),
-                  whole_spec(rows, HEAD), whole_spec(rows, HEAD), column, column, column],
-        out_specs=(column, column, column, whole_spec(rows, width), whole_spec(1, width)),
+                  whole_spec(rows, HEAD), whole_spec(rows, HEAD), column, column, column]
+        + [pl.BlockSpec((part, v.shape[1]), lambda i: (i, 0)) for v in sums],
+        out_specs=(column, column, column, whole_spec(rows, width), whole_spec(1, width)) + tuple(
+            pl.BlockSpec((v.shape[1], part), lambda i: (0, i)) if n == 2
+            else pl.BlockSpec((part, v.shape[1]), lambda i: (i, 0)) for n, v in enumerate(sums)),
         scratch_shapes=[pltpu.VMEM((rows, width), jnp.float32)],
         cost_estimate=pl.CostEstimate(flops=12 * rows * width * width, bytes_accessed=12 * width * width, transcendentals=0),
         name="finish",
-    )(tokens, gain[None, :], residual_grad, hidden, query_grad, pair_grads, cosine, sine, wq, wk, wv)
+    )(tokens, gain[None, :], residual_grad, hidden, query_grad, pair_grads, cosine, sine, wq, wk, wv, *sums)
 
 
 def experts_kernel(
@@ -1441,7 +1448,6 @@
         back_sum, gate_sum, up_sum, down_sum = scatter_experts(
             back, (flat_in, result_grad), (pre_grad, lift_grad, middle), 3
         )
-        gate_sum, up_sum, down_sum = gate_sum[None], up_sum[None], down_sum.T[None]
     else:
         back_sum = scatter_rows(back, False, 3)
         split = width // group_count
@@ -1483,10 +1489,12 @@
 
     routed, pair_grads = lax.optimization_barrier((routed, pair_grads))
     layer_out = residual + shared_out + wide(routed)
-    query_part, key_part, value_part, tokens_grad, mixer_gain_grad = finish(
+    query_part, key_part, value_part, tokens_grad, mixer_gain_grad, *carried = finish(
         tokens[0], mixer_gain, residual_grad, hidden_low, query_lin_grad, pair_grads, cosine, sine,
-        query_weight, key_weight, value_weight,
+        query_weight, key_weight, value_weight, (gate_sum, up_sum, down_sum) if group_count == 2 else (),
     )
+    if carried:
+        gate_sum, up_sum, down_sum = (v[None] for v in carried)
     squares = jnp.stack(
         [jnp.sum(residual * residual), jnp.sum(mixer_out * mixer_out), jnp.sum(layer_out * layer_out)]
     )

time: 699 us -> 692 us (0.990)
  local copies, waits for them, and re-layouts: 25.5 us -> 17.4 us
    unnamed x58 -> x53, local copies, waits for them, and re-layouts: 10.8 us -> 2.81 us
  transfers between devices with their start and end apart: 2 -> 2, of which waited for: 0 -> 0; matrix products, arithmetic and copies ran while one was open for 5% -> 4% of each run, Pallas kernels for 61% -> 61%
where the time goes in v10:
time: 692 us; the launch traced here: 683 us
  Pallas kernels  621 us (90%)
  between operations  17.5 us (3%)
  local copies, waits for them, and re-layouts  17.4 us (3%)
  other arithmetic  14.6 us (2%)
  matrix products  13.1 us (2%)
    pallas_call x1, Pallas kernels, gather_shared(): pl.pallas_call(kernel, out_shape=(jax.ShapeDtypeStruct((ep_count,) + bloc...  161 us
    pallas_call x1, Pallas kernels, attend_back_sum(): pl.pallas_call(kernel, out_shape=(jax.ShapeDtypeStruct((part_rows, part_w...  128 us
    pallas_call x1, Pallas kernels, scatter_experts(): pl.pallas_call(kernel, out_shape=tuple(outs), in_specs=[anywhere] * 6, ou...  123 us
    pallas_call x1, Pallas kernels, run_experts(): pl.pallas_call(experts_kernel, out_shape=(shape(count, rows, side), shape...  73.6 us
    pallas_call x1, Pallas kernels, scatter_whole(): pl.pallas_call(kernel, out_shape=tuple(out_shape), in_specs=[anywhere] *...  64.4 us
    pallas_call x1, Pallas kernels, gather_rows(): pl.pallas_call(functools.partial(gather_kernel, plan, pieces, lambda n: N...  34.8 us
    pallas_call x1, Pallas kernels, finish(): pl.pallas_call(finish_kernel, out_shape=(jax.ShapeDtypeStruct((width, wid...  19.5 us
  transfers between devices with their start and end apart: 2, of which 0 were waited for; matrix products, arithmetic and copies ran while one was open for 4% of the time, Pallas kernels for 61%

profile of v10, /device:TPU:0, one launch (start us, length us, event | category | flops | bytes accessed | tf_op | source)
XLA Modules:
  0.0 683.5 jit_solution(10241363988057757711)
XLA Ops:
  7.3 1.3 broadcast_in_dim.98.gain_ref
  8.6 0.5 fusion.7
  9.1 0.8 pad_maximum_fusion.cos_ref
  9.9 0.8 pad_maximum_fusion.1.sin_ref
  10.6 8.6 %project.1 = (bf16[256,1280]{1,0:T(8,128)(2,1)}, bf16[256,1280]{1,0:T(8,128)(2,1)}, bf16[256,2560]{1,0:T(8,128)(2,1)}) custom-call(bf16[256,1280]{1,0:T(8,128)(2,1)} %bitcast.56, f32[1,1280]{1,0:T(1,128)} %broadcast_in_dim.98.gain_ref, f32[256,128]{1,0:T(8,128)} %pad_maximum_fusion.cos_ref, f32[256,128]{1,0:T(8,128)} %pad_maximum_fusion.1.sin_ref, ...), custom_call_target="tpu_custom_call" | custom-call | flops 2516582400 | bytes 9830400 | tf_op jit(solution)/shard_map/project/pallas_call | solution.py:890
  19.2 34.8 %gather_rows.1.kv_ref.pair_ref = bf16[16,256,2560]{2,1,0:T(8,128)(2,1)} custom-call(bf16[256,2560]{1,0:T(8,128)(2,1)} %get-tuple-element.55.x_ref), custom_call_target="tpu_custom_call" | custom-call | tf_op jit(solution)/shard_map/gather_rows/pallas_call | solution.py:236
  54.1 0.2 reduce-window.8
  54.4 0.5 slice.56
  57.7 0.6 pad_add_fusion.info
  58.3 7.4 %attend.1 = (f32[10,128,256]{2,1,0:T(8,128)}, bf16[256,1280]{1,0:T(8,128)(2,1)}, f32[10,1,256]{2,1,0:T(1,128)}) custom-call(s32[2]{0:T(128)} %pad_add_fusion.info, bf16[256,1280]{1,0:T(8,128)(2,1)} %get-tuple-element.54.q_ref, s32[1,256]{1,0:T(1,128)} %bitcast.66, bf16[16,256,2560]{2,1,0:T(8,128)(2,1)} %gather_rows.1.kv_ref.pair_ref), custom_call_target="tpu_custom_call" | custom-call | flops 3019898880 | bytes 11796480 | tf_op jit(solution)/shard_map/attend/pallas_call | solution.py:948
  65.7 3.9 multiply_reduce_fusion.5
  69.6 0.2 multiply_convert_fusion
  69.8 0.6 copy-done.12
  70.4 0.4 fusion.15
  70.8 0.2 fusion.6
  71.0 0.8 subtract_convert_fusion
  71.8 1.0 concatenate.15.x_ref
  72.8 161.3 %gather_shared.1 = (bf16[16,256,1408]{2,1,0:T(8,128)(2,1)}, f32[256,1280]{1,0:T(8,128)}, f32[256,1280]{1,0:T(8,128)}, bf16[1280,896]{1,0:T(8,128)(2,1)}, bf16[12...) custom-call(bf16[256,1408]{1,0:T(8,128)(2,1)} %concatenate.15.x_ref, bf16[256,1280]{1,0:T(8,128)(2,1)} %bitcast.52, ...), custom_call_target="tpu_custom_call" | custom-call | tf_op jit(solution)/shard_map/gather_shared/pallas_call | solution.py:294
  234.2 2.5 select_reduce_fusion
  236.7 0.6 broadcast_in_dim.108.share_row
  237.5 0.6 copy.56.rank_row
  238.1 2.0 copy.57.rank_col
  240.1 0.6 pad_add_fusion.1.where_ref
  240.6 73.6 %run_experts.1 = (bf16[16,256,1408]{2,1,0:T(8,128)(2,1)}, bf16[16,256,1280]{2,1,0:T(8,128)(2,1)}, bf16[3072,1280]{1,0:T(8,128)(2,1)}, bf16[3072,896]{1,0:T(8,128...) custom-call(s32[2]{0:T(128)} %pad_add_fusion.1.where_ref, ...), custom_call_target="tpu_custom_call" | custom-call | flops 56371445760 | bytes 62914560 | tf_op jit(solution)/shard_map/run_experts/pallas_call | solution.py:1182
  314.2 123.0 %scatter_experts.1 = (bf16[256,1408]{1,0:T(8,128)(2,1)}, f32[640,896]{1,0:T(8,128)}, f32[640,896]{1,0:T(8,128)}, f32[640,896]{1,0:T(8,128)}) custom-call(bf16[16,256,1408]{2,1,0:T(8,128)(2,1)} %get-tuple-element.63.p_ref, bf16[3072,1280]{1,0:T(8,128)(2,1)} %get-tuple-element.64.in_ref, bf16[3072,1280]{1,0:T(8,128)(2,1)} %get-tuple-element.65.og_ref, ...), custom_call_target="tpu_custom_call" | custom-call | tf_op jit(solution)/shard_map/scatter_experts/pallas_call | solution.py:831
  437.3 1.1 multiply_reduce_fusion.6
  438.5 2.8 multiply_reduce_fusion.2
  441.3 0.6 broadcast_in_dim.112
  441.9 0.4 fusion.res_ref
  442.3 0.7 copy-done.8
  443.0 2.8 convolution_convert_fusion
  445.8 0.5 copy-done.23
  446.3 1.9 convolution_convert_fusion.1.g_ref
  448.2 128.1 %attend_back_sum.1 = (f32[40,3968]{1,0:T(8,128)}, bf16[256,2560]{1,0:T(8,128)(2,1)}, bf16[256,1280]{1,0:T(8,128)(2,1)}) custom-call(bf16[256,1280]{1,0:T(8,128)(2,1)} %get-tuple-element.54.q_ref, bf16[256,1280]{1,0:T(8,128)(2,1)} %convolution_convert_fusion.1.g_ref, f32[10,128,256]{2,1,0:T(8,128)} %get-tuple-element.70.mixed_ref, s32[1,256]{1,0:T(1,128)} %bitcast.67, ...), custom_call_target="tpu_custom_call" | custom-call | tf_op jit(solution)/shard_map/attend_back_sum/pallas_call | solution.py:1349
  576.3 1.7 slice.66
  578.0 1.8 slice_bitcast_fusion
  579.9 1.2 convolution_convert_fusion.2
  581.1 19.5 %finish.1 = (bf16[1280,1280]{1,0:T(8,128)(2,1)}, bf16[1280,1280]{1,0:T(8,128)(2,1)}, bf16[1280,1280]{1,0:T(8,128)(2,1)}, bf16[256,1280]{1,0:T(8,128)(2,1)}, f32[...) custom-call(bf16[256,1280]{1,0:T(8,128)(2,1)} %bitcast.57, ...), custom_call_target="tpu_custom_call" | custom-call | flops 5033164800 | bytes 19660800 | tf_op jit(solution)/shard_map/finish/pallas_call | solution.py:1105
  600.6 0.7 convert_bitcast_fusion.1
  601.3 1.8 multiply_reduce_fusion.4
  603.1 2.0 maximum_convert_fusion
  605.2 0.2 copy.62
  605.5 0.8 pad.5.clone
  606.3 64.4 %scatter_whole.1 = f32[40,3968]{1,0:T(8,128)} custom-call(bf16[32,40,1280]{2,1,0:T(8,128)(2,1)} %bitcast.53, bf16[32,40,1280]{2,1,0:T(8,128)(2,1)} %bitcast.54, bf16[32,40,1280]{2,1,0:T(8,128)(2,1)} %bitcast.55, bf16[32,40,128]{2,1,0:T(8,128)(2,1)} %bitcast.61), custom_call_target="tpu_custom_call" | custom-call | tf_op jit(solution)/shard_map/scatter_whole/pallas_call | solution.py:713
  670.7 1.3 sqrt_bitcast_fusion
  672.0 1.5 slice_reduce_fusion
  673.5 2.0 fusion.14
  675.5 0.7 copy.59
  (68 shorter events, 0.8 us)
Async XLA Ops:
  7.2 233.5 %all-gather.3.cloned.1.call-start = ((), (), s32[]{:S(2)}) async-start(), calls=%async_computation.2 | async-start | bytes 11141120 | tf_op jit(solution)/shard_map/all_gather | solution.py:1412
  19.2 34.9 %copy-start.24 = (s32[1,4]{1,0:T(1,128)S(1)}, s32[1,4]{1,0:T(1,128)}, u32[]{:S(2)}) copy-start(s32[1,4]{1,0:T(1,128)} %param.18) | copy-start | bytes 52
  19.2 38.3 %copy-start.20 = (s32[1,256,7]{1,0,2:T(1,128)S(1)}, s32[1,256,7]{1,0,2:T(1,128)}, u32[]{:S(2)}) copy-start(s32[1,256,7]{1,0,2:T(1,128)} %param.19) | copy-start | bytes 21508
  54.0 527.1 %reduce-scatter.2.cloned.1.call-start = ((), (), s32[]{:S(2)}) async-start(), calls=%async_computation.1 | async-start | bytes 11141120 | tf_op jit(solution)/shard_map/reduce_scatter | solution.py:1445
  54.4 3.9 copy-start.18
  58.3 7.5 %copy-start.7 = (bf16[1,256,1280]{2,1,0:T(8,128)(2,1)S(1)}, bf16[1,256,1280]{2,1,0:T(8,128)(2,1)}, u32[]{:S(2)}) copy-start(bf16[1,256,1280]{2,1,0:T(8,128)(2,1)} %param.17) | copy-start | bytes 1966084
  65.7 3.9 copy-start.13
  69.6 1.2 copy-start
  69.6 1.2 copy-start.21
  69.6 0.8 copy-start.12
  69.6 1.2 copy-start.16
  70.4 1.4 copy-start.4
  438.4 2.9 copy-start.19
  438.4 3.5 copy-start.22
  438.4 3.5 copy-start.1
  438.4 3.5 copy-start.6
  438.5 3.5 copy-start.14
  438.5 3.5 copy-start.17
  441.9 1.1 copy-start.8
  443.0 2.8 copy-start.3
  443.0 3.3 copy-start.23
  576.3 3.5 copy-start.5
  576.3 3.5 copy-start.9
  581.1 20.2 %copy-start.2 = (f32[256,1280]{1,0:T(8,128)S(1)}, f32[256,1280]{1,0:T(8,128)}, u32[]{:S(2)}) copy-start(f32[256,1280]{1,0:T(8,128)} %copy-done) | copy-start | bytes 3932164
  581.1 20.2 %copy-start.10 = (f32[256,1280]{1,0:T(8,128)S(1)}, f32[256,1280]{1,0:T(8,128)}, u32[]{:S(2)}) copy-start(f32[256,1280]{1,0:T(8,128)} %get-tuple-element.58) | copy-start | bytes 3932164
  581.1 20.2 %copy-start.11 = (bf16[1,256,1280]{2,1,0:T(8,128)(2,1)S(1)}, bf16[1,256,1280]{2,1,0:T(8,128)(2,1)}, u32[]{:S(2)}) copy-start(bf16[1,256,1280]{2,1,0:T(8,128)(2,1)} %reduce-scatter.2.cloned.1.call-done) | copy-start | bytes 1966084
  601.3 3.9 copy-start.15
  670.7 4.8 slice-start
Sparse Core Ops, SparseCore 0:
  54.2 159.1 all-gather.2
  314.4 151.1 reduce-scatter.1

commit v11 on v10

--- a/solution.py
+++ b/solution.py
@@ -731,7 +731,7 @@
     plan, pieces = Plan(ep_count, False), 4
     place = Place(lax.axis_size("grp"), ep_count)
     left_of = [0, 0, 1]
-    hooks = (4, 5, 6, 7, 10, 11, 12, 13, 16, 17)
+    hooks = (8, 9, 10, 11, 13, 14, 15, 16)
     kinds, units = len(rights), 2 * len(rights)
     steps = units * 3
 

time: 692 us -> 720 us (1.040)
  Pallas kernels: 621 us -> 653 us
    pallas_call x1, Pallas kernels: 123 us -> 156 us  [scatter_experts(): pl.pallas_call(kernel, out_shape=tuple(outs), in_specs=[anywhere] * 6, ou...]
  transfers between devices with their start and end apart: 2 -> 2, of which waited for: 0 -> 0; matrix products, arithmetic and copies ran while one was open for 4% -> 4% of each run, Pallas kernels for 61% -> 63%
where the time goes in v11:
time: 720 us; the launch traced here: 716 us
  Pallas kernels  653 us (91%)
  local copies, waits for them, and re-layouts  17.5 us (2%)
  between operations  17.5 us (2%)
  other arithmetic  14.6 us (2%)
  matrix products  13.1 us (2%)
    pallas_call x1, Pallas kernels, gather_shared(): pl.pallas_call(kernel, out_shape=(jax.ShapeDtypeStruct((ep_count,) + bloc...  160 us
    pallas_call x1, Pallas kernels, scatter_experts(): pl.pallas_call(kernel, out_shape=tuple(outs), in_specs=[anywhere] * 6, ou...  156 us
    pallas_call x1, Pallas kernels, attend_back_sum(): pl.pallas_call(kernel, out_shape=(jax.ShapeDtypeStruct((part_rows, part_w...  129 us
    pallas_call x1, Pallas kernels, run_experts(): pl.pallas_call(experts_kernel, out_shape=(shape(count, rows, side), shape...  73.6 us
    pallas_call x1, Pallas kernels, scatter_whole(): pl.pallas_call(kernel, out_shape=tuple(out_shape), in_specs=[anywhere] *...  64.4 us
    pallas_call x1, Pallas kernels, gather_rows(): pl.pallas_call(functools.partial(gather_kernel, plan, pieces, lambda n: N...  34.8 us
    pallas_call x1, Pallas kernels, finish(): pl.pallas_call(finish_kernel, out_shape=(jax.ShapeDtypeStruct((width, wid...  19.5 us
  transfers between devices with their start and end apart: 2, of which 0 were waited for; matrix products, arithmetic and copies ran while one was open for 4% of the time, Pallas kernels for 63%

profile of v11, /device:TPU:0, one launch (start us, length us, event | category | flops | bytes accessed | tf_op | source)
XLA Modules:
  0.0 715.6 jit_solution(5353605260535797565)
XLA Ops:
  7.3 1.3 broadcast_in_dim.98.gain_ref
  8.6 0.5 fusion.7
  9.1 0.8 pad_maximum_fusion.cos_ref
  9.9 0.8 pad_maximum_fusion.1.sin_ref
  10.6 8.6 %project.1 = (bf16[256,1280]{1,0:T(8,128)(2,1)}, bf16[256,1280]{1,0:T(8,128)(2,1)}, bf16[256,2560]{1,0:T(8,128)(2,1)}) custom-call(bf16[256,1280]{1,0:T(8,128)(2,1)} %bitcast.56, f32[1,1280]{1,0:T(1,128)} %broadcast_in_dim.98.gain_ref, f32[256,128]{1,0:T(8,128)} %pad_maximum_fusion.cos_ref, f32[256,128]{1,0:T(8,128)} %pad_maximum_fusion.1.sin_ref, ...), custom_call_target="tpu_custom_call" | custom-call | flops 2516582400 | bytes 9830400 | tf_op jit(solution)/shard_map/project/pallas_call | solution.py:890
  19.2 34.8 %gather_rows.1.kv_ref.pair_ref = bf16[16,256,2560]{2,1,0:T(8,128)(2,1)} custom-call(bf16[256,2560]{1,0:T(8,128)(2,1)} %get-tuple-element.55.x_ref), custom_call_target="tpu_custom_call" | custom-call | tf_op jit(solution)/shard_map/gather_rows/pallas_call | solution.py:236
  54.1 0.2 reduce-window.8
  54.4 0.5 slice.56
  57.7 0.6 pad_add_fusion.info
  58.3 7.4 %attend.1 = (f32[10,128,256]{2,1,0:T(8,128)}, bf16[256,1280]{1,0:T(8,128)(2,1)}, f32[10,1,256]{2,1,0:T(1,128)}) custom-call(s32[2]{0:T(128)} %pad_add_fusion.info, bf16[256,1280]{1,0:T(8,128)(2,1)} %get-tuple-element.54.q_ref, s32[1,256]{1,0:T(1,128)} %bitcast.66, bf16[16,256,2560]{2,1,0:T(8,128)(2,1)} %gather_rows.1.kv_ref.pair_ref), custom_call_target="tpu_custom_call" | custom-call | flops 3019898880 | bytes 11796480 | tf_op jit(solution)/shard_map/attend/pallas_call | solution.py:948
  65.7 3.9 multiply_reduce_fusion.5
  69.6 0.2 multiply_convert_fusion
  69.8 0.6 copy-done.12
  70.4 0.4 fusion.15
  70.8 0.2 fusion.6
  71.0 0.8 subtract_convert_fusion
  71.8 1.0 concatenate.15.x_ref
  72.8 159.5 %gather_shared.1 = (bf16[16,256,1408]{2,1,0:T(8,128)(2,1)}, f32[256,1280]{1,0:T(8,128)}, f32[256,1280]{1,0:T(8,128)}, bf16[1280,896]{1,0:T(8,128)(2,1)}, bf16[12...) custom-call(bf16[256,1408]{1,0:T(8,128)(2,1)} %concatenate.15.x_ref, bf16[256,1280]{1,0:T(8,128)(2,1)} %bitcast.52, ...), custom_call_target="tpu_custom_call" | custom-call | tf_op jit(solution)/shard_map/gather_shared/pallas_call | solution.py:294
  232.4 2.5 select_reduce_fusion
  234.9 0.6 broadcast_in_dim.108.share_row
  235.6 0.6 copy.56.rank_row
  236.3 2.0 copy.57.rank_col
  238.2 0.6 pad_add_fusion.1.where_ref
  238.8 73.6 %run_experts.1 = (bf16[16,256,1408]{2,1,0:T(8,128)(2,1)}, bf16[16,256,1280]{2,1,0:T(8,128)(2,1)}, bf16[3072,1280]{1,0:T(8,128)(2,1)}, bf16[3072,896]{1,0:T(8,128...) custom-call(s32[2]{0:T(128)} %pad_add_fusion.1.where_ref, ...), custom_call_target="tpu_custom_call" | custom-call | flops 56371445760 | bytes 62914560 | tf_op jit(solution)/shard_map/run_experts/pallas_call | solution.py:1182
  312.4 155.7 %scatter_experts.1 = (bf16[256,1408]{1,0:T(8,128)(2,1)}, f32[640,896]{1,0:T(8,128)}, f32[640,896]{1,0:T(8,128)}, f32[640,896]{1,0:T(8,128)}) custom-call(bf16[16,256,1408]{2,1,0:T(8,128)(2,1)} %get-tuple-element.63.p_ref, bf16[3072,1280]{1,0:T(8,128)(2,1)} %get-tuple-element.64.in_ref, bf16[3072,1280]{1,0:T(8,128)(2,1)} %get-tuple-element.65.og_ref, ...), custom_call_target="tpu_custom_call" | custom-call | tf_op jit(solution)/shard_map/scatter_experts/pallas_call | solution.py:831
  468.1 1.1 multiply_reduce_fusion.6
  469.3 2.8 multiply_reduce_fusion.2
  472.1 0.6 broadcast_in_dim.112
  472.8 0.4 fusion.res_ref
  473.1 0.7 copy-done.8
  473.8 2.8 convolution_convert_fusion
  476.6 0.5 copy-done.23
  477.1 1.9 convolution_convert_fusion.1.g_ref
  479.0 129.4 %attend_back_sum.1 = (f32[40,3968]{1,0:T(8,128)}, bf16[256,2560]{1,0:T(8,128)(2,1)}, bf16[256,1280]{1,0:T(8,128)(2,1)}) custom-call(bf16[256,1280]{1,0:T(8,128)(2,1)} %get-tuple-element.54.q_ref, bf16[256,1280]{1,0:T(8,128)(2,1)} %convolution_convert_fusion.1.g_ref, f32[10,128,256]{2,1,0:T(8,128)} %get-tuple-element.70.mixed_ref, s32[1,256]{1,0:T(1,128)} %bitcast.67, ...), custom_call_target="tpu_custom_call" | custom-call | tf_op jit(solution)/shard_map/attend_back_sum/pallas_call | solution.py:1349
  608.5 1.7 slice.66
  610.2 1.8 slice_bitcast_fusion
  612.0 1.2 convolution_convert_fusion.2
  613.3 19.5 %finish.1 = (bf16[1280,1280]{1,0:T(8,128)(2,1)}, bf16[1280,1280]{1,0:T(8,128)(2,1)}, bf16[1280,1280]{1,0:T(8,128)(2,1)}, bf16[256,1280]{1,0:T(8,128)(2,1)}, f32[...) custom-call(bf16[256,1280]{1,0:T(8,128)(2,1)} %bitcast.57, ...), custom_call_target="tpu_custom_call" | custom-call | flops 5033164800 | bytes 19660800 | tf_op jit(solution)/shard_map/finish/pallas_call | solution.py:1105
  632.7 0.7 convert_bitcast_fusion.1
  633.4 1.8 multiply_reduce_fusion.4
  635.2 2.0 maximum_convert_fusion
  637.4 0.2 copy.62
  637.6 0.8 pad.5.clone
  638.4 64.4 %scatter_whole.1 = f32[40,3968]{1,0:T(8,128)} custom-call(bf16[32,40,1280]{2,1,0:T(8,128)(2,1)} %bitcast.53, bf16[32,40,1280]{2,1,0:T(8,128)(2,1)} %bitcast.54, bf16[32,40,1280]{2,1,0:T(8,128)(2,1)} %bitcast.55, bf16[32,40,128]{2,1,0:T(8,128)(2,1)} %bitcast.61), custom_call_target="tpu_custom_call" | custom-call | tf_op jit(solution)/shard_map/scatter_whole/pallas_call | solution.py:713
  702.9 1.3 sqrt_bitcast_fusion
  704.2 1.5 slice_reduce_fusion
  705.7 2.0 fusion.14
  707.6 0.7 copy.59
  (68 shorter events, 0.8 us)
Async XLA Ops:
  7.2 231.6 %all-gather.3.cloned.1.call-start = ((), (), s32[]{:S(2)}) async-start(), calls=%async_computation.2 | async-start | bytes 11141120 | tf_op jit(solution)/shard_map/all_gather | solution.py:1412
  19.2 34.9 %copy-start.24 = (s32[1,4]{1,0:T(1,128)S(1)}, s32[1,4]{1,0:T(1,128)}, u32[]{:S(2)}) copy-start(s32[1,4]{1,0:T(1,128)} %param.18) | copy-start | bytes 52
  19.2 38.3 %copy-start.20 = (s32[1,256,7]{1,0,2:T(1,128)S(1)}, s32[1,256,7]{1,0,2:T(1,128)}, u32[]{:S(2)}) copy-start(s32[1,256,7]{1,0,2:T(1,128)} %param.19) | copy-start | bytes 21508
  54.0 559.2 %reduce-scatter.2.cloned.1.call-start = ((), (), s32[]{:S(2)}) async-start(), calls=%async_computation.1 | async-start | bytes 11141120 | tf_op jit(solution)/shard_map/reduce_scatter | solution.py:1445
  54.4 3.9 copy-start.18
  58.3 7.5 %copy-start.7 = (bf16[1,256,1280]{2,1,0:T(8,128)(2,1)S(1)}, bf16[1,256,1280]{2,1,0:T(8,128)(2,1)}, u32[]{:S(2)}) copy-start(bf16[1,256,1280]{2,1,0:T(8,128)(2,1)} %param.17) | copy-start | bytes 1966084
  65.7 3.9 copy-start.13
  69.6 1.2 copy-start
  69.6 1.2 copy-start.21
  69.6 0.8 copy-start.12
  69.6 1.2 copy-start.16
  70.4 1.4 copy-start.4
  469.2 2.9 copy-start.19
  469.2 3.5 copy-start.22
  469.2 3.5 copy-start.1
  469.3 3.5 copy-start.6
  469.3 3.5 copy-start.14
  469.3 3.5 copy-start.17
  472.7 1.1 copy-start.8
  473.8 2.8 copy-start.3
  473.8 3.3 copy-start.23
  608.5 3.5 copy-start.5
  608.5 3.5 copy-start.9
  613.2 20.2 %copy-start.2 = (f32[256,1280]{1,0:T(8,128)S(1)}, f32[256,1280]{1,0:T(8,128)}, u32[]{:S(2)}) copy-start(f32[256,1280]{1,0:T(8,128)} %copy-done) | copy-start | bytes 3932164
  613.2 20.2 %copy-start.10 = (f32[256,1280]{1,0:T(8,128)S(1)}, f32[256,1280]{1,0:T(8,128)}, u32[]{:S(2)}) copy-start(f32[256,1280]{1,0:T(8,128)} %get-tuple-element.58) | copy-start | bytes 3932164
  613.2 20.2 %copy-start.11 = (bf16[1,256,1280]{2,1,0:T(8,128)(2,1)S(1)}, bf16[1,256,1280]{2,1,0:T(8,128)(2,1)}, u32[]{:S(2)}) copy-start(bf16[1,256,1280]{2,1,0:T(8,128)(2,1)} %reduce-scatter.2.cloned.1.call-done) | copy-start | bytes 1966084
  633.4 3.9 copy-start.15
  702.8 4.8 slice-start
Sparse Core Ops, SparseCore 0:
  54.2 163.7 all-gather.2
  312.5 153.9 reduce-scatter.1
